TPU v7x, 32 devices: a whole 2x2x4 slice. The times are simulated.
32 devices in a mesh: dp: 8 (over z, x), tensor: 4 (over y, core).
Axes of the slice: x: 2, y: 2, z: 4, core: 2. Of those that a mesh axis runs over, the one named last changes fastest.
Arguments:
- inputs: bfloat16 [8192, 2048], P('dp'), may hold values from -8 to 8
- gain_attn: float32 [2048], replicated, may hold values from 0.5 to 1.5
- w_query: bfloat16 [2048, 2048], P(None, 'tensor'), may hold values from -0.125 to 0.125
- w_key: bfloat16 [2048, 2048], P(None, 'tensor'), may hold values from -0.125 to 0.125
- w_value: bfloat16 [2048, 2048], P(None, 'tensor'), may hold values from -0.125 to 0.125
- gate_logit: float32 [16], P('tensor'), may hold values from -1.5 to 1.5
- w_out: bfloat16 [2048, 2048], P('tensor'), may hold values from -0.25 to 0.25
- gain_mlp: float32 [2048], replicated, may hold values from 0.5 to 1.5
- w_up: bfloat16 [2048, 8192], P(None, 'tensor'), may hold values from -0.125 to 0.125
- w_down: bfloat16 [8192, 2048], P('tensor'), may hold values from -0.0625 to 0.0625
- seg_parent: int32 [16], replicated, may hold values from -1 to 15, as said below
- out_grad: bfloat16 [8192, 2048], P('dp'), may hold values from -6 to 6
Outputs:
- outputs: bfloat16 [8192, 2048], P('dp')
- input_grad: bfloat16 [8192, 2048], P('dp')
- gain_attn_grad: float32 [2048], P('dp')
- w_query_grad: float32 [2048, 2048], P('dp', 'tensor')
- w_key_grad: float32 [2048, 2048], P('dp', 'tensor')
- w_value_grad: float32 [2048, 2048], P('dp', 'tensor')
- gate_grad: float32 [16], P('tensor')
- w_out_grad: float32 [2048, 2048], P('tensor', 'dp')
- gain_mlp_grad: float32 [2048], P('dp')
- w_up_grad: float32 [2048, 8192], P('dp', 'tensor')
- w_down_grad: float32 [8192, 2048], P('tensor', 'dp')
Inputs may be any that keep to these rules, and one draw needn't show every extreme that they name: `seg_parent`: segments form trees of 16 segments: a chain of 4 trunk segments whose first has parent -1, 4 branch segments whose parent is the trunk's last, and 2 leaves whose parent is one branch, for each branch. Segments of a tree lie on any devices; segment 16 - 1 is the last trunk segment of some tree.
All inputs are finite; a program needn't handle non-finite values.
Results may differ from a plain program's by a relative error of at most 0.015.
Values sent between devices are 32-bit elements; how exact they have to be, the bound alone decides.
A program may use at most 256 MiB of HBM per device.

v0:
```python
import jax
import jax.numpy as jnp
from jax import lax
from jax.sharding import PartitionSpec as P

DH = 128
SEG = 512
DEPTH = 5


topmost_level = lax.Precision.HIGHEST
norm_eps = 1e-06


def feature_map(values):
    return jnp.where(values > 0, values + 1.0, jnp.exp(jnp.minimum(values, 0.0)))


def feature_slope(values):
    return jnp.where(values > 0, 1.0, jnp.exp(jnp.minimum(values, 0.0)))


def gelu_tanh(values):
    return jax.nn.gelu(values, approximate=True)


def ancestor_table(seg_parent):
    seg_total = seg_parent.shape[0]
    columns = jnp.arange(seg_total, dtype=jnp.int32)
    current = seg_parent
    lineage_table = jnp.zeros((seg_total, seg_total), jnp.float32)
    for depth_level in range(DEPTH):
        onehot = current[:, None] == columns[None, :]
        lineage_table = lineage_table + onehot.astype(jnp.float32)
        lifted = jnp.sum(jnp.where(onehot, seg_parent[None, :], 0), axis=1)
        current = jnp.where(current >= 0, lifted, -1)
    return lineage_table


def rms_forward(values, gain_vec):
    inverse = lax.rsqrt(jnp.mean(values * values, axis=-1, keepdims=True) + norm_eps)
    return (values * inverse * gain_vec, inverse)


def rms_backward(values, inverse, gain_vec, upstream):
    scaled = upstream * gain_vec
    inner_mean = jnp.mean(scaled * values, axis=-1, keepdims=True)
    grad_values = inverse * scaled - values * inverse * inverse * inverse * inner_mean
    grad_gain = jnp.sum(upstream * values * inverse, axis=0)
    return (grad_values, grad_gain)


def body(
    inputs,
    gain_attn,
    w_query,
    w_key,
    w_value,
    gate_logit,
    w_out,
    gain_mlp,
    w_up,
    w_down,
    seg_parent,
    out_grad,
):
    tok_count = inputs.shape[0]
    seg_count = tok_count // SEG
    head_count = w_query.shape[1] // DH
    score_scale = DH ** (-0.5)
    input_float = inputs.astype(jnp.float32)
    normed_attn, inv_attn = rms_forward(input_float, gain_attn)
    hidden_attn = normed_attn.astype(jnp.bfloat16)

    def heads_of(matrix):
        return (
            jnp.dot(hidden_attn, matrix, preferred_element_type=jnp.float32)
            .astype(jnp.bfloat16)
            .reshape(seg_count, SEG, head_count, DH)
        )

    query_heads = heads_of(w_query)
    key_heads = heads_of(w_key)
    value_heads = heads_of(w_value)
    query_float = query_heads.astype(jnp.float32)
    key_float = key_heads.astype(jnp.float32)
    value_float = value_heads.astype(jnp.float32)
    key_feat = feature_map(key_float)
    mem_delta = jnp.einsum("nshd,nshe->nhde", key_feat, value_float, precision=topmost_level)
    key_feature_sum = jnp.sum(key_feat, axis=1)
    lineage_table = ancestor_table(seg_parent)
    first_segment = lax.axis_index("dp") * seg_count
    ancestor_rows = lax.dynamic_slice_in_dim(lineage_table, first_segment, seg_count, 0)
    ancestor_columns = lax.dynamic_slice_in_dim(lineage_table, first_segment, seg_count, 1)
    segment_parts = (
        lax.all_gather(mem_delta, "dp", axis=0, tiled=True),
        lax.all_gather(key_feature_sum, "dp", axis=0, tiled=True),
    )
    weight_list = ancestor_rows
    memory = jnp.einsum("mn,nhde->mhde", weight_list, segment_parts[0], precision=topmost_level)
    memory_norm_term = jnp.einsum(
        "zr,rqp->zqp", weight_list, segment_parts[1], precision=topmost_level
    )
    causal = jnp.arange(SEG)[:, None] >= jnp.arange(SEG)[None, :]
    scores = (
        jnp.einsum("nshd,nthd->nhst", query_heads, key_heads, preferred_element_type=jnp.float32)
        * score_scale
    )
    masked = jnp.where(causal, scores, -1e30)
    row_top = jnp.max(masked, axis=-1, keepdims=True)
    log_total = row_top + jnp.log(jnp.sum(jnp.exp(masked - row_top), axis=-1, keepdims=True))
    prob_low = jnp.exp(masked - log_total).astype(jnp.bfloat16)
    local = jnp.einsum("nhst,nthd->nshd", prob_low, value_heads, preferred_element_type=jnp.float32)
    query_feat = feature_map(query_float)
    numerator = jnp.einsum("nshd,nhde->nshe", query_feat, memory, precision=topmost_level)
    denominator = (
        jnp.einsum("nshd,nhd->nsh", query_feat, memory_norm_term, precision=topmost_level)[
            ..., None
        ]
        + 1.0
    )
    retrieved = numerator / denominator
    gate_value = jax.nn.sigmoid(gate_logit)
    gate_open = gate_value[None, None, :, None]
    mixed = gate_open * retrieved + (1.0 - gate_open) * local
    mixed_low = mixed.reshape(tok_count, head_count * DH).astype(jnp.bfloat16)
    attn_out = lax.psum(jnp.dot(mixed_low, w_out, preferred_element_type=jnp.float32), "tensor")
    residual = input_float + attn_out
    normed_mlp, inv_mlp = rms_forward(residual, gain_mlp)
    hidden_mlp = normed_mlp.astype(jnp.bfloat16)
    preact = jnp.dot(hidden_mlp, w_up, preferred_element_type=jnp.float32)
    activated = gelu_tanh(preact).astype(jnp.bfloat16)
    mlp_out = lax.psum(jnp.dot(activated, w_down, preferred_element_type=jnp.float32), "tensor")
    outputs = (residual + mlp_out).astype(jnp.bfloat16)
    up_grad = jnp.einsum("td,fd->tf", out_grad, w_down, preferred_element_type=jnp.float32)
    gelu_pull = jax.vjp(gelu_tanh, preact)[1]
    pre_grad = gelu_pull(up_grad)[0].astype(jnp.bfloat16)
    w_down_grad = jnp.einsum("tf,td->fd", activated, out_grad, preferred_element_type=jnp.float32)
    w_up_grad = jnp.einsum("td,tf->df", hidden_mlp, pre_grad, preferred_element_type=jnp.float32)
    hidden_grad = lax.psum(
        jnp.einsum("tf,df->td", pre_grad, w_up, preferred_element_type=jnp.float32), "tensor"
    )
    resid_norm_grad, gain_mlp_grad = rms_backward(residual, inv_mlp, gain_mlp, hidden_grad)
    residual_grad = out_grad.astype(jnp.float32) + resid_norm_grad
    residual_low = residual_grad.astype(jnp.bfloat16)
    w_out_grad = jnp.einsum(
        "te,td->ed", mixed_low, residual_low, preferred_element_type=jnp.float32
    )
    mixed_grad = (
        jnp.einsum("td,ed->te", residual_low, w_out, preferred_element_type=jnp.float32)
        .astype(jnp.bfloat16)
        .reshape(seg_count, SEG, head_count, DH)
    )
    mixed_float = mixed_grad.astype(jnp.float32)
    gate_grad = (
        jnp.sum(mixed_float * (retrieved - local), axis=(0, 1, 3)) * gate_value * (1.0 - gate_value)
    )
    keep_scores = (1.0 - gate_value)[None, :, None, None]
    keep_values = (1.0 - gate_value)[None, None, :, None]
    prob_grad = keep_scores * jnp.einsum(
        "nshd,nthd->nhst", mixed_grad, value_heads, preferred_element_type=jnp.float32
    )
    scores_again = (
        jnp.einsum("nshd,nthd->nhst", query_heads, key_heads, preferred_element_type=jnp.float32)
        * score_scale
    )
    probs_again = jnp.exp(jnp.where(causal, scores_again, -1e30) - log_total)
    again_low = probs_again.astype(jnp.bfloat16)
    score_grad = (
        probs_again * (prob_grad - jnp.sum(prob_grad * probs_again, axis=-1, keepdims=True))
    ).astype(jnp.bfloat16)
    value_grad = keep_values * jnp.einsum(
        "nhst,nshd->nthd", again_low, mixed_grad, preferred_element_type=jnp.float32
    )
    query_grad = (
        jnp.einsum("nhst,nthd->nshd", score_grad, key_heads, preferred_element_type=jnp.float32)
        * score_scale
    )
    key_grad = (
        jnp.einsum("nhst,nshd->nthd", score_grad, query_heads, preferred_element_type=jnp.float32)
        * score_scale
    )
    read_grad = gate_open * mixed_float / denominator
    norm_grad = -jnp.sum(read_grad * retrieved, axis=-1)
    feat_grad = (
        jnp.einsum("nshe,nhde->nshd", read_grad, memory, precision=topmost_level)
        + norm_grad[..., None] * memory_norm_term[:, None]
    )
    query_grad = query_grad + feat_grad * feature_slope(query_float)
    memory_grad = jnp.einsum("nshd,nshe->nhde", query_feat, read_grad, precision=topmost_level)
    memory_norm_grad = jnp.einsum("nshd,nsh->nhd", query_feat, norm_grad, precision=topmost_level)
    segment_parts = (
        lax.all_gather(memory_grad, "dp", axis=0, tiled=True),
        lax.all_gather(memory_norm_grad, "dp", axis=0, tiled=True),
    )
    weight_list = ancestor_columns
    delta_grad = jnp.einsum("nm,nhde->mhde", weight_list, segment_parts[0], precision=topmost_level)
    summed_gradient = jnp.einsum(
        "kz,kti->zti", weight_list, segment_parts[1], precision=topmost_level
    )
    key_feat_grad = (
        jnp.einsum("nshe,nhde->nshd", value_float, delta_grad, precision=topmost_level)
        + summed_gradient[:, None]
    )
    key_grad = key_grad + key_feat_grad * feature_slope(key_float)
    value_grad = value_grad + jnp.einsum(
        "nshd,nhde->nshe", key_feat, delta_grad, precision=topmost_level
    )
    query_low = query_grad.reshape(tok_count, head_count * DH).astype(jnp.bfloat16)
    key_low = key_grad.reshape(tok_count, head_count * DH).astype(jnp.bfloat16)
    value_low = value_grad.reshape(tok_count, head_count * DH).astype(jnp.bfloat16)
    w_query_grad = jnp.einsum(
        "td,te->de", hidden_attn, query_low, preferred_element_type=jnp.float32
    )
    w_key_grad = jnp.einsum("td,te->de", hidden_attn, key_low, preferred_element_type=jnp.float32)
    w_value_grad = jnp.einsum(
        "td,te->de", hidden_attn, value_low, preferred_element_type=jnp.float32
    )
    attn_terms = (
        jnp.einsum("te,de->td", query_low, w_query, preferred_element_type=jnp.float32)
        + jnp.einsum("te,de->td", key_low, w_key, preferred_element_type=jnp.float32)
        + jnp.einsum("te,de->td", value_low, w_value, preferred_element_type=jnp.float32)
    )
    attn_hidden_grad = lax.psum(attn_terms, "tensor")
    input_norm_grad, gain_attn_grad = rms_backward(
        input_float, inv_attn, gain_attn, attn_hidden_grad
    )
    input_grad = (residual_grad + input_norm_grad).astype(jnp.bfloat16)
    gate_tiles = jnp.tile(gate_grad, lax.axis_size("dp"))
    (
        w_query_grad,
        w_key_grad,
        w_value_grad,
        w_out_grad,
        w_up_grad,
        w_down_grad,
        gain_attn_grad,
        gain_mlp_grad,
        gate_grad,
    ) = (
        lax.psum_scatter(w_query_grad, "dp", scatter_dimension=0, tiled=True),
        lax.psum_scatter(w_key_grad, "dp", scatter_dimension=0, tiled=True),
        lax.psum_scatter(w_value_grad, "dp", scatter_dimension=0, tiled=True),
        lax.psum_scatter(w_out_grad, "dp", scatter_dimension=1, tiled=True),
        lax.psum_scatter(w_up_grad, "dp", scatter_dimension=0, tiled=True),
        lax.psum_scatter(w_down_grad, "dp", scatter_dimension=1, tiled=True),
        lax.psum_scatter(gain_attn_grad, "dp", scatter_dimension=0, tiled=True),
        lax.psum_scatter(gain_mlp_grad, "dp", scatter_dimension=0, tiled=True),
        lax.psum_scatter(gate_tiles, "dp", scatter_dimension=0, tiled=True),
    )
    return (
        outputs,
        input_grad,
        gain_attn_grad,
        w_query_grad,
        w_key_grad,
        w_value_grad,
        gate_grad,
        w_out_grad,
        gain_mlp_grad,
        w_up_grad,
        w_down_grad,
    )


def solution(mesh):
    placed = (
        P("dp", None),
        P(),
        P(None, "tensor"),
        P(None, "tensor"),
        P(None, "tensor"),
        P("tensor"),
        P("tensor", None),
        P(),
        P(None, "tensor"),
        P("tensor", None),
        P(),
        P("dp", None),
    )
    return jax.shard_map(
        body,
        mesh=mesh,
        in_specs=placed,
        out_specs=(
            P("dp", None),
            P("dp", None),
            P("dp"),
            P("dp", "tensor"),
            P("dp", "tensor"),
            P("dp", "tensor"),
            P("tensor"),
            P("tensor", "dp"),
            P("dp"),
            P("dp", "tensor"),
            P("tensor", "dp"),
        ),
        check_vma=False,
    )
```

profile of v0, /device:TPU:0, one launch (start us, length us, event | category | flops | bytes accessed | tf_op | source)
XLA Modules:
  0.0 1861.3 jit_solution(2788611272157754015)
XLA Ops:
  41.0 32.8 %all_gather.13 = f32[16,4,128]{2,1,0:T(4,128)S(1)} all-gather(f32[2,4,128]{2,1,0:T(4,128)S(1)} %fusion.46), channel_id=1, replica_groups=mesh['dp'=8,'tensor'=4] {'dp'}, dimensions={0}, use_global_device_ids=true | all-gather | bytes 36864 | tf_op jit(solution)/shard_map/all_gather | solution.py:97
  82.6 23.8 %all-gather.3.cloned.1.call-done = f32[16,4,128,128]{3,2,1,0:T(8,128)} async-done(((f32[2,4,128,128]{3,2,1,0:T(8,128)}), f32[16,4,128,128]{3,2,1,0:T(8,128)}) %all-gather.3.cloned.1.call-update) | async-done | bytes 4194320 | tf_op jit(solution)/shard_map/all_gather | solution.py:96
  130.5 14.6 fusion.150
  145.0 136.6 %all-reduce.9.cloned.1.call-done = f32[1024,2048]{1,0:T(8,128)} async-done(((f32[1024,2048]{1,0:T(8,128)}), f32[1024,2048]{1,0:T(8,128)}) %all-reduce.9.cloned.1.call-update) | async-done | bytes 8388624 | tf_op jit(solution)/shard_map/psum | solution.py:127
  287.4 23.6 %fusion.14 = (bf16[1024,2048]{1,0:T(8,128)(2,1)}, f32[1024,2048]{1,0:T(8,128)}) fusion(f32[1024,2048]{1,0:T(8,128)} %fusion.150, bf16[2048,2048]{1,0:T(8,128)(2,1)} %param.20, f32[1024,2048]{1,0:T(8,128)S(1)} %get-tuple-element.23, f32[2048]{0:T(1024)S(1)} %copy-done.26, f32[1024]{0:T(1024)S(1)} %add_rsqrt_fusion), kind=kOutput, calls=%fused_computation.21 | convolution fusion | flops 8638169088 | bytes 37761024 | tf_op jit(solution)/shard_map/dot_general | solution.py:131
  311.0 14.7 fusion.151
  325.8 153.1 %all-reduce.11.cloned.1.call-done = f32[1024,2048]{1,0:T(8,128)} async-done(((f32[1024,2048]{1,0:T(8,128)}), f32[1024,2048]{1,0:T(8,128)}) %all-reduce.11.cloned.1.call-update) | async-done | bytes 8388624 | tf_op jit(solution)/shard_map/psum | solution.py:140
  478.9 7.8 multiply_reduce_fusion
  507.4 16.6 fusion.143
  527.2 30.9 %all_gather.15 = f32[16,4,128]{2,1,0:T(4,128)S(1)} all-gather(f32[2,4,128]{2,1,0:T(4,128)S(1)} %bitcast.127), channel_id=1, replica_groups=mesh['dp'=8,'tensor'=4] {'dp'}, dimensions={0}, use_global_device_ids=true | all-gather | bytes 36864 | tf_op jit(solution)/shard_map/all_gather | solution.py:194
  588.0 7.1 fusion.21
  612.9 9.3 add_add_fusion
  623.5 7.7 fusion.41
  653.3 16.2 fusion.140
  669.6 16.8 fusion.142
  689.0 222.3 %all-reduce.13.cloned.1.call-done = (f32[1024,2048]{1,0:T(8,128)}, f32[1024,2048]{1,0:T(8,128)}) async-done(((f32[1024,2048]{1,0:T(8,128)}, f32[1024,2048]{1,0:T(8,128)}), (f32[1024,2048]{1,0:T(8,128)}, f32[1024,2048]{1,0:T(8,128)})) %all-reduce.13.cloned.1.call-update) | async-done | bytes 16777232 | tf_op jit(solution)/shard_map/psum | solution.py:133
  917.4 39.0 %all-reduce.3 = (f32[2048]{0:T(1024)S(1)}, f32[32]{0:T(128)S(1)}, f32[2048]{0:T(1024)S(1)}) all-reduce(f32[2048]{0:T(1024)S(1)} %get-tuple-element.13, f32[32]{0:T(128)S(1)} %tile.10, f32[2048]{0:T(1024)S(1)} %copy-done.27), channel_id=2, replica_groups=mesh['dp'=8,'tensor'=4] {'dp'}, use_global_device_ids=true, to_apply=%region_18.19.clone | all-reduce | flops 4128 | bytes 33024
  958.3 18.6 fusion.7
  976.8 27.5 %reduce-scatter.13.cloned.1.call-done = f32[512,256]{1,0:T(8,128)} async-done(((f32[512,2048]{1,0:T(8,128)}), f32[512,256]{1,0:T(8,128)}) %reduce-scatter.13.cloned.1.call-update) | async-done | bytes 524304 | tf_op jit(solution)/shard_map/reduce_scatter | solution.py:244
  1004.3 92.3 %reduce-scatter.7.cloned.1.call-done = f32[256,512]{1,0:T(8,128)} async-done(((f32[2048,512]{1,0:T(8,128)}), f32[256,512]{1,0:T(8,128)}) %reduce-scatter.7.cloned.1.call-update) | async-done | bytes 524304 | tf_op jit(solution)/shard_map/reduce_scatter | solution.py:241
  1096.6 91.9 %reduce-scatter.11.cloned.1.call-done = f32[256,512]{1,0:T(8,128)} async-done(((f32[2048,512]{1,0:T(8,128)}), f32[256,512]{1,0:T(8,128)}) %reduce-scatter.11.cloned.1.call-update) | async-done | bytes 524304 | tf_op jit(solution)/shard_map/reduce_scatter | solution.py:243
  1188.5 92.4 %reduce-scatter.9.cloned.1.call-done = f32[256,512]{1,0:T(8,128)} async-done(((f32[2048,512]{1,0:T(8,128)}), f32[256,512]{1,0:T(8,128)}) %reduce-scatter.9.cloned.1.call-update) | async-done | bytes 524304 | tf_op jit(solution)/shard_map/reduce_scatter | solution.py:242
  1280.8 286.7 %reduce-scatter.15.cloned.1.call-done = f32[256,2048]{1,0:T(8,128)} async-done(((f32[2048,2048]{1,0:T(8,128)}), f32[256,2048]{1,0:T(8,128)}) %reduce-scatter.15.cloned.1.call-update) | async-done | bytes 2097168 | tf_op jit(solution)/shard_map/reduce_scatter | solution.py:245
  1567.6 286.7 %reduce-scatter.17.cloned.1.call-done = f32[2048,256]{1,0:T(8,128)} async-done(((f32[2048,2048]{1,0:T(8,128)}), f32[2048,256]{1,0:T(8,128)}) %reduce-scatter.17.cloned.1.call-update) | async-done | bytes 2097168 | tf_op jit(solution)/shard_map/reduce_scatter | solution.py:246
  (180 shorter events, 176.3 us)
Async XLA Ops:
  7.2 116.5 %copy-start = (bf16[512,2048]{1,0:T(8,128)(2,1)S(1)}, bf16[512,2048]{1,0:T(8,128)(2,1)}, u32[]{:S(2)}) copy-start(bf16[512,2048]{1,0:T(8,128)(2,1)} %param.18) | copy-start | bytes 6291460
  7.2 99.2 %all-gather.3.cloned.1.call-start = ((), (), s32[]{:S(2)}) async-start(), calls=%async_computation.6 | async-start | bytes 4718592 | tf_op jit(solution)/shard_map/all_gather | solution.py:96
  10.8 18.8 %copy-start.24 = (f32[1024]{0:T(1024)}, f32[1024]{0:T(1024)S(1)}, u32[]{:S(2)}) copy-start(f32[1024]{0:T(1024)S(1)} %add_rsqrt_fusion.1) | copy-start | bytes 12292
  29.5 252.1 %all-reduce.9.cloned.1.call-start = ((), (), s32[]{:S(2)}) async-start(), calls=%async_computation.7 | async-start | bytes 16777216 | tf_op jit(solution)/shard_map/psum | solution.py:127
  35.8 37.9 %copy-start.30 = (s32[16]{0:T(128)S(1)}, s32[16]{0:T(128)}, u32[]{:S(2)}) copy-start(s32[16]{0:T(128)} %param.22) | copy-start | bytes 196
  35.8 38.8 %copy-start.32 = (f32[4]{0:T(128)S(1)}, f32[4]{0:T(128)}, u32[]{:S(2)}) copy-start(f32[4]{0:T(128)} %param.17) | copy-start | bytes 52
  40.4 37.3 %copy-start.8 = (bf16[2,512,4,128]{1,3,2,0:T(8,128)(2,1)S(1)}, bf16[2,512,4,128]{1,3,2,0:T(8,128)(2,1)}, u32[]{:S(2)}) copy-start(bf16[2,512,4,128]{1,3,2,0:T(8,128)(2,1)} %copy.82) | copy-start | bytes 3145732
  130.4 348.4 %all-reduce.11.cloned.1.call-start = ((), (), s32[]{:S(2)}) async-start(), calls=%async_computation.8 | async-start | bytes 16777216 | tf_op jit(solution)/shard_map/psum | solution.py:140
  145.0 142.4 %copy-start.26 = (f32[2048]{0:T(1024)S(1)}, f32[2048]{0:T(1024)}, u32[]{:S(2)}) copy-start(f32[2048]{0:T(1024)} %param.19) | copy-start | bytes 24580
  287.4 23.6 %copy-start.2 = (f32[1024,2048]{1,0:T(8,128)}, f32[1024,2048]{1,0:T(8,128)S(1)}, u32[]{:S(2)}) copy-start(f32[1024,2048]{1,0:T(8,128)S(1)} %get-tuple-element.23) | copy-start | bytes 25165828
  325.7 262.3 %all-gather.5.cloned.1.call-start = ((), (), s32[]{:S(2)}) async-start(), calls=%async_computation.9 | async-start | bytes 4718592 | tf_op jit(solution)/shard_map/all_gather | solution.py:193
  507.3 404.1 %all-reduce.13.cloned.1.call-start = ((), (), s32[]{:S(2)}) async-start(), calls=%async_computation.16 | async-start | bytes 33554432 | tf_op jit(solution)/shard_map/psum | solution.py:133
  507.3 51.0 %slice-start.2 = ((s8[8388608]{0:T(1024)(128)(4,1)}), s8[4194304]{0:T(1024)(128)(4,1)S(1)}, s32[]{:S(2)}) async-start(s8[8388608]{0:T(1024)(128)(4,1)} %bitcast.108), calls=%async_computation.19 | async-start | bytes 8388608
  507.3 16.7 copy-start.17
  507.3 16.7 copy-start.18
  507.3 51.0 %slice-start.3 = ((s8[8388608]{0:T(1024)(128)(4,1)}), s8[4194304]{0:T(1024)(128)(4,1)S(1)}, s32[]{:S(2)}) async-start(s8[8388608]{0:T(1024)(128)(4,1)} %bitcast.108), calls=%async_computation.20 | async-start | bytes 8388608
  524.0 34.3 %copy-start.12 = (bf16[2,512,4,128]{3,2,1,0:T(4,128)(2,1)S(1)}, bf16[2,512,4,128]{3,2,1,0:T(4,128)(2,1)}, u32[]{:S(2)}) copy-start(bf16[2,512,4,128]{3,2,1,0:T(4,128)(2,1)} %reshape.98) | copy-start | bytes 3145732
  622.3 382.0 %reduce-scatter.13.cloned.1.call-start = ((), (), s32[]{:S(2)}) async-start(), calls=%async_computation.13 | async-start | bytes 4718592 | tf_op jit(solution)/shard_map/reduce_scatter | solution.py:244
  631.2 465.4 %reduce-scatter.7.cloned.1.call-start = ((), (), s32[]{:S(2)}) async-start(), calls=%async_computation.10 | async-start | bytes 4718592 | tf_op jit(solution)/shard_map/reduce_scatter | solution.py:241
  639.2 549.3 %reduce-scatter.11.cloned.1.call-start = ((), (), s32[]{:S(2)}) async-start(), calls=%async_computation.12 | async-start | bytes 4718592 | tf_op jit(solution)/shard_map/reduce_scatter | solution.py:243
  646.1 634.8 %reduce-scatter.9.cloned.1.call-start = ((), (), s32[]{:S(2)}) async-start(), calls=%async_computation.11 | async-start | bytes 4718592 | tf_op jit(solution)/shard_map/reduce_scatter | solution.py:242
  653.0 914.5 %reduce-scatter.15.cloned.1.call-start = ((), (), s32[]{:S(2)}) async-start(), calls=%async_computation.14 | async-start | bytes 18874368 | tf_op jit(solution)/shard_map/reduce_scatter | solution.py:245
  669.6 1184.7 %reduce-scatter.17.cloned.1.call-start = ((), (), s32[]{:S(2)}) async-start(), calls=%async_computation.15 | async-start | bytes 18874368 | tf_op jit(solution)/shard_map/reduce_scatter | solution.py:246
  958.3 896.0 %copy-start.1 = (bf16[512,2048]{1,0:T(8,128)(2,1)S(1)}, bf16[512,2048]{1,0:T(8,128)(2,1)}, u32[]{:S(2)}) copy-start(bf16[512,2048]{1,0:T(8,128)(2,1)} %param.18) | copy-start | bytes 6291460
  (27 other events, 116.4 us)
Sparse Core Ops, SparseCore 0:
  29.6 76.6 all-gather.2
  130.6 151.0 all-reduce.8
  325.8 152.9 all-reduce.10
  507.4 73.8 all-gather.4
  622.4 288.8 all-reduce.12
  915.4 88.8 reduce-scatter.12
  1008.9 87.6 reduce-scatter.6
  1100.8 87.6 reduce-scatter.10
  1193.1 87.6 reduce-scatter.8
  1285.1 282.4 reduce-scatter.14
  1572.4 281.7 reduce-scatter.16
where the time goes:
time: 1870 us; the launch traced here: 1860 us
  waiting for transfers between devices  1410 us (75%)
  matrix products  238 us (13%)
  blocking collectives  103 us (6%)
  other arithmetic  53.6 us (3%)
  local copies, waits for them, and re-layouts  36.7 us (2%)
    reduce_scatter x1, waiting for transfers between devices, body(): lax.psum_scatter(w_up_grad, 'dp', scatter_dimension=0, tiled=True)  287 us
    reduce_scatter x1, waiting for transfers between devices, body(): lax.psum_scatter(w_down_grad, 'dp', scatter_dimension=1, tiled=True)  287 us
    psum x1, waiting for transfers between devices, body(): lax.psum(jnp.dot(activated, w_down, preferred_element_type=jnp.float32),...  222 us
    psum x1, waiting for transfers between devices, body(): lax.psum(jnp.einsum('tf,df->td', pre_grad, w_up, preferred_element_type=j...  153 us
    psum x1, waiting for transfers between devices, body(): lax.psum(jnp.dot(mixed_low, w_out, preferred_element_type=jnp.float32), '...  137 us
    reduce_scatter x1, waiting for transfers between devices, body(): lax.psum_scatter(w_key_grad, 'dp', scatter_dimension=0, tiled=True)  92.4 us
    reduce_scatter x1, waiting for transfers between devices, body(): lax.psum_scatter(w_query_grad, 'dp', scatter_dimension=0, tiled=True)  92.3 us
    reduce_scatter x1, waiting for transfers between devices, body(): lax.psum_scatter(w_value_grad, 'dp', scatter_dimension=0, tiled=True)  91.9 us
  transfers between devices with their start and end apart: 11, of which 10 were waited for; matrix products, arithmetic and copies ran while one was open for 9% of the time, Pallas kernels for 0%

commit v1 on v0

v1 whole, which is shorter than its diff:
```python
import jax
import jax.numpy as jnp
from jax import lax
from jax.sharding import PartitionSpec as P

DH = 128
SEG = 512
DEPTH = 5
EPS = 1e-06

F32 = jnp.float32
BF16 = jnp.bfloat16


def feature_map(values):
    return jnp.where(values > 0, values + 1.0, jnp.exp(jnp.minimum(values, 0.0)))


def feature_slope(values):
    return jnp.where(values > 0, 1.0, jnp.exp(jnp.minimum(values, 0.0)))


def gelu_tanh(values):
    return jax.nn.gelu(values, approximate=True)


def ancestor_table(seg_parent):
    seg_total = seg_parent.shape[0]
    columns = jnp.arange(seg_total, dtype=jnp.int32)
    current = seg_parent
    lineage_table = jnp.zeros((seg_total, seg_total), F32)
    for _ in range(DEPTH):
        onehot = current[:, None] == columns[None, :]
        lineage_table = lineage_table + onehot.astype(F32)
        lifted = jnp.sum(jnp.where(onehot, seg_parent[None, :], 0), axis=1)
        current = jnp.where(current >= 0, lifted, -1)
    return lineage_table


def dot(a, b):
    return jnp.dot(a, b, preferred_element_type=F32)


def dot_t(a, b):
    return lax.dot_general(a, b, (((0,), (0,)), ((), ())), preferred_element_type=F32)


def dot_nt(a, b):
    return lax.dot_general(a, b, (((1,), (1,)), ((), ())), preferred_element_type=F32)


def body(
    inputs,
    gain_attn,
    w_query,
    w_key,
    w_value,
    gate_logit,
    w_out,
    gain_mlp,
    w_up,
    w_down,
    seg_parent,
    out_grad,
):
    tokens, width = inputs.shape
    half = tokens // 2
    segs = tokens // SEG
    heads = w_query.shape[1] // DH
    units = w_up.shape[1]
    scale = DH ** (-0.5)
    dp = lax.axis_size("dp")
    tn = lax.axis_size("tensor")
    depth = dp // 2
    rows = width // dp
    di = lax.axis_index("dp")
    ti = lax.axis_index("tensor")
    core = ti % 2
    xi = di % 2
    zi = di // 2

    one = jnp.where(seg_parent[0] < tokens * dp, 1.0, 2.0)

    def low_after_wire(v):
        return (v * one).astype(BF16)

    def swap_core(v):
        return lax.ppermute(v, "tensor", [(i, i ^ 1) for i in range(tn)])

    def swap_y(v):
        return lax.ppermute(v, "tensor", [(i, i ^ 2) for i in range(tn)])

    def swap_x(v):
        return lax.ppermute(v, "dp", [(i, i ^ 1) for i in range(dp)])

    z_groups = [[z * 2 + x for z in range(depth)] for x in range(2)]

    def scatter_z(v):
        return lax.psum_scatter(v, "dp", scatter_dimension=0, axis_index_groups=z_groups, tiled=True)

    def pick(v, index, axis):
        size = v.shape[axis] // 2
        return lax.dynamic_slice_in_dim(v, index * size, size, axis)

    def place(own, other, index, axis):
        return jnp.where(
            index == 0,
            jnp.concatenate([own, other], axis),
            jnp.concatenate([other, own], axis),
        )

    def tensor_sum(lhs, weight_dot, chunks=1):
        out = []
        step = half // chunks
        for c in range(chunks):
            lo = c * step
            send = swap_core(weight_dot(lhs[half + lo : half + lo + step]))
            part = weight_dot(lhs[lo : lo + step]) + send
            out.append(part + swap_y(part))
        return out

    x_own = pick(inputs, core, 0).astype(F32)
    x_oth = pick(inputs, 1 - core, 0).astype(F32)
    og_own = pick(out_grad, core, 0)
    og_oth = pick(out_grad, 1 - core, 0)
    og = jnp.concatenate([og_own, og_oth], 0)

    def inv_rms(v):
        return lax.rsqrt(jnp.mean(v * v, axis=-1, keepdims=True) + EPS)

    inv_own = inv_rms(x_own)
    inv_oth = inv_rms(x_oth)
    h1 = jnp.concatenate(
        [
            (x_own * inv_own * gain_attn).astype(BF16),
            (x_oth * inv_oth * gain_attn).astype(BF16),
        ],
        0,
    )

    def heads_of(matrix):
        return dot(h1, matrix).astype(BF16).reshape(segs, SEG, heads, DH)

    kh = heads_of(w_key)
    vh = heads_of(w_value)
    kf = kh.astype(F32)
    sk = feature_map(kf)
    sk16 = sk.astype(BF16)
    delta = jnp.einsum("nshd,nshe->nhde", sk16, vh, preferred_element_type=F32)
    zsum = jnp.sum(sk, axis=1)

    lineage = ancestor_table(seg_parent)
    sub = segs // 2

    def seg_ids(z, x, c):
        base = (z * 2 + x) * segs
        ids = jnp.arange(sub, dtype=jnp.int32)
        return jnp.concatenate([base + c * sub + ids, base + (1 - c) * sub + ids])

    mine = seg_ids(zi, xi, core)

    def pack(big, small):
        return jnp.concatenate([big.reshape(-1, DH), small.reshape(-1, DH)], 0)

    def unpack(v):
        n = segs * heads
        return v[: n * DH].reshape(segs, heads, DH, DH), v[n * DH :].reshape(segs, heads, DH)

    def zup(v):
        return lax.ppermute(v, "dp", [(i, i + 2) for i in range(dp - 2)])

    def zdn(v):
        return lax.ppermute(v, "dp", [(i + 2, i) for i in range(dp - 2)])

    def exchange(block, table):
        if depth == 4:
            xs = [swap_x(block)]
            r1 = zup(block)
            d1 = zdn(block)
            r2 = zup(r1)
            d2 = zdn(d1)
            r3 = zup(r2)
            d3 = zdn(d2)
            s1 = jnp.where(zi <= 1, d1, r1)
            s2 = jnp.where(zi == 0, d2, jnp.where(zi == 1, r1, jnp.where(zi == 2, d1, r2)))
            s3 = jnp.where(zi == 0, d3, jnp.where(zi == 1, d2, jnp.where(zi == 2, r2, r3)))
            xs = xs + [swap_x(s) for s in (s1, s2, s3)]
            q1 = jnp.where(zi <= 1, zi + 1, zi - 1)
            q2 = jnp.where(zi == 0, 2, jnp.where(zi == 1, 0, jnp.where(zi == 2, 3, 1)))
            q3 = jnp.where(zi == 0, 3, jnp.where(zi == 1, 3, 0))
            zs = [zi, q1, q2, q3]
            blocks = [block, s1, s2, s3]
            pairs = [(b, seg_ids(q, xi, core)) for b, q in zip(blocks, zs)]
            pairs += [(b, seg_ids(q, 1 - xi, core)) for b, q in zip(xs, zs)]
        else:
            every = lax.all_gather(block, "dp", axis=0, tiled=False)
            pairs = [(every[d], seg_ids(d // 2, d % 2, core)) for d in range(dp)]
        big = 0.0
        small = 0.0
        mine_rows = jnp.take(table, mine, axis=0)
        for b, ids in pairs:
            weight = jnp.take(mine_rows, ids, axis=1)
            bb, bs = unpack(b)
            for n in range(segs):
                big = big + weight[:, n][:, None, None, None] * bb[n][None]
                small = small + weight[:, n][:, None, None] * bs[n][None]
        return big, small

    memory, zin = exchange(pack(delta, zsum), lineage)

    og_b_own = swap_x(og_own.astype(F32))
    x_b_own = swap_x(x_own)

    qh = heads_of(w_query)
    qf = qh.astype(F32)
    causal = jnp.arange(SEG)[:, None] >= jnp.arange(SEG)[None, :]
    scores = jnp.einsum("nshd,nthd->nhst", qh, kh, preferred_element_type=F32) * scale
    masked = jnp.where(causal, scores, -1e30)
    row_top = jnp.max(masked, axis=-1, keepdims=True)
    lse = row_top + jnp.log(jnp.sum(jnp.exp(masked - row_top), axis=-1, keepdims=True))
    prob_low = jnp.exp(masked - lse).astype(BF16)
    local = jnp.einsum("nhst,nthd->nshd", prob_low, vh, preferred_element_type=F32)
    sq = feature_map(qf)
    sq16 = sq.astype(BF16)

    wu_keep = pick(w_up, xi, 1)
    wu_send = pick(w_up, 1 - xi, 1)
    wd_keep = pick(w_down, xi, 0)
    wd_send = pick(w_down, 1 - xi, 0)
    ug_keep = dot_nt(og, wd_keep)
    ug_send = dot_nt(og, wd_send)

    mem16 = memory.astype(BF16)
    den = jnp.einsum("nshd,nhd->nsh", sq, zin)[..., None] + 1.0
    retrieved = jnp.einsum("nshd,nhde->nshe", sq16, mem16, preferred_element_type=F32) / den
    gate = jax.nn.sigmoid(gate_logit)
    g4 = gate[None, None, :, None]
    a16 = (g4 * retrieved + (1.0 - g4) * local).reshape(tokens, heads * DH).astype(BF16)

    resid = x_own + jnp.concatenate(tensor_sum(a16, lambda l: dot(l, w_out), 2), 0)
    inv_mlp = inv_rms(resid)
    normed = resid * inv_mlp
    h2 = jnp.concatenate(
        [(normed * gain_mlp).astype(BF16), (swap_core(normed) * gain_mlp).astype(BF16)], 0
    )

    pre_send = dot(h2, wu_send)
    act_send = gelu_tanh(pre_send).astype(BF16)
    act_b = [swap_x(p.astype(F32)) for p in jnp.split(act_send, 2, axis=1)]
    pre_keep = dot(h2, wu_keep)
    act_keep = gelu_tanh(pre_keep).astype(BF16)
    dp_send = jax.vjp(gelu_tanh, pre_send)[1](ug_send)[0].astype(BF16)
    dp_keep = jax.vjp(gelu_tanh, pre_keep)[1](ug_keep)[0].astype(BF16)

    dh2 = jnp.concatenate(
        tensor_sum(
            jnp.concatenate([dp_keep, dp_send], 1),
            lambda l: dot_nt(l[:, : units // 2], wu_keep) + dot_nt(l[:, units // 2 :], wu_send),
            2,
        ),
        0,
    )

    og_b = jnp.concatenate(
        [low_after_wire(og_b_own), low_after_wire(swap_core(og_b_own))], 0
    )
    down = []
    for k, p in zip(jnp.split(act_keep, 2, axis=1), act_b):
        down.append(scatter_z(dot_t(og, k) + dot_t(og_b, low_after_wire(p))))
    down = jnp.concatenate(down, 1)
    down_mine = pick(down, xi, 0)
    down_theirs = swap_x(pick(down, 1 - xi, 0))
    w_down_grad = place(down_mine, down_theirs, xi, 1).T

    def columns_of(v, x):
        return lax.dynamic_index_in_dim(
            v.reshape(tokens, depth, 2, rows), x, 2, keepdims=False
        ).reshape(tokens, depth * rows)

    h2_keep = columns_of(h2, xi)
    h2_send = columns_of(h2, 1 - xi)
    to_send = swap_x(dot_t(h2_send, dp_keep))
    to_keep = swap_x(dot_t(h2_send, dp_send))
    up_send = scatter_z(dot_t(h2_keep, dp_send) + to_send)
    up_keep = scatter_z(dot_t(h2_keep, dp_keep) + to_keep)
    w_up_grad = place(up_keep, up_send, xi, 1)

    mlp_out = jnp.concatenate(
        tensor_sum(
            jnp.concatenate([act_keep, act_send], 1),
            lambda l: dot(l[:, : units // 2], wd_keep) + dot(l[:, units // 2 :], wd_send),
            2,
        ),
        0,
    )
    out_own = (resid + mlp_out).astype(BF16)
    outputs = place(out_own, low_after_wire(swap_core(out_own.astype(F32))), core, 0)

    gs = dh2 * gain_mlp
    dresid = (
        og_own.astype(F32)
        + inv_mlp * gs
        - resid * inv_mlp * inv_mlp * inv_mlp * jnp.mean(gs * resid, axis=-1, keepdims=True)
    )
    gain_mlp_part = jnp.sum(dh2 * resid * inv_mlp, axis=0)
    dr_own = dresid.astype(BF16)
    dr = jnp.concatenate([dr_own, low_after_wire(swap_core(dr_own.astype(F32)))], 0)

    da = dot_nt(dr, w_out).astype(BF16).reshape(segs, SEG, heads, DH)
    daf = da.astype(F32)
    gate_part = jnp.sum(daf * (retrieved - local), axis=(0, 1, 3)) * gate * (1.0 - gate)

    dnum = g4 * daf / den
    dden = -jnp.sum(dnum * retrieved, axis=-1)
    dnum16 = dnum.astype(BF16)
    dmem = jnp.einsum("nshd,nshe->nhde", sq16, dnum16, preferred_element_type=F32)
    dzin = jnp.einsum("nshd,nsh->nhd", sq, dden)
    ddelta, dzsum = exchange(pack(dmem, dzin), lineage.T)

    keep_s = (1.0 - gate)[None, :, None, None]
    dprobs = keep_s * jnp.einsum("nshd,nthd->nhst", da, vh, preferred_element_type=F32)
    scores2 = jnp.einsum("nshd,nthd->nhst", qh, kh, preferred_element_type=F32) * scale
    probs = jnp.exp(jnp.where(causal, scores2, -1e30) - lse)
    p16 = probs.astype(BF16)
    ds16 = (probs * (dprobs - jnp.sum(dprobs * probs, axis=-1, keepdims=True))).astype(BF16)
    dv = (1.0 - g4) * jnp.einsum("nhst,nshd->nthd", p16, da, preferred_element_type=F32)
    dq = jnp.einsum("nhst,nthd->nshd", ds16, kh, preferred_element_type=F32) * scale
    dk = jnp.einsum("nhst,nshd->nthd", ds16, qh, preferred_element_type=F32) * scale
    dsq = (
        jnp.einsum("nshe,nhde->nshd", dnum16, mem16, preferred_element_type=F32)
        + dden[..., None] * zin[:, None]
    )
    dq = dq + dsq * feature_slope(qf)

    g_out_send = swap_x(dot_t(columns_of(dr, 1 - xi), a16))
    w_out_rows = scatter_z(dot_t(columns_of(dr, xi), a16) + g_out_send)
    w_out_grad = w_out_rows.T

    dd16 = ddelta.astype(BF16)
    dsk = (
        jnp.einsum("nshe,nhde->nshd", vh, dd16, preferred_element_type=F32) + dzsum[:, None]
    )
    dk = dk + dsk * feature_slope(kf)
    dv = dv + jnp.einsum("nshd,nhde->nshe", sk16, dd16, preferred_element_type=F32)

    flat = (tokens, heads * DH)
    dq16 = dq.reshape(flat).astype(BF16)
    dk16 = dk.reshape(flat).astype(BF16)
    dv16 = dv.reshape(flat).astype(BF16)

    d_keep = jnp.concatenate([pick(v, xi, 1) for v in (dq16, dk16, dv16)], 1)
    d_send = jnp.concatenate([pick(v, 1 - xi, 1) for v in (dq16, dk16, dv16)], 1)
    d_b = low_after_wire(swap_x(d_send.astype(F32)))
    x_b_oth = swap_core(x_b_own)
    h1_b = jnp.concatenate(
        [(v * inv_rms(v) * gain_attn).astype(BF16) for v in (x_b_own, x_b_oth)], 0
    )
    qkv = scatter_z(dot_t(h1, d_keep) + dot_t(h1_b, d_b))
    qkv_mine = pick(qkv, xi, 0)
    qkv_theirs = swap_x(pick(qkv, 1 - xi, 0))
    n3 = qkv.shape[1] // 3
    w_query_grad, w_key_grad, w_value_grad = (
        place(qkv_mine[:, i * n3 : (i + 1) * n3], qkv_theirs[:, i * n3 : (i + 1) * n3], xi, 1)
        for i in range(3)
    )

    n1 = heads * DH
    dh1 = jnp.concatenate(
        tensor_sum(
            jnp.concatenate([dq16, dk16, dv16], 1),
            lambda l: dot_nt(l[:, :n1], w_query)
            + dot_nt(l[:, n1 : 2 * n1], w_key)
            + dot_nt(l[:, 2 * n1 :], w_value),
            2,
        ),
        0,
    )
    gs1 = dh1 * gain_attn
    dx = (
        dresid
        + inv_own * gs1
        - x_own * inv_own * inv_own * inv_own * jnp.mean(gs1 * x_own, axis=-1, keepdims=True)
    )
    gain_attn_part = jnp.sum(dh1 * x_own * inv_own, axis=0)
    dx_own = dx.astype(BF16)
    input_grad = place(dx_own, low_after_wire(swap_core(dx_own.astype(F32))), core, 0)

    gains = jnp.concatenate([gain_attn_part, gain_mlp_part])
    small = jnp.concatenate([gains + swap_core(gains), jnp.pad(gate_part, (0, DH - heads))])
    bit = 1
    while bit < dp:
        small = small + lax.ppermute(small, "dp", [(i, i ^ bit) for i in range(dp)])
        bit *= 2
    gain_attn_grad = lax.dynamic_slice_in_dim(small, di * rows, rows, 0)
    gain_mlp_grad = lax.dynamic_slice_in_dim(small, width + di * rows, rows, 0)
    gate_grad = small[2 * width : 2 * width + heads]

    return (
        outputs,
        input_grad,
        gain_attn_grad,
        w_query_grad,
        w_key_grad,
        w_value_grad,
        gate_grad,
        w_out_grad,
        gain_mlp_grad,
        w_up_grad,
        w_down_grad,
    )


def solution(mesh):
    placed = (
        P("dp", None),
        P(),
        P(None, "tensor"),
        P(None, "tensor"),
        P(None, "tensor"),
        P("tensor"),
        P("tensor", None),
        P(),
        P(None, "tensor"),
        P("tensor", None),
        P(),
        P("dp", None),
    )
    return jax.shard_map(
        body,
        mesh=mesh,
        in_specs=placed,
        out_specs=(
            P("dp", None),
            P("dp", None),
            P("dp"),
            P("dp", "tensor"),
            P("dp", "tensor"),
            P("dp", "tensor"),
            P("tensor"),
            P("tensor", "dp"),
            P("dp"),
            P("dp", "tensor"),
            P("tensor", "dp"),
        ),
        check_vma=False,
    )
```

time: 1870 us -> 1230 us (0.66)
  waiting for transfers between devices: 1410 us -> 567 us
  local copies, waits for them, and re-layouts: 36.7 us -> 200 us
  blocking collectives: 103 us -> 0 us
  starting transfers between devices: 0.92 us -> 76.4 us
  other arithmetic: 53.6 us -> 116 us
    reduce_scatter x6, waiting for transfers between devices: 877 us -> 52.1 us  [scatter_z(): lax.psum_scatter(v, 'dp', scatter_dimension=0, axis_index_groups=z_groups...]
    ppermute x0 -> x56, waiting for transfers between devices: none -> 515 us  [the longest x8 239 us: swap_y(): return lax.ppermute(v, 'tensor', [(i, i ^ 2) for i in range(tn)])]
    psum x3 -> x0, waiting for transfers between devices: 512 us -> none  [the longest x1 222 us: body(): lax.psum(jnp.dot(activated, w_down, preferred_element_type=jnp.float32),...]
    ppermute x0 -> x56, starting transfers between devices: none -> 75.4 us  [the longest x6 32.7 us: zup(): return lax.ppermute(v, 'dp', [(i, i + 2) for i in range(dp - 2)])]
    all_gather x2 -> x0, blocking collectives: 63.6 us -> none  [the longest x1 32.8 us: body(): lax.all_gather(key_feature_sum, 'dp', axis=0, tiled=True)]
    unnamed x84 -> x277, local copies, waits for them, and re-layouts: 15 us -> 71.8 us
    unnamed x1 -> x0, blocking collectives: 39 us -> none
    convert_element_type x2 -> x17, other arithmetic: 21.6 us -> 50.6 us  [the longest x5 15.7 us: low_after_wire(): return (v * one).astype(BF16)]
  transfers between devices with their start and end apart: 11 -> 62, of which waited for: 10 -> 28; matrix products, arithmetic and copies ran while one was open for 9% -> 41% of each run, Pallas kernels for 0% -> 0%
where the time goes in v1:
time: 1230 us; the launch traced here: 1220 us
  waiting for transfers between devices  567 us (46%)
  matrix products  242 us (20%)
  local copies, waits for them, and re-layouts  200 us (16%)
  other arithmetic  116 us (9%)
  starting transfers between devices  76.4 us (6%)
  between operations  17 us (1%)
    ppermute x8, waiting for transfers between devices, swap_y(): return lax.ppermute(v, 'tensor', [(i, i ^ 2) for i in range(tn)])  239 us
    ppermute x18, waiting for transfers between devices, swap_x(): return lax.ppermute(v, 'dp', [(i, i ^ 1) for i in range(dp)])  205 us
    dot_general x23, matrix products, dot_nt(): lax.dot_general(a, b, (((1,), (1,)), ((), ())), preferred_element_type=F32)  83 us
    unnamed x277, local copies, waits for them, and re-layouts  71.8 us
    dot_general x12, matrix products, dot_t(): lax.dot_general(a, b, (((0,), (0,)), ((), ())), preferred_element_type=F32)  67.2 us
    dot_general x17, matrix products, dot(): return jnp.dot(a, b, preferred_element_type=F32)  60.2 us
    reduce_scatter x6, waiting for transfers between devices, scatter_z(): lax.psum_scatter(v, 'dp', scatter_dimension=0, axis_index_groups=z_groups...  52.1 us
    ppermute x6, waiting for transfers between devices, zdn(): return lax.ppermute(v, 'dp', [(i + 2, i) for i in range(dp - 2)])  33.6 us
  transfers between devices with their start and end apart: 62, of which 28 were waited for; matrix products, arithmetic and copies ran while one was open for 41% of the time, Pallas kernels for 0%

profile of v1, /device:TPU:0, one launch (start us, length us, event | category | flops | bytes accessed | tf_op | source)
XLA Modules:
  0.0 1217.8 jit_solution(4508256651436533368)
XLA Ops:
  108.7 30.6 %collective-permute-done.9 = f32[1032,128]{1,0:T(8,128)S(1)} collective-permute-done((f32[1032,128]{1,0:T(8,128)S(1)}, f32[1032,128]{1,0:T(8,128)S(1)}, u32[]{:S(2)}, u32[]{:S(2)}) %collective-permute-start.9) | collective-permute-done | bytes 528416 | tf_op jit(solution)/shard_map/ppermute | solution.py:94
  162.8 40.6 %collective-permute-done.13 = f32[256,2048]{1,0:T(8,128)S(1)} collective-permute-done((f32[256,2048]{1,0:T(8,128)S(1)}, f32[256,2048]{1,0:T(8,128)S(1)}, u32[]{:S(2)}, u32[]{:S(2)}) %collective-permute-start.13) | collective-permute-done | bytes 2097184 | tf_op jit(solution)/shard_map/ppermute | solution.py:91
  203.7 43.8 %collective-permute-done.11 = f32[256,2048]{1,0:T(8,128)S(1)} collective-permute-done((f32[256,2048]{1,0:T(8,128)S(1)}, f32[256,2048]{1,0:T(8,128)S(1)}, u32[]{:S(2)}, u32[]{:S(2)}) %collective-permute-start.11) | collective-permute-done | bytes 2097184 | tf_op jit(solution)/shard_map/ppermute | solution.py:91
  262.6 10.9 multiply_convert_fusion.8
  293.4 29.8 %collective-permute-done.53 = f32[1024,512]{1,0:T(8,128)S(1)} collective-permute-done((f32[1024,512]{1,0:T(8,128)S(1)}, f32[1024,512]{1,0:T(8,128)S(1)}, u32[]{:S(2)}, u32[]{:S(2)}) %collective-permute-start.53) | collective-permute-done | bytes 2097184 | tf_op jit(solution)/shard_map/ppermute | solution.py:94
  336.4 11.1 fusion.22
  347.5 27.5 %collective-permute-done.54 = f32[1024,512]{1,0:T(8,128)S(1)} collective-permute-done((f32[1024,512]{1,0:T(8,128)}, f32[1024,512]{1,0:T(8,128)S(1)}, u32[]{:S(2)}, u32[]{:S(2)}) %collective-permute-start.54) | collective-permute-done | bytes 2097184 | tf_op jit(solution)/shard_map/ppermute | solution.py:94
  382.1 11.3 fusion.29
  413.6 11.3 constant_dynamic-slice_fusion.4
  424.9 10.5 copy.160
  460.6 10.7 copy.159
  501.8 33.4 %collective-permute-done.50 = f32[1024,1024]{1,0:T(8,128)} collective-permute-done((f32[1024,1024]{1,0:T(8,128)}, f32[1024,1024]{1,0:T(8,128)}, u32[]{:S(2)}, u32[]{:S(2)}) %collective-permute-start.50) | collective-permute-done | bytes 4194336 | tf_op jit(solution)/shard_map/ppermute | solution.py:94
  560.1 23.4 %collective-permute-done.21 = f32[256,2048]{1,0:T(8,128)} collective-permute-done((f32[256,2048]{1,0:T(8,128)}, f32[256,2048]{1,0:T(8,128)}, u32[]{:S(2)}, u32[]{:S(2)}) %collective-permute-start.21) | collective-permute-done | bytes 2097184 | tf_op jit(solution)/shard_map/ppermute | solution.py:91
  586.0 42.4 %collective-permute-done.18 = f32[256,2048]{1,0:T(8,128)} collective-permute-done((f32[256,2048]{1,0:T(8,128)}, f32[256,2048]{1,0:T(8,128)}, u32[]{:S(2)}, u32[]{:S(2)}) %collective-permute-start.18) | collective-permute-done | bytes 2097184 | tf_op jit(solution)/shard_map/ppermute | solution.py:91
  631.0 41.6 %collective-permute-done.16 = f32[256,2048]{1,0:T(8,128)S(1)} collective-permute-done((f32[256,2048]{1,0:T(8,128)S(1)}, f32[256,2048]{1,0:T(8,128)S(1)}, u32[]{:S(2)}, u32[]{:S(2)}) %collective-permute-start.16) | collective-permute-done | bytes 2097184 | tf_op jit(solution)/shard_map/ppermute | solution.py:91
  684.7 48.7 %collective-permute-done.49 = f32[1024,1024]{1,0:T(8,128)} collective-permute-done((f32[1024,1024]{1,0:T(8,128)}, f32[1024,1024]{1,0:T(8,128)}, u32[]{:S(2)}, u32[]{:S(2)}) %collective-permute-start.49) | collective-permute-done | bytes 4194336 | tf_op jit(solution)/shard_map/ppermute | solution.py:94
  795.0 11.3 constant_dynamic-slice_fusion.6
  821.6 18.4 %collective-permute-done.27 = f32[1032,128]{1,0:T(8,128)} collective-permute-done((f32[1032,128]{1,0:T(8,128)}, f32[1032,128]{1,0:T(8,128)}, u32[]{:S(2)}, u32[]{:S(2)}) %collective-permute-start.27) | collective-permute-done | bytes 528416 | tf_op jit(solution)/shard_map/ppermute | solution.py:173
  942.3 10.7 copy.157
  971.6 17.3 %collective-permute-done.48 = f32[1024,512]{1,0:T(8,128)} collective-permute-done((f32[1024,512]{1,0:T(8,128)}, f32[1024,512]{1,0:T(8,128)}, u32[]{:S(2)}, u32[]{:S(2)}) %collective-permute-start.48) | collective-permute-done | bytes 2097184 | tf_op jit(solution)/shard_map/ppermute | solution.py:94
  1017.0 41.3 %collective-permute-done.36 = f32[256,2048]{1,0:T(8,128)} collective-permute-done((f32[256,2048]{1,0:T(8,128)}, f32[256,2048]{1,0:T(8,128)}, u32[]{:S(2)}, u32[]{:S(2)}) %collective-permute-start.36) | collective-permute-done | bytes 2097184 | tf_op jit(solution)/shard_map/ppermute | solution.py:91
  1103.2 18.7 %collective-permute-done.41 = f32[4224]{0:T(1024)S(1)} collective-permute-done((f32[4224]{0:T(1024)S(1)}, f32[4224]{0:T(1024)S(1)}, u32[]{:S(2)}, u32[]{:S(2)}) %collective-permute-start.41) | collective-permute-done | bytes 16928 | tf_op jit(solution)/shard_map/ppermute | solution.py:392
  1135.3 52.1 %reduce-scatter.7.cloned.1.call-done = f32[512,768]{1,0:T(8,128)} async-done(((f32[2048,768]{1,0:T(8,128)}), f32[512,768]{1,0:T(8,128)}) %reduce-scatter.7.cloned.1.call-update) | async-done | bytes 1572880 | tf_op jit(solution)/shard_map/reduce_scatter | solution.py:99
  1196.5 11.5 collective-permute-done.47
  (661 shorter events, 591.9 us)
Async XLA Ops:
  7.2 1082.5 %reduce-scatter.15.cloned.1.call-start = ((), (), s32[]{:S(2)}) async-start(), calls=%async_computation.10 | async-start | bytes 5242880 | tf_op jit(solution)/shard_map/reduce_scatter | solution.py:99
  39.4 55.7 %collective-permute-start.6 = (f32[1032,128]{1,0:T(8,128)}, f32[1032,128]{1,0:T(8,128)}, u32[]{:S(2)}, u32[]{:S(2)}) collective-permute-start(f32[1032,128]{1,0:T(8,128)} %pad_maximum_fusion.9), channel_id=1, source_target_pairs={{0,4},{4,0},{8,12},{12,8},{16,20},{20,16},{24,28},{28,24},{1,5},{5... | collective-permute-start | bytes 1585160 | tf_op jit(solution)/shard_map/ppermute | solution.py:94
  157.8 89.7 %collective-permute-start.11 = (f32[256,2048]{1,0:T(8,128)S(1)}, f32[256,2048]{1,0:T(8,128)S(1)}, u32[]{:S(2)}, u32[]{:S(2)}) collective-permute-start(f32[256,2048]{1,0:T(8,128)S(1)} %convolution_add_fusion.11), channel_id=1, source_target_pairs={{0,2},{1,3},{2,0},{3,1},{4,6},{5,7},{6,4},{7,5},{8,10},{9,11},{10,... | collective-permute-start | bytes 6291464 | tf_op jit(solution)/shard_map/ppermute | solution.py:91
  162.2 92.4 %collective-permute-start.51 = (f32[512,2048]{1,0:T(8,128)S(1)}, f32[512,2048]{1,0:T(8,128)}, u32[]{:S(2)}, u32[]{:S(2)}) collective-permute-start(f32[512,2048]{1,0:T(8,128)S(1)} %get-tuple-element.43), channel_id=1, source_target_pairs={{0,4},{4,0},{8,12},{12,8},{16,20},{20,16},{24,28},{28,24},{1,5},{5... | collective-permute-start | bytes 12582920 | tf_op jit(solution)/shard_map/ppermute | solution.py:94
  327.8 764.1 %reduce-scatter.17.cloned.1.call-start = ((), (), s32[]{:S(2)}) async-start(), calls=%async_computation.11 | async-start | bytes 5242880 | tf_op jit(solution)/shard_map/reduce_scatter | solution.py:99
  381.8 745.3 %reduce-scatter.13.cloned.1.call-start = ((), (), s32[]{:S(2)}) async-start(), calls=%async_computation.9 | async-start | bytes 5242880 | tf_op jit(solution)/shard_map/reduce_scatter | solution.py:99
  402.8 82.6 %collective-permute-start.22 = (f32[256,2048]{1,0:T(8,128)}, f32[256,2048]{1,0:T(8,128)}, u32[]{:S(2)}, u32[]{:S(2)}) collective-permute-start(f32[256,2048]{1,0:T(8,128)} %convolution_add_fusion.12), channel_id=1, source_target_pairs={{0,1},{1,0},{2,3},{3,2},{4,5},{5,4},{6,7},{7,6},{8,9},{9,8},{10,11... | collective-permute-start | bytes 6291464 | tf_op jit(solution)/shard_map/ppermute | solution.py:88
  441.9 93.3 %collective-permute-start.50 = (f32[1024,1024]{1,0:T(8,128)}, f32[1024,1024]{1,0:T(8,128)}, u32[]{:S(2)}, u32[]{:S(2)}) collective-permute-start(f32[1024,1024]{1,0:T(8,128)} %fusion.265), channel_id=1, source_target_pairs={{0,4},{4,0},{8,12},{12,8},{16,20},{20,16},{24,28},{28,24},{1,5},{5... | collective-permute-start | bytes 12582920 | tf_op jit(solution)/shard_map/ppermute | solution.py:94
  460.3 81.7 %collective-permute-start.15 = (f32[256,2048]{1,0:T(8,128)}, f32[256,2048]{1,0:T(8,128)}, u32[]{:S(2)}, u32[]{:S(2)}) collective-permute-start(f32[256,2048]{1,0:T(8,128)} %convolution_add_fusion.18), channel_id=1, source_target_pairs={{0,1},{1,0},{2,3},{3,2},{4,5},{5,4},{6,7},{7,6},{8,9},{9,8},{10,11... | collective-permute-start | bytes 6291464 | tf_op jit(solution)/shard_map/ppermute | solution.py:88
  489.8 66.5 %collective-permute-start.23 = (f32[256,2048]{1,0:T(8,128)}, f32[256,2048]{1,0:T(8,128)}, u32[]{:S(2)}, u32[]{:S(2)}) collective-permute-start(f32[256,2048]{1,0:T(8,128)} %fusion.43), channel_id=1, source_target_pairs={{0,2},{1,3},{2,0},{3,1},{4,6},{5,7},{6,4},{7,5},{8,10},{9,11},{10,... | collective-permute-start | bytes 6291464 | tf_op jit(solution)/shard_map/ppermute | solution.py:91
  495.2 88.3 %collective-permute-start.21 = (f32[256,2048]{1,0:T(8,128)}, f32[256,2048]{1,0:T(8,128)}, u32[]{:S(2)}, u32[]{:S(2)}) collective-permute-start(f32[256,2048]{1,0:T(8,128)} %fusion.42), channel_id=1, source_target_pairs={{0,2},{1,3},{2,0},{3,1},{4,6},{5,7},{6,4},{7,5},{8,10},{9,11},{10,... | collective-permute-start | bytes 6291464 | tf_op jit(solution)/shard_map/ppermute | solution.py:91
  500.6 127.8 %collective-permute-start.18 = (f32[256,2048]{1,0:T(8,128)}, f32[256,2048]{1,0:T(8,128)}, u32[]{:S(2)}, u32[]{:S(2)}) collective-permute-start(f32[256,2048]{1,0:T(8,128)} %fusion.41), channel_id=1, source_target_pairs={{0,2},{1,3},{2,0},{3,1},{4,6},{5,7},{6,4},{7,5},{8,10},{9,11},{10,... | collective-permute-start | bytes 6291464 | tf_op jit(solution)/shard_map/ppermute | solution.py:91
  541.7 585.4 %reduce-scatter.11.cloned.1.call-start = ((), (), s32[]{:S(2)}) async-start(), calls=%async_computation.8 | async-start | bytes 5242880 | tf_op jit(solution)/shard_map/reduce_scatter | solution.py:99
  547.1 125.4 %collective-permute-start.16 = (f32[256,2048]{1,0:T(8,128)S(1)}, f32[256,2048]{1,0:T(8,128)S(1)}, u32[]{:S(2)}, u32[]{:S(2)}) collective-permute-start(f32[256,2048]{1,0:T(8,128)S(1)} %fusion.40), channel_id=1, source_target_pairs={{0,2},{1,3},{2,0},{3,1},{4,6},{5,7},{6,4},{7,5},{8,10},{9,11},{10,... | collective-permute-start | bytes 6291464 | tf_op jit(solution)/shard_map/ppermute | solution.py:91
  551.2 132.9 %collective-permute-start.44 = (f32[512,2048]{1,0:T(8,128)}, f32[512,2048]{1,0:T(8,128)}, u32[]{:S(2)}, u32[]{:S(2)}) collective-permute-start(f32[512,2048]{1,0:T(8,128)} %dynamic-slice_convert_fusion), channel_id=1, source_target_pairs={{0,4},{4,0},{8,12},{12,8},{16,20},{20,16},{24,28},{28,24},{1,5},{5... | collective-permute-start | bytes 12582920 | tf_op jit(solution)/shard_map/ppermute | solution.py:94
  556.3 177.1 %collective-permute-start.49 = (f32[1024,1024]{1,0:T(8,128)}, f32[1024,1024]{1,0:T(8,128)}, u32[]{:S(2)}, u32[]{:S(2)}) collective-permute-start(f32[1024,1024]{1,0:T(8,128)} %fusion.264), channel_id=1, source_target_pairs={{0,4},{4,0},{8,12},{12,8},{16,20},{20,16},{24,28},{28,24},{1,5},{5... | collective-permute-start | bytes 12582920 | tf_op jit(solution)/shard_map/ppermute | solution.py:94
  684.0 57.6 %collective-permute-start.24 = (f32[512,2048]{1,0:T(8,128)}, f32[512,2048]{1,0:T(8,128)}, u32[]{:S(2)}, u32[]{:S(2)}) collective-permute-start(f32[512,2048]{1,0:T(8,128)} %get-tuple-element.47), channel_id=1, source_target_pairs={{0,1},{1,0},{2,3},{3,2},{4,5},{5,4},{6,7},{7,6},{8,9},{9,8},{10,11... | collective-permute-start | bytes 12582920 | tf_op jit(solution)/shard_map/ppermute | solution.py:88
  684.2 315.5 %collective-permute-start.45 = (f32[512,2048]{1,0:T(8,128)}, f32[512,2048]{1,0:T(8,128)}, u32[]{:S(2)}, u32[]{:S(2)}) collective-permute-start(f32[512,2048]{1,0:T(8,128)} %collective-permute-done.44), channel_id=1, source_target_pairs={{0,1},{1,0},{2,3},{3,2},{4,5},{5,4},{6,7},{7,6},{8,9},{9,8},{10,11... | collective-permute-start | bytes 12582920 | tf_op jit(solution)/shard_map/ppermute | solution.py:88
  741.2 389.9 %reduce-scatter.9.cloned.1.call-start = ((), (), s32[]{:S(2)}) async-start(), calls=%async_computation.7 | async-start | bytes 2621440 | tf_op jit(solution)/shard_map/reduce_scatter | solution.py:99
  768.3 91.9 %collective-permute-start.31 = (f32[1032,128]{1,0:T(8,128)}, f32[1032,128]{1,0:T(8,128)}, u32[]{:S(2)}, u32[]{:S(2)}) collective-permute-start(f32[1032,128]{1,0:T(8,128)} %pad_maximum_fusion.10), channel_id=1, source_target_pairs={{0,4},{4,0},{8,12},{12,8},{16,20},{20,16},{24,28},{28,24},{1,5},{5... | collective-permute-start | bytes 1585160 | tf_op jit(solution)/shard_map/ppermute | solution.py:94
  971.1 87.3 %collective-permute-start.36 = (f32[256,2048]{1,0:T(8,128)}, f32[256,2048]{1,0:T(8,128)}, u32[]{:S(2)}, u32[]{:S(2)}) collective-permute-start(f32[256,2048]{1,0:T(8,128)} %fusion.39), channel_id=1, source_target_pairs={{0,2},{1,3},{2,0},{3,1},{4,6},{5,7},{6,4},{7,5},{8,10},{9,11},{10,... | collective-permute-start | bytes 6291464 | tf_op jit(solution)/shard_map/ppermute | solution.py:91
  993.2 194.2 %reduce-scatter.7.cloned.1.call-start = ((), (), s32[]{:S(2)}) async-start(), calls=%async_computation.6 | async-start | bytes 7864320 | tf_op jit(solution)/shard_map/reduce_scatter | solution.py:99
  995.1 74.7 %collective-permute-start.46 = (f32[1024,768]{1,0:T(8,128)S(1)}, f32[1024,768]{1,0:T(8,128)}, u32[]{:S(2)}, u32[]{:S(2)}) collective-permute-start(f32[1024,768]{1,0:T(8,128)S(1)} %maximum_convert_fusion), channel_id=1, source_target_pairs={{0,4},{4,0},{8,12},{12,8},{16,20},{20,16},{24,28},{28,24},{1,5},{5... | collective-permute-start | bytes 9437192 | tf_op jit(solution)/shard_map/ppermute | solution.py:94
  1078.2 111.9 %collective-permute-start.39 = (f32[512,2048]{1,0:T(8,128)}, f32[512,2048]{1,0:T(8,128)}, u32[]{:S(2)}, u32[]{:S(2)}) collective-permute-start(f32[512,2048]{1,0:T(8,128)} %get-tuple-element.45), channel_id=1, source_target_pairs={{0,1},{1,0},{2,3},{3,2},{4,5},{5,4},{6,7},{7,6},{8,9},{9,8},{10,11... | collective-permute-start | bytes 12582920 | tf_op jit(solution)/shard_map/ppermute | solution.py:88
  (171 other events, 2737.7 us)
Sparse Core Ops, SparseCore 0:
  328.0 77.9 reduce-scatter.14
  408.4 77.2 reduce-scatter.16
  541.9 77.9 reduce-scatter.12
  741.4 97.4 reduce-scatter.10
  993.3 42.2 reduce-scatter.8
  1078.3 109.0 reduce-scatter.6

commit v2 on v1

v2 whole, which is shorter than its diff:
```python
import functools

import jax
import jax.numpy as jnp
from jax import lax
from jax.experimental import pallas as pl
from jax.experimental.pallas import tpu as pltpu
from jax.sharding import PartitionSpec as P

DH = 128
SEG = 512
DEPTH = 5
EPS = 1e-06

F32 = jnp.float32
BF16 = jnp.bfloat16

AG_CHUNKS = 2
SUM_CHUNKS = 2
ACT_PIECES = (256, 256, 512)
UP_PIECES = (512, 512, 512, 512)


def feature_map(values):
    return jnp.where(values > 0, values + 1.0, jnp.exp(jnp.minimum(values, 0.0)))


def feature_slope(values):
    return jnp.where(values > 0, 1.0, jnp.exp(jnp.minimum(values, 0.0)))


def ancestor_table(seg_parent):
    seg_total = seg_parent.shape[0]
    columns = jnp.arange(seg_total, dtype=jnp.int32)
    current = seg_parent
    lineage_table = jnp.zeros((seg_total, seg_total), F32)
    for _ in range(DEPTH):
        onehot = current[:, None] == columns[None, :]
        lineage_table = lineage_table + onehot.astype(F32)
        lifted = jnp.sum(jnp.where(onehot, seg_parent[None, :], 0), axis=1)
        current = jnp.where(current >= 0, lifted, -1)
    return lineage_table


def dot(a, b):
    return jnp.dot(a, b, preferred_element_type=F32)


def dot_t(a, b):
    return lax.dot_general(a, b, (((0,), (0,)), ((), ())), preferred_element_type=F32)


def dot_nt(a, b):
    return lax.dot_general(a, b, (((1,), (1,)), ((), ())), preferred_element_type=F32)


def after(value, *earlier):
    return lax.optimization_barrier((value, earlier))[0]


def nbytes(*arrays):
    return sum(a.size * a.dtype.itemsize for a in arrays)


def copy_kernel(ids_ref, in_ref, out_ref):
    out_ref[...] = in_ref[...]


def block_columns(v, ids, size):
    if size % 128:
        return jnp.concatenate([lax.dynamic_slice_in_dim(v, i * size, size, 1) for i in ids], 1)
    height, width = v.shape
    return pl.pallas_call(
        copy_kernel,
        out_shape=jax.ShapeDtypeStruct(v.shape, v.dtype),
        grid_spec=pltpu.PrefetchScalarGridSpec(
            num_scalar_prefetch=1,
            grid=(width // size,),
            in_specs=[pl.BlockSpec((height, size), lambda k, ids: (0, ids[k]))],
            out_specs=pl.BlockSpec((height, size), lambda k, ids: (0, k)),
        ),
        cost_estimate=pl.CostEstimate(flops=0, transcendentals=0, bytes_accessed=2 * nbytes(v)),
    )(jnp.stack(ids), v)


SMEM = pl.BlockSpec(memory_space=pltpu.SMEM)


def causal_mask():
    row = lax.broadcasted_iota(jnp.int32, (SEG, SEG), 0)
    col = lax.broadcasted_iota(jnp.int32, (SEG, SEG), 1)
    return row >= col


def softmax_rows(q, k, scale):
    scores = dot_nt(q, k) * scale
    scores = jnp.where(causal_mask(), scores, -1e30)
    top = jnp.max(scores, axis=-1, keepdims=True)
    e = jnp.exp(scores - top)
    return e * (1.0 / jnp.sum(e, axis=-1, keepdims=True))


def head_part(heads, p):
    s, h = p // heads, p % heads
    return pl.ds(pl.multiple_of(s * SEG, SEG), SEG), pl.ds(pl.multiple_of(h * DH, DH), DH)


def matrix_part(p):
    return pl.ds(pl.multiple_of(p * DH, DH), DH)


def weighted(w_ref, p, heads, segs, blocks_ref):
    s, h = p // heads, p % heads
    pairs = segs * heads
    big = jnp.zeros((DH, DH), F32)
    small = jnp.zeros((1, DH), F32)
    for d in range(blocks_ref.shape[0]):
        for n in range(segs):
            w = w_ref[s, d * segs + n]
            o = n * heads + h
            big = big + w * blocks_ref[d, matrix_part(o), :]
            small = small + w * blocks_ref[d, pl.ds(pairs * DH + o, 1), :]
    return big, small


def spread_order(dp):
    low = [0]
    for b in reversed(range(1, dp.bit_length() - 1)):
        low = low + [v ^ (1 << b) for v in low]
    return low + [v ^ 1 for v in low]


def greet(dp):
    me = lax.axis_index("dp")
    barrier = pltpu.get_barrier_semaphore()
    bits = dp.bit_length() - 1
    for b in range(bits):
        pl.semaphore_signal(
            barrier,
            inc=1,
            device_id={"dp": me ^ (1 << b)},
            device_id_type=pl.DeviceIdType.MESH,
        )
    pl.semaphore_wait(barrier, bits)


def spread(dp, blocks_ref, send_sem, recv_sem, compute):
    me = lax.axis_index("dp")
    slot = {j: k for k, j in enumerate(spread_order(dp))}
    copies = {}

    def send(j, mask):
        to = j ^ mask
        k = slot[to]
        copies[to] = pltpu.make_async_remote_copy(
            src_ref=blocks_ref.at[slot[j]],
            dst_ref=blocks_ref.at[k],
            send_sem=send_sem.at[k],
            recv_sem=recv_sem.at[k],
            device_id={"dp": me ^ mask},
            device_id_type=pl.DeviceIdType.MESH,
        )
        copies[to].start()

    bits = [1 << b for b in range(1, dp.bit_length() - 1)]
    for m in bits:
        send(0, m)
    send(0, 1)
    compute()
    for m in bits:
        copies[m].wait_recv()
        if m == bits[-1]:
            near = [0, m]
            for n in reversed(bits[:-1]):
                for j in near[1:]:
                    send(j, n)
                near = near + [n] + [j ^ n for j in near[1:]]
                if n != bits[0]:
                    for j in near:
                        if j & n and j != n:
                            copies[j].wait_recv()
        send(m, 1)
    last = [j for j in near if j and j not in bits]
    for j in last:
        if j & bits[0] or len(bits) == 1:
            copies[j].wait_recv()
        send(j, 1)
    for j in near:
        copies[j ^ 1].wait_recv()
    for c in copies.values():
        c.wait_send()


def attention_kernel(
    dp, heads, segs, scale, w_ref, g_ref, q_ref, k_ref, v_ref,
    a16_ref, a32_ref, local_ref, mem_ref, zin_ref, blocks_ref, send_sem, recv_sem,
):
    pairs = segs * heads
    greet(dp)

    @pl.loop(0, pairs)
    def _(p):
        at = head_part(heads, p)
        sk = feature_map(k_ref[at].astype(F32))
        blocks_ref[0, matrix_part(p), :] = dot_t(sk.astype(BF16), v_ref[at])
        blocks_ref[0, pl.ds(pairs * DH + p, 1), :] = jnp.sum(sk, axis=0, keepdims=True)

    def compute():
        @pl.loop(0, pairs)
        def _(p):
            at = head_part(heads, p)
            probs = softmax_rows(q_ref[at], k_ref[at], scale)
            local_ref[at] = dot(probs.astype(BF16), v_ref[at])

    spread(dp, blocks_ref, send_sem, recv_sem, compute)

    @pl.loop(0, pairs)
    def _(p):
        at = head_part(heads, p)
        mem, zin = weighted(w_ref, p, heads, segs, blocks_ref)
        mem_ref[matrix_part(p), :] = mem
        zin_ref[pl.ds(p, 1), :] = zin
        g = g_ref[0, p % heads]
        sq = feature_map(q_ref[at].astype(F32))
        den = jnp.sum(sq * zin, axis=-1, keepdims=True) + 1.0
        retrieved = dot(sq.astype(BF16), mem.astype(BF16)) / den
        mixed = (g * retrieved + (1.0 - g) * local_ref[at]).astype(BF16)
        a16_ref[at] = mixed
        a32_ref[at] = mixed.astype(F32)


def attention_back_kernel(
    dp, heads, segs, scale, w_ref, g_ref, q_ref, k_ref, v_ref, da_ref, local_ref, mem_ref, zin_ref,
    dq_ref, dk_ref, dv_ref, gate_ref, dqm_ref, dkl_ref, dvl_ref, blocks_ref, send_sem, recv_sem,
):
    pairs = segs * heads
    greet(dp)

    @pl.loop(0, pairs)
    def _(p):
        at = head_part(heads, p)
        g = g_ref[0, p % heads]
        qf = q_ref[at].astype(F32)
        sq = feature_map(qf)
        sq16 = sq.astype(BF16)
        mem16 = mem_ref[matrix_part(p), :].astype(BF16)
        zin = zin_ref[pl.ds(p, 1), :]
        inv_den = 1.0 / (jnp.sum(sq * zin, axis=-1, keepdims=True) + 1.0)
        retrieved = dot(sq16, mem16) * inv_den
        da = da_ref[at].astype(F32)
        gate_ref[pl.ds(p, 1), :] = jnp.sum(da * (retrieved - local_ref[at]), axis=0, keepdims=True)
        dnum = g * da * inv_den
        dden = -jnp.sum(dnum * retrieved, axis=-1, keepdims=True)
        dnum16 = dnum.astype(BF16)
        blocks_ref[0, matrix_part(p), :] = dot_t(sq16, dnum16)
        blocks_ref[0, pl.ds(pairs * DH + p, 1), :] = jnp.sum(sq * dden, axis=0, keepdims=True)
        dsq = dot_nt(dnum16, mem16) + dden * zin
        dqm_ref[at] = dsq * feature_slope(qf)

    def compute():
        @pl.loop(0, pairs)
        def _(p):
            at = head_part(heads, p)
            g = g_ref[0, p % heads]
            q, k, v, da = q_ref[at], k_ref[at], v_ref[at], da_ref[at]
            probs = softmax_rows(q, k, scale)
            dprobs = (1.0 - g) * dot_nt(da, v)
            inner = jnp.sum(dprobs * probs, axis=-1, keepdims=True)
            ds16 = (probs * (dprobs - inner)).astype(BF16)
            dq_ref[at] = (dot(ds16, k) * scale + dqm_ref[at]).astype(BF16)
            dkl_ref[at] = dot_t(ds16, q) * scale
            dvl_ref[at] = (1.0 - g) * dot_t(probs.astype(BF16), da)

    spread(dp, blocks_ref, send_sem, recv_sem, compute)

    @pl.loop(0, pairs)
    def _(p):
        at = head_part(heads, p)
        dd, dz = weighted(w_ref, p, heads, segs, blocks_ref)
        dd16 = dd.astype(BF16)
        kf = k_ref[at].astype(F32)
        dsk = dot_nt(v_ref[at], dd16) + dz
        dk_ref[at] = (dkl_ref[at] + dsk * feature_slope(kf)).astype(BF16)
        dv_ref[at] = (dvl_ref[at] + dot(feature_map(kf).astype(BF16), dd16)).astype(BF16)


def greet_core():
    me = lax.axis_index("tensor")
    barrier = pltpu.get_barrier_semaphore()
    pl.semaphore_signal(
        barrier, inc=1, device_id={"tensor": me ^ 1}, device_id_type=pl.DeviceIdType.MESH
    )
    pl.semaphore_wait(barrier, 1)
    return me ^ 1


def core_copy(peer, src, dst, send_sem, recv_sem):
    return pltpu.make_async_remote_copy(
        src_ref=src,
        dst_ref=dst,
        send_sem=send_sem,
        recv_sem=recv_sem,
        device_id={"tensor": peer},
        device_id_type=pl.DeviceIdType.MESH,
    )


def core_sum_kernel(transposed, tiles, l_ref, w_ref, out_ref, send_ref, recv_ref, send_sem, recv_sem):
    peer = greet_core()
    half = out_ref.shape[0]
    size = out_ref.shape[1] // tiles
    copies = []

    def term(rows, c):
        cols = slice(c * size, (c + 1) * size)
        if transposed:
            return dot_nt(l_ref[rows, :], w_ref[cols, :])
        return dot(l_ref[rows, :], w_ref[:, cols])

    for c in range(tiles):
        send_ref[c] = term(slice(half, 2 * half), c)
        copies.append(
            core_copy(peer, send_ref.at[c], recv_ref.at[c], send_sem.at[c], recv_sem.at[c])
        )
        copies[-1].start()
    for c in range(tiles):
        part = term(slice(0, half), c)
        copies[c].wait_recv()
        out_ref[:, c * size : (c + 1) * size] = part + recv_ref[c]
    for c in copies:
        c.wait_send()


def core_sum(ident, lhs, w, transposed):
    tokens = lhs.shape[0]
    half = tokens // 2
    n = w.shape[0] if transposed else w.shape[1]
    tiles = 4
    out = jax.ShapeDtypeStruct((half, n), F32)
    full = pl.BlockSpec(memory_space=pltpu.VMEM)
    return pl.pallas_call(
        functools.partial(core_sum_kernel, transposed, tiles),
        out_shape=out,
        in_specs=[full, full],
        out_specs=full,
        scratch_shapes=[
            pltpu.VMEM((tiles, half, n // tiles), F32),
            pltpu.VMEM((tiles, half, n // tiles), F32),
            pltpu.SemaphoreType.DMA((tiles,)),
            pltpu.SemaphoreType.DMA((tiles,)),
        ],
        compiler_params=pltpu.CompilerParams(
            collective_id=ident, has_side_effects=True, vmem_limit_bytes=52 << 20
        ),
        cost_estimate=pl.CostEstimate(
            flops=2 * tokens * w.size, transcendentals=0, bytes_accessed=nbytes(lhs, w, out)
        ),
    )(lhs, w)


def core_gather_kernel(norm, tiles, v_ref, gain_ref, out_ref, send_ref, recv_ref, send_sem, recv_sem):
    peer = greet_core()
    half = v_ref.shape[0]
    size = half // tiles
    copies = []
    for c in range(tiles):
        rows = slice(c * size, (c + 1) * size)
        v = v_ref[rows, :]
        if norm:
            inv = lax.rsqrt(jnp.mean(v * v, axis=-1, keepdims=True) + EPS)
            v = v * inv * gain_ref[...]
            send_ref[rows, :] = v
        out_ref[rows, :] = v.astype(BF16)
        src = send_ref if norm else v_ref
        copies.append(
            core_copy(
                peer, src.at[rows, :], recv_ref.at[rows, :], send_sem.at[c], recv_sem.at[c]
            )
        )
        copies[-1].start()
    for c in range(tiles):
        rows = slice(c * size, (c + 1) * size)
        copies[c].wait_recv()
        out_ref[half + c * size : half + (c + 1) * size, :] = recv_ref[rows, :].astype(BF16)
    for c in copies:
        c.wait_send()


def core_gather(ident, v, gain=None):
    half, n = v.shape
    tiles = 4
    out = jax.ShapeDtypeStruct((2 * half, n), BF16)
    full = pl.BlockSpec(memory_space=pltpu.VMEM)
    norm = gain is not None
    return pl.pallas_call(
        functools.partial(core_gather_kernel, norm, tiles),
        out_shape=out,
        in_specs=[full, full],
        out_specs=full,
        scratch_shapes=[
            pltpu.VMEM((half, n) if norm else (8, DH), F32),
            pltpu.VMEM((half, n), F32),
            pltpu.SemaphoreType.DMA((tiles,)),
            pltpu.SemaphoreType.DMA((tiles,)),
        ],
        compiler_params=pltpu.CompilerParams(
            collective_id=ident, has_side_effects=True, vmem_limit_bytes=48 << 20
        ),
        cost_estimate=pl.CostEstimate(
            flops=0, transcendentals=0, bytes_accessed=nbytes(v, v, v, out)
        ),
    )(v, gain[None, :] if norm else jnp.zeros((8, DH), F32))


def feed_kernel(wire, off_ref, h_ref, w_ref, u_ref, *refs):
    act_ref, dpre_ref, extra_ref = refs[-3:]
    pre = dot(h_ref[...], w_ref[...])
    c = 0.7978845608028654
    sq = pre * pre
    th = jnp.tanh(c * pre * (1.0 + 0.044715 * sq))
    half = 0.5 * (1.0 + th)
    act = (pre * half).astype(BF16)
    act_ref[...] = act
    extra_ref[...] = act.astype(F32) if wire else act
    slope = half + 0.5 * pre * (1.0 - th * th) * (c * (1.0 + 0.134145 * sq))
    dpre_ref[...] = (u_ref[...] * slope).astype(BF16)


def feed(h2, w_up, up_grad, offset, count, tile, wire, held):
    tokens, width = h2.shape
    units = w_up.shape[1]
    full = jax.ShapeDtypeStruct((tokens, units), BF16)
    extra = jax.ShapeDtypeStruct((tokens, count), F32 if wire else BF16)
    at = lambda j, off: (0, off[0] + j)
    held = list(held)
    return pl.pallas_call(
        functools.partial(feed_kernel, wire),
        out_shape=[full, full, extra],
        grid_spec=pltpu.PrefetchScalarGridSpec(
            num_scalar_prefetch=1,
            grid=(count // tile,),
            in_specs=[
                pl.BlockSpec((tokens, width), lambda j, off: (0, 0)),
                pl.BlockSpec((width, tile), at),
                pl.BlockSpec((tokens, tile), at),
            ]
            + [pl.BlockSpec(memory_space=pl.ANY)] * len(held),
            out_specs=[
                pl.BlockSpec((tokens, tile), at),
                pl.BlockSpec((tokens, tile), at),
                pl.BlockSpec((tokens, tile), lambda j, off: (0, j)),
            ],
        ),
        input_output_aliases={4: 0, 5: 1} if held else {},
        compiler_params=pltpu.CompilerParams(vmem_limit_bytes=48 << 20),
        cost_estimate=pl.CostEstimate(
            flops=2 * tokens * width * count,
            transcendentals=tokens * count,
            bytes_accessed=2 * width * (tokens + count) + 12 * tokens * count,
        ),
    )((offset // tile)[None], h2, w_up, up_grad, *held)


def body(
    inputs,
    gain_attn,
    w_query,
    w_key,
    w_value,
    gate_logit,
    w_out,
    gain_mlp,
    w_up,
    w_down,
    seg_parent,
    out_grad,
):
    tokens, width = inputs.shape
    half = tokens // 2
    segs = tokens // SEG
    heads = w_query.shape[1] // DH
    pairs = segs * heads
    units = w_up.shape[1]
    flat = heads * DH
    scale = DH ** (-0.5)
    dp = lax.axis_size("dp")
    tn = lax.axis_size("tensor")
    rows = width // dp
    di = lax.axis_index("dp")
    core = lax.axis_index("tensor") % 2

    one = jnp.where(seg_parent[0] < tokens * dp, 1.0, 2.0)

    def low_after_wire(v):
        return (v * one).astype(BF16)

    def swap_core(v):
        return lax.ppermute(v, "tensor", [(i, i ^ 1) for i in range(tn)])

    def swap_y(v):
        return lax.ppermute(v, "tensor", [(i, i ^ 2) for i in range(tn)])

    def swap_dp(v, mask):
        return lax.ppermute(v, "dp", [(i, i ^ mask) for i in range(dp)])

    z_groups = [[z * 2 + x for z in range(dp // 2)] for x in range(2)]

    def scatter_z(v):
        return lax.psum_scatter(v, "dp", scatter_dimension=0, axis_index_groups=z_groups, tiled=True)

    xi = di % 2

    def columns(v):
        ids = [2 * z + 1 - xi for z in range(dp // 2)] + [2 * z + xi for z in range(dp // 2)]
        return block_columns(v, ids, rows)

    cut = width // 2

    class Reduce:
        def __init__(self, lhs, rhs):
            self.lhs, self.rhs = lhs, rhs
            self.term = dot_t(lhs[:, :cut], rhs)
            self.got = swap_dp(self.term, 1)

        def scatter(self, *earlier):
            got = after(self.got, *earlier)
            self.part = dot_t(self.lhs[:, cut:], self.rhs) + got
            self.out = scatter_z(self.part)
            return self.part

    def pick(v, index, axis):
        size = v.shape[axis] // 2
        return lax.dynamic_slice_in_dim(v, index * size, size, axis)

    def place(own, other, index, axis):
        return jnp.where(
            index == 0,
            jnp.concatenate([own, other], axis),
            jnp.concatenate([other, own], axis),
        )

    def inv_rms(v):
        return lax.rsqrt(jnp.mean(v * v, axis=-1, keepdims=True) + EPS)

    w_out_all = lax.all_gather(w_out.astype(F32), "tensor", axis=0, tiled=True)

    x_own = pick(inputs, core, 0).astype(F32)
    x_oth = pick(inputs, 1 - core, 0).astype(F32)
    inv_own = inv_rms(x_own)
    inv_oth = inv_rms(x_oth)
    h1 = jnp.concatenate(
        [
            (x_own * inv_own * gain_attn).astype(BF16),
            (x_oth * inv_oth * gain_attn).astype(BF16),
        ],
        0,
    )

    def project(matrix):
        return dot(h1, matrix).astype(BF16)

    qh = project(w_query)
    kh = project(w_key)
    vh = project(w_value)

    sub = segs // 2
    every = jnp.arange(seg_parent.shape[0], dtype=jnp.int32)
    sub_ids = jnp.arange(sub, dtype=jnp.int32)
    seg_local = jnp.concatenate([core * sub + sub_ids, (1 - core) * sub + sub_ids])
    order = spread_order(dp)
    ids = jnp.concatenate([(di ^ j) * segs + seg_local for j in order])
    mine_hot = (ids[:segs, None] == every[None, :]).astype(F32)
    ids_hot = (ids[:, None] == every[None, :]).astype(F32)
    lineage = ancestor_table(seg_parent)

    def weights_of(table):
        mine_rows = jnp.sum(mine_hot[:, :, None] * table[None], axis=1)
        return jnp.sum(mine_rows[:, None, :] * ids_hot[None], axis=-1)

    up_weight = weights_of(lineage)
    down_weight = weights_of(lineage.T)

    gate = jax.nn.sigmoid(gate_logit)
    gate_row = gate[None, :]

    og_own = pick(out_grad, core, 0)
    og = jnp.concatenate([og_own, pick(out_grad, 1 - core, 0)], 0)
    block_rows = pairs * DH + pairs
    act_f32 = jax.ShapeDtypeStruct((tokens, flat), F32)
    act_b16 = jax.ShapeDtypeStruct((tokens, flat), BF16)
    mem_shape = jax.ShapeDtypeStruct((pairs * DH, DH), F32)
    zin_shape = jax.ShapeDtypeStruct((pairs, DH), F32)
    full = pl.BlockSpec(memory_space=pltpu.VMEM)

    def attention_call(kernel, ident, outs, scratch, args, n_smem, flops):
        return pl.pallas_call(
            functools.partial(kernel, dp, heads, segs, scale),
            out_shape=outs,
            in_specs=[SMEM] * n_smem + [full] * (len(args) - n_smem),
            out_specs=[full] * len(outs),
            scratch_shapes=scratch
            + [
                pltpu.VMEM((dp, block_rows, DH), F32),
                pltpu.SemaphoreType.DMA((dp,)),
                pltpu.SemaphoreType.DMA((dp,)),
            ],
            compiler_params=pltpu.CompilerParams(
                collective_id=ident, has_side_effects=True, vmem_limit_bytes=56 << 20
            ),
            cost_estimate=pl.CostEstimate(
                flops=flops, transcendentals=0, bytes_accessed=64 << 20
            ),
        )(*args)

    head_flops = 2 * segs * heads * SEG * SEG * DH
    a16, a32, local, memory, zin = attention_call(
        attention_kernel,
        0,
        [act_b16, act_f32, act_f32, mem_shape, zin_shape],
        [],
        (up_weight, gate_row, qh, kh, vh),
        2,
        3 * head_flops,
    )
    og_pair = lax.all_gather(
        after(og_own, a32).astype(F32), "dp", axis=0, tiled=True,
        axis_index_groups=[[2 * i, 2 * i + 1] for i in range(dp // 2)],
    )

    up_grad = dot_nt(og, after(w_down, a32))

    step = half // AG_CHUNKS
    a_core = [
        swap_core(a32[half + c * step : half + (c + 1) * step]) for c in range(AG_CHUNKS)
    ]
    a_pair = [
        jnp.concatenate([a32[c * step : (c + 1) * step], a_core[c]], 1) for c in range(AG_CHUNKS)
    ]
    a_far = [swap_y(v) for v in a_pair]
    ti = lax.axis_index("tensor")

    def w_rows(j):
        return low_after_wire(lax.dynamic_slice_in_dim(w_out_all, (ti ^ j) * flat, flat, 0))

    w_out_core = w_rows(1)
    w_out_far = jnp.concatenate([w_rows(2), w_rows(3)], 0)
    near = [
        x_own[c * step : (c + 1) * step]
        + dot(a16[c * step : (c + 1) * step], w_out)
        + dot(low_after_wire(a_core[c]), w_out_core)
        for c in range(AG_CHUNKS)
    ]
    h1_a = columns(after(h1, up_grad))
    resids = [
        n + dot(low_after_wire(after(f, w_out_far, h1_a)), w_out_far)
        for n, f in zip(near, a_far)
    ]
    resid = jnp.concatenate(resids, 0)
    inv_mlp = inv_rms(resid)
    h2 = core_gather(1, resid, gain_mlp)

    part = units // 2
    held = ()
    act_b = []
    at = (1 - xi) * part
    for n in ACT_PIECES:
        act, dpre, wire = feed(h2, w_up, up_grad, at, n, 256, True, held)
        held = (act, dpre)
        act_b.append(swap_dp(wire, 1))
        at = at + n
    act, dpre, act_keep = feed(h2, w_up, up_grad, xi * part, part, 256, False, held)

    def tensor_sum_start(ident, lhs, w, transposed):
        total = core_sum(ident, lhs, w, transposed)
        size = half // SUM_CHUNKS
        parts = [total[c * size : (c + 1) * size] for c in range(SUM_CHUNKS)]
        return [(p, swap_y(p)) for p in parts]

    def tensor_sum_end(parts, *earlier):
        return jnp.concatenate([p + after(r, *earlier) for p, r in parts], 0)

    dh2_parts = tensor_sum_start(2, dpre, w_up, True)
    sent = [p for p, _ in dh2_parts]

    h2_a = columns(after(h2, *sent))
    up = []
    starts = [0]
    for n in UP_PIECES:
        starts.append(starts[-1] + n)

    def up_piece(p, *earlier):
        up.append(Reduce(h2_a, after(dpre, *earlier)[:, starts[p] : starts[p + 1]]))
        return up[-1].term

    og_b_own = lax.dynamic_slice_in_dim(og_pair, (1 - xi) * half, half, 0)
    og_b = core_gather(3, after(og_b_own, h2_a))
    down = []

    def down_piece(p, *earlier):
        lo = sum(ACT_PIECES[:p])
        piece = act_keep[:, lo : lo + ACT_PIECES[p]]
        got = low_after_wire(after(act_b[p], *earlier))
        total = dot_t(og, piece) + dot_t(og_b, got)
        down.append(scatter_z(total))
        return total

    e = up_piece(0, *sent)
    e = down_piece(0, e)
    e = up_piece(1, e)
    e = down_piece(1, e)

    dh2 = tensor_sum_end(dh2_parts, e)
    gs = dh2 * gain_mlp
    dresid = (
        og_own.astype(F32)
        + inv_mlp * gs
        - resid * inv_mlp * inv_mlp * inv_mlp * jnp.mean(gs * resid, axis=-1, keepdims=True)
    )
    gain_mlp_part = jnp.sum(dh2 * resid * inv_mlp, axis=0)
    dr = core_gather(4, dresid)

    e = down_piece(2, dr)
    da = dot_nt(after(dr, e), w_out).astype(BF16)
    e = up[0].scatter(da)
    e = up_piece(2, e)
    dq16, dk16, dv16, gate_rows = attention_call(
        attention_back_kernel,
        5,
        [act_b16, act_b16, act_b16, zin_shape],
        [pltpu.VMEM((tokens, flat), F32)] * 3,
        (down_weight, gate_row, qh, kh, vh, after(da, e), local, memory, zin),
        2,
        9 * head_flops,
    )
    gate_part = jnp.sum(gate_rows.reshape(segs, heads, DH), axis=(0, 2)) * gate * (1.0 - gate)

    e = up[1].scatter(dq16)
    e = up_piece(3, e)
    out_w = Reduce(columns(after(dr, e)), a16)

    out_parts = tensor_sum_start(6, after(act, out_w.term), w_down, False)
    query = Reduce(h1_a, after(dq16, *[p for p, _ in out_parts]))

    w_qkv = jnp.concatenate([after(w, up_grad) for w in (w_query, w_key, w_value)], 1)
    d_qkv = jnp.concatenate([dq16, dk16, dv16], 1)
    dh1_parts = tensor_sum_start(7, after(d_qkv, query.term), w_qkv, True)
    sent = [p for p, _ in dh1_parts]
    e = up[2].scatter(*sent)
    key = Reduce(h1_a, after(dk16, e))
    e = up[3].scatter(key.term)
    value = Reduce(h1_a, after(dv16, e))
    e = out_w.scatter(value.term)

    out_own = (resid + tensor_sum_end(out_parts, e)).astype(BF16)
    outputs = place(out_own, low_after_wire(swap_core(out_own.astype(F32))), core, 0)

    e = query.scatter(out_own)
    e = key.scatter(e)

    dh1 = tensor_sum_end(dh1_parts, e)
    gs1 = dh1 * gain_attn
    dx = (
        dresid
        + inv_own * gs1
        - x_own * inv_own * inv_own * inv_own * jnp.mean(gs1 * x_own, axis=-1, keepdims=True)
    )
    gain_attn_part = jnp.sum(dh1 * x_own * inv_own, axis=0)
    dx_own = dx.astype(BF16)
    input_grad = place(dx_own, low_after_wire(swap_core(dx_own.astype(F32))), core, 0)

    e = value.scatter(dx_own)

    down = jnp.concatenate(down, 1)
    down_theirs = swap_dp(pick(down, 1 - xi, 0), 1)
    w_down_grad = place(pick(down, xi, 0), down_theirs, xi, 1).T
    w_up_grad = jnp.concatenate([v.out for v in up], 1)
    w_out_grad = out_w.out.T
    w_query_grad, w_key_grad, w_value_grad = query.out, key.out, value.out

    gains = jnp.concatenate([gain_attn_part, gain_mlp_part])
    small = jnp.concatenate([gains + swap_core(gains), jnp.pad(gate_part, (0, DH - heads))])
    bit = 1
    while bit < dp:
        small = small + swap_dp(small, bit)
        bit *= 2
    gain_attn_grad = lax.dynamic_slice_in_dim(small, di * rows, rows, 0)
    gain_mlp_grad = lax.dynamic_slice_in_dim(small, width + di * rows, rows, 0)
    gate_grad = small[2 * width : 2 * width + heads]

    return (
        outputs,
        input_grad,
        gain_attn_grad,
        w_query_grad,
        w_key_grad,
        w_value_grad,
        gate_grad,
        w_out_grad,
        gain_mlp_grad,
        w_up_grad,
        w_down_grad,
    )


def solution(mesh):
    placed = (
        P("dp", None),
        P(),
        P(None, "tensor"),
        P(None, "tensor"),
        P(None, "tensor"),
        P("tensor"),
        P("tensor", None),
        P(),
        P(None, "tensor"),
        P("tensor", None),
        P(),
        P("dp", None),
    )
    return jax.shard_map(
        body,
        mesh=mesh,
        in_specs=placed,
        out_specs=(
            P("dp", None),
            P("dp", None),
            P("dp"),
            P("dp", "tensor"),
            P("dp", "tensor"),
            P("dp", "tensor"),
            P("tensor"),
            P("tensor", "dp"),
            P("dp"),
            P("dp", "tensor"),
            P("tensor", "dp"),
        ),
        check_vma=False,
    )
```

time: 1230 us -> 1190 us (0.967)
  Pallas kernels: 0 us -> 334 us
  local copies, waits for them, and re-layouts: 200 us -> 47.4 us
  matrix products: 242 us -> 115 us
  waiting for transfers between devices: 567 us -> 531 us
  starting transfers between devices: 76.4 us -> 41.9 us
  other arithmetic: 116 us -> 98.4 us
    pallas_call x0 -> x15, Pallas kernels: none -> 334 us  [the longest x2 202 us: attention_call(): pl.pallas_call(functools.partial(kernel, dp, heads, segs, scale), out_sha...]
    all_gather x0 -> x2, waiting for transfers between devices: none -> 156 us  [the longest x1 103 us: body(): w_out_all = lax.all_gather(w_out.astype(F32), 'tensor', axis=0, tiled=True)]
    ppermute x33 -> x15, waiting for transfers between devices: 259 us -> 189 us  [swap_dp(): return lax.ppermute(v, 'dp', [(i, i ^ mask) for i in range(dp)])]
    dot_general x23 -> x2, matrix products: 83 us -> 16.9 us  [dot_nt(): lax.dot_general(a, b, (((1,), (1,)), ((), ())), preferred_element_type=F32)]
    ppermute x8, waiting for transfers between devices: 239 us -> 185 us  [swap_y(): return lax.ppermute(v, 'tensor', [(i, i ^ 2) for i in range(tn)])]
    unnamed x277 -> x150, local copies, waits for them, and re-layouts: 71.8 us -> 19.2 us
    reduce_scatter x6 -> x11, waiting for transfers between devices: 52.1 us -> 0.02 us  [scatter_z(): lax.psum_scatter(v, 'dp', scatter_dimension=0, axis_index_groups=z_groups...]
    ppermute x33 -> x15, starting transfers between devices: 62.5 us -> 19.8 us  [swap_dp(): return lax.ppermute(v, 'dp', [(i, i ^ mask) for i in range(dp)])]
  transfers between devices with their start and end apart: 62 -> 41, of which waited for: 28 -> 18; matrix products, arithmetic and copies ran while one was open for 41% -> 17% of each run, Pallas kernels for 0% -> 21%
where the time goes in v2:
time: 1190 us; the launch traced here: 1180 us
  waiting for transfers between devices  531 us (45%)
  Pallas kernels  334 us (28%)
  matrix products  115 us (10%)
  other arithmetic  98.4 us (8%)
  local copies, waits for them, and re-layouts  47.4 us (4%)
  starting transfers between devices  41.9 us (4%)
  between operations  15.1 us (1%)
    pallas_call x2, Pallas kernels, attention_call(): pl.pallas_call(functools.partial(kernel, dp, heads, segs, scale), out_sha...  202 us
    ppermute x15, waiting for transfers between devices, swap_dp(): return lax.ppermute(v, 'dp', [(i, i ^ mask) for i in range(dp)])  189 us
    ppermute x8, waiting for transfers between devices, swap_y(): return lax.ppermute(v, 'tensor', [(i, i ^ 2) for i in range(tn)])  185 us
    all_gather x1, waiting for transfers between devices, body(): w_out_all = lax.all_gather(w_out.astype(F32), 'tensor', axis=0, tiled=True)  103 us
    dot_general x22, matrix products, dot_t(): lax.dot_general(a, b, (((0,), (0,)), ((), ())), preferred_element_type=F32)  77 us
    all_gather x1, waiting for transfers between devices, body(): lax.all_gather(after(og_own, a32).astype(F32), 'dp', axis=0, tiled=True,...  52.8 us
    pallas_call x3, Pallas kernels, core_sum(): pl.pallas_call(functools.partial(core_sum_kernel, transposed, tiles), out...  50.4 us
    pallas_call x4, Pallas kernels, feed(): pl.pallas_call(functools.partial(feed_kernel, wire), out_shape=[full, ful...  30.1 us
  transfers between devices with their start and end apart: 41, of which 18 were waited for; matrix products, arithmetic and copies ran while one was open for 17% of the time, Pallas kernels for 21%

profile of v2, /device:TPU:0, one launch (start us, length us, event | category | flops | bytes accessed | tf_op | source)
XLA Modules:
  0.0 1183.3 jit_solution(1897757723970676800)
XLA Ops:
  35.5 73.9 %shard_map.203 = (bf16[1024,512]{1,0:T(8,128)(2,1)}, f32[1024,512]{1,0:T(8,128)}, f32[1024,512]{1,0:T(8,128)}, f32[1024,128]{1,0:T(8,128)}, f32[8,128]{1,0:T(8,128)}) custom-call(f32[2,16]{1,0:T(2,128)} %fusion.88.w_ref, f32[1,4]{1,0:T(1,128)} %fusion.109.g_ref, bf16[1024,512]{1,0:T(8,128)(2,1)} %convolution_convert_fusion.3.q_ref, ...), custom_call_target="tpu_custom_call" | custom-call | flops 1610612736 | bytes 67108864 | tf_op jit(solution)/shard_map/pallas_call | solution.py:596
  114.5 12.0 %reduce-scatter.28.cloned.1.call-start = ((), (), s32[]{:S(2)}) async-start(), calls=%async_computation.21 | async-start | bytes 2621440 | tf_op jit(solution)/shard_map/reduce_scatter | solution.py:509
  129.8 13.6 %fusion.79.u_ref = f32[1024,2048]{1,0:T(8,128)} fusion(bf16[2048,2048]{1,0:T(8,128)(2,1)} %w_ref.11, bf16[512,2048]{1,0:T(8,128)(2,1)S(1)} %copy-done.50, bf16[512,2048]{1,0:T(8,128)(2,1)S(1)} %copy-done.23), kind=kOutput, calls=%fused_computation.187 | convolution fusion | flops 8598323200 | bytes 20971520 | tf_op jit(solution)/shard_map/dot_general | solution.py:54
  160.6 52.8 %all-gather.5.cloned.1.call-done = f32[1024,2048]{1,0:T(8,128)} async-done(((f32[512,2048]{1,0:T(8,128)}), f32[1024,2048]{1,0:T(8,128)}) %all-gather.5.cloned.1.call-update) | async-done | bytes 8388624 | tf_op jit(solution)/shard_map/all_gather | solution.py:625
  218.0 103.5 %all-gather.3.cloned.1.call-done = f32[2048,2048]{1,0:T(8,128)} async-done(((f32[512,2048]{1,0:T(8,128)}), f32[2048,2048]{1,0:T(8,128)}) %all-gather.3.cloned.1.call-update) | async-done | bytes 16777232 | tf_op jit(solution)/shard_map/all_gather | solution.py:545
  337.7 9.7 shard_map.205.h_ref.in_ref
  371.5 11.5 shard_map.209
  384.2 17.7 %shard_map.210 = f32[512,2048]{1,0:T(8,128)} custom-call(bf16[1024,2048]{1,0:T(8,128)(2,1)} %get-tuple-element.108.l_ref, bf16[2048,2048]{1,0:T(8,128)(2,1)} %w_ref.10), custom_call_target="tpu_custom_call" | custom-call | flops 8589934592 | bytes 16777216 | tf_op jit(solution)/shard_map/pallas_call | solution.py:341
  414.3 9.8 shard_map.212
  445.6 15.2 %collective-permute-done.5 = f32[1024,256]{1,0:T(8,128)S(1)} collective-permute-done((f32[1024,256]{1,0:T(8,128)S(1)}, f32[1024,256]{1,0:T(8,128)S(1)}, u32[]{:S(2)}, u32[]{:S(2)}) %collective-permute-start.5) | collective-permute-done | bytes 1048608 | tf_op jit(solution)/shard_map/ppermute | solution.py:504
  471.6 13.1 %collective-permute-done.4 = f32[256,2048]{1,0:T(8,128)} collective-permute-done((f32[256,2048]{1,0:T(8,128)}, f32[256,2048]{1,0:T(8,128)}, u32[]{:S(2)}, u32[]{:S(2)}) %collective-permute-start.4) | collective-permute-done | bytes 2097184 | tf_op jit(solution)/shard_map/ppermute | solution.py:501
  484.8 44.2 %collective-permute-done.7 = f32[256,2048]{1,0:T(8,128)} collective-permute-done((f32[256,2048]{1,0:T(8,128)}, f32[256,2048]{1,0:T(8,128)}, u32[]{:S(2)}, u32[]{:S(2)}) %collective-permute-start.7) | collective-permute-done | bytes 2097184 | tf_op jit(solution)/shard_map/ppermute | solution.py:501
  536.4 9.7 shard_map.213.in_ref
  563.0 39.6 %collective-permute-done.10 = f32[1024,512]{1,0:T(8,128)S(1)} collective-permute-done((f32[1024,512]{1,0:T(8,128)}, f32[1024,512]{1,0:T(8,128)S(1)}, u32[]{:S(2)}, u32[]{:S(2)}) %collective-permute-start.10) | collective-permute-done | bytes 2097184 | tf_op jit(solution)/shard_map/ppermute | solution.py:504
  618.0 127.8 %shard_map.214 = (bf16[1024,512]{1,0:T(8,128)(2,1)}, bf16[1024,512]{1,0:T(8,128)(2,1)}, bf16[1024,512]{1,0:T(8,128)(2,1)}, f32[8,128]{1,0:T(8,128)}) custom-call(f32[2,16]{1,0:T(2,128)} %fusion.89.w_ref, f32[1,4]{1,0:T(1,128)} %fusion.109.g_ref, bf16[1024,512]{1,0:T(8,128)(2,1)} %convolution_convert_fusion.3.q_ref, ...), custom_call_target="tpu_custom_call" | custom-call | flops 4831838208 | bytes 67108864 | tf_op jit(solution)/shard_map/pallas_call | solution.py:596
  770.6 17.6 %shard_map.216 = f32[512,2048]{1,0:T(8,128)} custom-call(bf16[1024,2048]{1,0:T(8,128)(2,1)} %get-tuple-element.110.l_ref, bf16[2048,2048]{1,0:T(8,128)(2,1)} %w_ref.11), custom_call_target="tpu_custom_call" | custom-call | flops 8589934592 | bytes 16777216 | tf_op jit(solution)/shard_map/pallas_call | solution.py:341
  795.6 15.1 %shard_map.217 = f32[512,2048]{1,0:T(8,128)} custom-call(bf16[1024,1536]{1,0:T(8,128)(2,1)} %pad_maximum_fusion.7.l_ref, bf16[2048,1536]{1,0:T(8,128)(2,1)} %pad_maximum_fusion.w_ref), custom_call_target="tpu_custom_call" | custom-call | flops 6442450944 | bytes 13631488 | tf_op jit(solution)/shard_map/pallas_call | solution.py:341
  824.8 40.9 %collective-permute-done.13 = f32[1024,512]{1,0:T(8,128)S(1)} collective-permute-done((f32[1024,512]{1,0:T(8,128)}, f32[1024,512]{1,0:T(8,128)S(1)}, u32[]{:S(2)}, u32[]{:S(2)}) %collective-permute-start.13) | collective-permute-done | bytes 2097184 | tf_op jit(solution)/shard_map/ppermute | solution.py:504
  874.6 40.4 %collective-permute-done.12 = f32[1024,512]{1,0:T(8,128)S(1)} collective-permute-done((f32[1024,512]{1,0:T(8,128)}, f32[1024,512]{1,0:T(8,128)S(1)}, u32[]{:S(2)}, u32[]{:S(2)}) %collective-permute-start.12) | collective-permute-done | bytes 2097184 | tf_op jit(solution)/shard_map/ppermute | solution.py:504
  923.5 42.2 %collective-permute-done.15 = f32[256,2048]{1,0:T(8,128)S(1)} collective-permute-done((f32[256,2048]{1,0:T(8,128)}, f32[256,2048]{1,0:T(8,128)S(1)}, u32[]{:S(2)}, u32[]{:S(2)}) %collective-permute-start.15) | collective-permute-done | bytes 2097184 | tf_op jit(solution)/shard_map/ppermute | solution.py:501
  965.7 42.6 %collective-permute-done.11 = f32[256,2048]{1,0:T(8,128)S(1)} collective-permute-done((f32[256,2048]{1,0:T(8,128)S(1)}, f32[256,2048]{1,0:T(8,128)S(1)}, u32[]{:S(2)}, u32[]{:S(2)}) %collective-permute-start.11) | collective-permute-done | bytes 2097184 | tf_op jit(solution)/shard_map/ppermute | solution.py:501
  1020.7 38.9 %collective-permute-done.18 = f32[1024,512]{1,0:T(8,128)S(1)} collective-permute-done((f32[1024,512]{1,0:T(8,128)}, f32[1024,512]{1,0:T(8,128)S(1)}, u32[]{:S(2)}, u32[]{:S(2)}) %collective-permute-start.18) | collective-permute-done | bytes 2097184 | tf_op jit(solution)/shard_map/ppermute | solution.py:504
  1064.5 41.4 %collective-permute-done.17 = f32[256,2048]{1,0:T(8,128)} collective-permute-done((f32[256,2048]{1,0:T(8,128)}, f32[256,2048]{1,0:T(8,128)}, u32[]{:S(2)}, u32[]{:S(2)}) %collective-permute-start.17) | collective-permute-done | bytes 2097184 | tf_op jit(solution)/shard_map/ppermute | solution.py:501
  1163.3 9.6 collective-permute-done.27
  (347 shorter events, 325.9 us)
Async XLA Ops:
  7.2 206.1 %all-gather.5.cloned.1.call-start = ((), (), s32[]{:S(2)}) async-start(), calls=%async_computation.12 | async-start | bytes 12582912 | tf_op jit(solution)/shard_map/all_gather | solution.py:625
  111.9 209.5 %all-gather.3.cloned.1.call-start = ((), (), s32[]{:S(2)}) async-start(), calls=%async_computation.11 | async-start | bytes 20971520 | tf_op jit(solution)/shard_map/all_gather | solution.py:545
  114.5 1015.7 %reduce-scatter.28.cloned.1.call-start = ((), (), s32[]{:S(2)}) async-start(), calls=%async_computation.21 | async-start | bytes 2621440 | tf_op jit(solution)/shard_map/reduce_scatter | solution.py:509
  147.6 178.6 %collective-permute-start.1 = (f32[256,1024]{1,0:T(8,128)S(1)}, f32[256,1024]{1,0:T(8,128)}, u32[]{:S(2)}, u32[]{:S(2)}) collective-permute-start(f32[256,1024]{1,0:T(8,128)S(1)} %pad_maximum_fusion.9), channel_id=1, source_target_pairs={{0,2},{1,3},{2,0},{3,1},{4,6},{5,7},{6,4},{7,5},{8,10},{9,11},{10,... | collective-permute-start | bytes 3145736 | tf_op jit(solution)/shard_map/ppermute | solution.py:501
  149.4 176.9 %collective-permute-start.3 = (f32[256,1024]{1,0:T(8,128)S(1)}, f32[256,1024]{1,0:T(8,128)}, u32[]{:S(2)}, u32[]{:S(2)}) collective-permute-start(f32[256,1024]{1,0:T(8,128)S(1)} %pad_maximum_fusion.10), channel_id=1, source_target_pairs={{0,2},{1,3},{2,0},{3,1},{4,6},{5,7},{6,4},{7,5},{8,10},{9,11},{10,... | collective-permute-start | bytes 3145736 | tf_op jit(solution)/shard_map/ppermute | solution.py:501
  355.1 76.2 %collective-permute-start.6 = (f32[1024,256]{1,0:T(8,128)}, f32[1024,256]{1,0:T(8,128)}, u32[]{:S(2)}, u32[]{:S(2)}) collective-permute-start(f32[1024,256]{1,0:T(8,128)} %get-tuple-element.90), channel_id=1, source_target_pairs={{0,4},{4,0},{8,12},{12,8},{16,20},{20,16},{24,28},{28,24},{1,5},{5... | collective-permute-start | bytes 3145736 | tf_op jit(solution)/shard_map/ppermute | solution.py:504
  435.2 699.9 %reduce-scatter.30.cloned.1.call-start = ((), (), s32[]{:S(2)}) async-start(), calls=%async_computation.22 | async-start | bytes 2621440 | tf_op jit(solution)/shard_map/reduce_scatter | solution.py:509
  436.3 92.6 %collective-permute-start.7 = (f32[256,2048]{1,0:T(8,128)}, f32[256,2048]{1,0:T(8,128)}, u32[]{:S(2)}, u32[]{:S(2)}) collective-permute-start(f32[256,2048]{1,0:T(8,128)} %get-tuple-element.182), channel_id=1, source_target_pairs={{0,2},{1,3},{2,0},{3,1},{4,6},{5,7},{6,4},{7,5},{8,10},{9,11},{10,... | collective-permute-start | bytes 6291464 | tf_op jit(solution)/shard_map/ppermute | solution.py:501
  463.7 681.7 %reduce-scatter.32.cloned.1.call-start = ((), (), s32[]{:S(2)}) async-start(), calls=%async_computation.23 | async-start | bytes 5242880 | tf_op jit(solution)/shard_map/reduce_scatter | solution.py:509
  463.8 84.3 %collective-permute-start.9 = (f32[1024,512]{1,0:T(8,128)S(1)}, f32[1024,512]{1,0:T(8,128)S(1)}, u32[]{:S(2)}, u32[]{:S(2)}) collective-permute-start(f32[1024,512]{1,0:T(8,128)S(1)} %get-tuple-element.97), channel_id=1, source_target_pairs={{0,4},{4,0},{8,12},{12,8},{16,20},{20,16},{24,28},{28,24},{1,5},{5... | collective-permute-start | bytes 6291464 | tf_op jit(solution)/shard_map/ppermute | solution.py:504
  554.6 597.2 %reduce-scatter.20.cloned.1.call-start = ((), (), s32[]{:S(2)}) async-start(), calls=%async_computation.17 | async-start | bytes 2621440 | tf_op jit(solution)/shard_map/reduce_scatter | solution.py:509
  604.4 547.5 %reduce-scatter.22.cloned.1.call-start = ((), (), s32[]{:S(2)}) async-start(), calls=%async_computation.18 | async-start | bytes 2621440 | tf_op jit(solution)/shard_map/reduce_scatter | solution.py:509
  604.4 141.4 %collective-permute-start.8 = (f32[1024,512]{1,0:T(8,128)}, f32[1024,512]{1,0:T(8,128)S(1)}, u32[]{:S(2)}, u32[]{:S(2)}) collective-permute-start(f32[1024,512]{1,0:T(8,128)} %fusion.37), channel_id=1, source_target_pairs={{0,4},{4,0},{8,12},{12,8},{16,20},{20,16},{24,28},{28,24},{1,5},{5... | collective-permute-start | bytes 6291464 | tf_op jit(solution)/shard_map/ppermute | solution.py:504
  617.4 198.2 %collective-permute-start.14 = (f32[1024,512]{1,0:T(8,128)}, f32[1024,512]{1,0:T(8,128)S(1)}, u32[]{:S(2)}, u32[]{:S(2)}) collective-permute-start(f32[1024,512]{1,0:T(8,128)} %fusion.35), channel_id=1, source_target_pairs={{0,4},{4,0},{8,12},{12,8},{16,20},{20,16},{24,28},{28,24},{1,5},{5... | collective-permute-start | bytes 6291464 | tf_op jit(solution)/shard_map/ppermute | solution.py:504
  747.7 404.1 %reduce-scatter.24.cloned.1.call-start = ((), (), s32[]{:S(2)}) async-start(), calls=%async_computation.19 | async-start | bytes 2621440 | tf_op jit(solution)/shard_map/reduce_scatter | solution.py:509
  817.4 334.4 %reduce-scatter.26.cloned.1.call-start = ((), (), s32[]{:S(2)}) async-start(), calls=%async_computation.20 | async-start | bytes 2621440 | tf_op jit(solution)/shard_map/reduce_scatter | solution.py:509
  867.6 287.4 %reduce-scatter.18.cloned.1.call-start = ((), (), s32[]{:S(2)}) async-start(), calls=%async_computation.16 | async-start | bytes 2621440 | tf_op jit(solution)/shard_map/reduce_scatter | solution.py:509
  916.8 259.8 %reduce-scatter.12.cloned.1.call-start = ((), (), s32[]{:S(2)}) async-start(), calls=%async_computation.13 | async-start | bytes 2621440 | tf_op jit(solution)/shard_map/reduce_scatter | solution.py:509
  917.3 91.0 %collective-permute-start.11 = (f32[256,2048]{1,0:T(8,128)S(1)}, f32[256,2048]{1,0:T(8,128)S(1)}, u32[]{:S(2)}, u32[]{:S(2)}) collective-permute-start(f32[256,2048]{1,0:T(8,128)S(1)} %copy-done.49), channel_id=1, source_target_pairs={{0,2},{1,3},{2,0},{3,1},{4,6},{5,7},{6,4},{7,5},{8,10},{9,11},{10,... | collective-permute-start | bytes 6291464 | tf_op jit(solution)/shard_map/ppermute | solution.py:501
  918.9 93.1 %collective-permute-start.19 = (f32[1024,512]{1,0:T(8,128)}, f32[1024,512]{1,0:T(8,128)S(1)}, u32[]{:S(2)}, u32[]{:S(2)}) collective-permute-start(f32[1024,512]{1,0:T(8,128)} %fusion.23), channel_id=1, source_target_pairs={{0,4},{4,0},{8,12},{12,8},{16,20},{20,16},{24,28},{28,24},{1,5},{5... | collective-permute-start | bytes 6291464 | tf_op jit(solution)/shard_map/ppermute | solution.py:504
  1013.9 162.7 %reduce-scatter.14.cloned.1.call-start = ((), (), s32[]{:S(2)}) async-start(), calls=%async_computation.14 | async-start | bytes 2621440 | tf_op jit(solution)/shard_map/reduce_scatter | solution.py:509
  1016.2 89.6 %collective-permute-start.17 = (f32[256,2048]{1,0:T(8,128)}, f32[256,2048]{1,0:T(8,128)}, u32[]{:S(2)}, u32[]{:S(2)}) collective-permute-start(f32[256,2048]{1,0:T(8,128)} %get-tuple-element.174), channel_id=1, source_target_pairs={{0,2},{1,3},{2,0},{3,1},{4,6},{5,7},{6,4},{7,5},{8,10},{9,11},{10,... | collective-permute-start | bytes 6291464 | tf_op jit(solution)/shard_map/ppermute | solution.py:501
  1061.5 115.1 %reduce-scatter.16.cloned.1.call-start = ((), (), s32[]{:S(2)}) async-start(), calls=%async_computation.15 | async-start | bytes 2621440 | tf_op jit(solution)/shard_map/reduce_scatter | solution.py:509
  1063.0 76.2 %collective-permute-start.16 = (f32[512,2048]{1,0:T(8,128)}, f32[512,2048]{1,0:T(8,128)}, u32[]{:S(2)}, u32[]{:S(2)}) collective-permute-start(f32[512,2048]{1,0:T(8,128)} %get-tuple-element.161), channel_id=1, source_target_pairs={{0,1},{1,0},{2,3},{3,2},{4,5},{5,4},{6,7},{7,6},{8,9},{9,8},{10,11... | collective-permute-start | bytes 12582920 | tf_op jit(solution)/shard_map/ppermute | solution.py:498
  (90 other events, 1794.4 us)
Sparse Core Ops, SparseCore 0:
  112.0 101.2 all-gather.4
  215.5 105.9 all-gather.2
  435.4 43.0 reduce-scatter.27
  480.7 43.1 reduce-scatter.29
  554.7 77.5 reduce-scatter.31
  634.6 66.1 reduce-scatter.19
  747.8 43.8 reduce-scatter.21
  817.5 43.9 reduce-scatter.23
  867.7 43.8 reduce-scatter.25
  916.9 43.8 reduce-scatter.17
  1014.0 43.8 reduce-scatter.11
  1061.6 43.8 reduce-scatter.13
  1123.5 43.7 reduce-scatter.15

commit v3 on v2

--- a/solution.py
+++ b/solution.py
@@ -16,9 +16,8 @@
 BF16 = jnp.bfloat16
 
 AG_CHUNKS = 2
-SUM_CHUNKS = 2
-ACT_PIECES = (256, 256, 512)
-UP_PIECES = (512, 512, 512, 512)
+Z_FIRST = (1, 0)
+X_FIRST = (0, 1)
 
 
 def feature_map(values):
@@ -130,18 +129,48 @@
     return low + [v ^ 1 for v in low]
 
 
-def greet(dp):
+def greet(*peers):
+    barrier = pltpu.get_barrier_semaphore()
+    for peer in peers:
+        pl.semaphore_signal(barrier, inc=1, device_id=peer, device_id_type=pl.DeviceIdType.MESH)
+    pl.semaphore_wait(barrier, len(peers))
+
+
+def dp_peers(dp):
     me = lax.axis_index("dp")
-    barrier = pltpu.get_barrier_semaphore()
-    bits = dp.bit_length() - 1
-    for b in range(bits):
-        pl.semaphore_signal(
-            barrier,
-            inc=1,
-            device_id={"dp": me ^ (1 << b)},
-            device_id_type=pl.DeviceIdType.MESH,
-        )
-    pl.semaphore_wait(barrier, bits)
+    return [{"dp": me ^ (1 << b)} for b in range(dp.bit_length() - 1)]
+
+
+def tensor_peer(mask):
+    return {"tensor": lax.axis_index("tensor") ^ mask}
+
+
+def halving(dp, order):
+    masks = [1 << b for b in order]
+    masks += [1 << b for b in range(len(order), dp.bit_length() - 1)]
+    seq = [0]
+    for m in reversed(masks):
+        seq = [m ^ v for v in seq] + seq
+    return masks, seq
+
+
+def block_of(ref, dp, order, k):
+    rows = ref.shape[1] // dp
+    if rows % DH:
+        return ref[:, k * rows : (k + 1) * rows]
+    at = (lax.axis_index("dp") ^ halving(dp, order)[1][k]) * rows
+    return ref[:, pl.ds(pl.multiple_of(at, rows), rows)]
+
+
+def remote(src, dst, send_sem, recv_sem, peer):
+    return pltpu.make_async_remote_copy(
+        src_ref=src,
+        dst_ref=dst,
+        send_sem=send_sem,
+        recv_sem=recv_sem,
+        device_id=peer,
+        device_id_type=pl.DeviceIdType.MESH,
+    )
 
 
 def spread(dp, blocks_ref, send_sem, recv_sem, compute):
@@ -191,12 +220,53 @@
         c.wait_send()
 
 
+W_CHUNKS = 4
+
+
 def attention_kernel(
-    dp, heads, segs, scale, w_ref, g_ref, q_ref, k_ref, v_ref,
-    a16_ref, a32_ref, local_ref, mem_ref, zin_ref, blocks_ref, send_sem, recv_sem,
+    dp, heads, segs, scale, w_ref, g_ref, h_ref, wq_ref, wk_ref, wv_ref, wo_ref,
+    q_ref, k_ref, v_ref, a16_ref, pair_ref, local_ref, mem_ref, zin_ref, all_ref,
+    wf_ref, asend_ref, w_send, w_recv, a_send, a_recv, blocks_ref, send_sem, recv_sem,
 ):
     pairs = segs * heads
-    greet(dp)
+    flat = heads * DH
+    half = segs * SEG // 2
+    core, far = tensor_peer(1), tensor_peer(2)
+    greet(*dp_peers(dp), core, far)
+
+    size = flat // W_CHUNKS
+    w_copies = {}
+
+    def w_send_chunk(j, c, to, peer):
+        rows = pl.ds(c * size, size)
+        k = (to - 1) * W_CHUNKS + c
+        w_copies[to, c] = remote(
+            wf_ref.at[j, rows, :], wf_ref.at[to, rows, :], w_send.at[k], w_recv.at[k], peer
+        )
+        w_copies[to, c].start()
+
+    def w_done(to, c):
+        rows = slice(c * size, (c + 1) * size)
+        w_copies[to, c].wait_recv()
+        all_ref[to * flat + c * size : to * flat + (c + 1) * size, :] = wf_ref[to, rows, :].astype(
+            BF16
+        )
+
+    for c in range(W_CHUNKS):
+        rows = slice(c * size, (c + 1) * size)
+        wf_ref[0, rows, :] = wo_ref[rows, :].astype(F32)
+        w_send_chunk(0, c, 2, far)
+        w_send_chunk(0, c, 1, core)
+    all_ref[:flat, :] = wo_ref[...]
+
+    def project(matrix_ref, out_ref):
+        @pl.loop(0, segs * SEG // 256)
+        def _(i):
+            rows = pl.ds(pl.multiple_of(i * 256, 256), 256)
+            out_ref[rows, :] = dot(h_ref[rows, :], matrix_ref[...]).astype(BF16)
+
+    project(wk_ref, k_ref)
+    project(wv_ref, v_ref)
 
     @pl.loop(0, pairs)
     def _(p):
@@ -206,6 +276,8 @@
         blocks_ref[0, pl.ds(pairs * DH + p, 1), :] = jnp.sum(sk, axis=0, keepdims=True)
 
     def compute():
+        project(wq_ref, q_ref)
+
         @pl.loop(0, pairs)
         def _(p):
             at = head_part(heads, p)
@@ -224,17 +296,50 @@
         sq = feature_map(q_ref[at].astype(F32))
         den = jnp.sum(sq * zin, axis=-1, keepdims=True) + 1.0
         retrieved = dot(sq.astype(BF16), mem.astype(BF16)) / den
-        mixed = (g * retrieved + (1.0 - g) * local_ref[at]).astype(BF16)
-        a16_ref[at] = mixed
-        a32_ref[at] = mixed.astype(F32)
+        a16_ref[at] = (g * retrieved + (1.0 - g) * local_ref[at]).astype(BF16)
+
+    asend_ref[...] = a16_ref[half:, :].astype(F32)
+    a_copy = remote(asend_ref, pair_ref.at[:, pl.ds(flat, flat)], a_send, a_recv, core)
+    a_copy.start()
+    pair_ref[:, :flat] = a16_ref[:half, :].astype(F32)
+    for c in range(W_CHUNKS):
+        w_done(1, c)
+    a_copy.wait_recv()
+    for c in range(W_CHUNKS):
+        w_copies[2, c].wait_recv()
+        w_send_chunk(2, c, 3, core)
+        rows = slice(c * size, (c + 1) * size)
+        all_ref[2 * flat + c * size : 2 * flat + (c + 1) * size, :] = wf_ref[2, rows, :].astype(BF16)
+    for c in range(W_CHUNKS):
+        w_done(3, c)
+    for copy in w_copies.values():
+        copy.wait_send()
+    a_copy.wait_send()
 
 
 def attention_back_kernel(
     dp, heads, segs, scale, w_ref, g_ref, q_ref, k_ref, v_ref, da_ref, local_ref, mem_ref, zin_ref,
-    dq_ref, dk_ref, dv_ref, gate_ref, dqm_ref, dkl_ref, dvl_ref, blocks_ref, send_sem, recv_sem,
+    dr_ref, a16_ref, d_pre_ref, u_pre_ref, out_part_ref,
+    dq_ref, dk_ref, dv_ref, gate_ref, o_pre_ref, d_rode_ref, u_rode_ref, out_far_ref,
+    dqm_ref, dkl_ref, dvl_ref, os_ref, ride_send, ride_recv, blocks_ref, send_sem, recv_sem,
 ):
     pairs = segs * heads
-    greet(dp)
+    me = lax.axis_index("dp")
+    far = tensor_peer(2)
+    greet(*dp_peers(dp), far)
+    quarter = d_rode_ref.shape[0]
+    first = pl.ds(0, quarter)
+    riders = [
+        remote(src, dst, ride_send.at[i], ride_recv.at[i], peer)
+        for i, (src, dst, peer) in enumerate(
+            (
+                (d_pre_ref.at[first, :], d_rode_ref, {"dp": me ^ 1}),
+                (u_pre_ref.at[first, :], u_rode_ref, {"dp": me ^ 2}),
+                (out_part_ref, out_far_ref, far),
+                (os_ref, o_pre_ref, {"dp": me ^ 2}),
+            )
+        )
+    ]
 
     @pl.loop(0, pairs)
     def _(p):
@@ -257,7 +362,18 @@
         dsq = dot_nt(dnum16, mem16) + dden * zin
         dqm_ref[at] = dsq * feature_slope(qf)
 
+    rows = dr_ref.shape[1] // dp
+    half_blocks = dp // 2
+
     def compute():
+        for r in riders[:3]:
+            r.start()
+        for j in range(half_blocks):
+            os_ref[j * rows : (j + 1) * rows, :] = dot_t(
+                block_of(dr_ref, dp, Z_FIRST, j), a16_ref[...]
+            )
+        riders[3].start()
+
         @pl.loop(0, pairs)
         def _(p):
             at = head_part(heads, p)
@@ -283,83 +399,154 @@
         dk_ref[at] = (dkl_ref[at] + dsk * feature_slope(kf)).astype(BF16)
         dv_ref[at] = (dvl_ref[at] + dot(feature_map(kf).astype(BF16), dd16)).astype(BF16)
 
-
-def greet_core():
-    me = lax.axis_index("tensor")
-    barrier = pltpu.get_barrier_semaphore()
-    pl.semaphore_signal(
-        barrier, inc=1, device_id={"tensor": me ^ 1}, device_id_type=pl.DeviceIdType.MESH
-    )
-    pl.semaphore_wait(barrier, 1)
-    return me ^ 1
-
-
-def core_copy(peer, src, dst, send_sem, recv_sem):
-    return pltpu.make_async_remote_copy(
-        src_ref=src,
-        dst_ref=dst,
-        send_sem=send_sem,
-        recv_sem=recv_sem,
-        device_id={"tensor": peer},
-        device_id_type=pl.DeviceIdType.MESH,
-    )
-
-
-def core_sum_kernel(transposed, tiles, l_ref, w_ref, out_ref, send_ref, recv_ref, send_sem, recv_sem):
-    peer = greet_core()
-    half = out_ref.shape[0]
-    size = out_ref.shape[1] // tiles
-    copies = []
-
-    def term(rows, c):
-        cols = slice(c * size, (c + 1) * size)
-        if transposed:
-            return dot_nt(l_ref[rows, :], w_ref[cols, :])
-        return dot(l_ref[rows, :], w_ref[:, cols])
-
-    for c in range(tiles):
-        send_ref[c] = term(slice(half, 2 * half), c)
-        copies.append(
-            core_copy(peer, send_ref.at[c], recv_ref.at[c], send_sem.at[c], recv_sem.at[c])
+    riders[3].wait()
+    for j in range(half_blocks):
+        o_pre_ref[j * rows : (j + 1) * rows, :] += dot_t(
+            block_of(dr_ref, dp, Z_FIRST, half_blocks + j), a16_ref[...]
         )
-        copies[-1].start()
-    for c in range(tiles):
-        part = term(slice(0, half), c)
-        copies[c].wait_recv()
-        out_ref[:, c * size : (c + 1) * size] = part + recv_ref[c]
-    for c in copies:
+    for r in riders[:3]:
+        r.wait()
+
+
+def tail_kernel(
+    dp, order, o_order, ht_ref, dq_ref, dk_ref, dv_ref, wq_ref, wk_ref, wv_ref, o_pre_ref, d3_ref, u3_ref,
+    gq_ref, gk_ref, gv_ref, go_ref, part_ref, far_ref, d3_got_ref, u3_got_ref,
+    cs_ref, cr_ref, c_send, c_recv, y_send, y_recv, ride_send, ride_recv, e_send, e_recv, *bufs,
+):
+    me = lax.axis_index("dp")
+    core, far = tensor_peer(1), tensor_peer(2)
+    greet(*dp_peers(dp), core, far)
+    masks, _ = halving(dp, order)
+    o_masks, _ = halving(dp, o_order)
+    steps = len(masks)
+    rows = ht_ref.shape[0] // dp
+    half, width = part_ref.shape
+    lhs = (dq_ref, dk_ref, dv_ref, None)
+    outs = (gq_ref, gk_ref, gv_ref, go_ref)
+    copies = {}
+
+    def buffers(i, step):
+        k = 2 * (i * steps + step)
+        return bufs[k], bufs[k + 1]
+
+    def term(i, step):
+        lo = rows * sum(dp >> (n + 1) for n in range(step))
+        count = rows * (dp >> (step + 1)) if step < steps else rows
+        start = 0
+        if i < 3:
+            value = dot(ht_ref[lo : lo + count, :], lhs[i][...])
+        else:
+            base = rows * (dp // 2)
+            value = o_pre_ref[lo - base : lo - base + count, :]
+            start = 1
+        for n in range(start, step):
+            at = lo - rows * sum(dp >> (m + 1) for m in range(n + 1))
+            value = value + buffers(i, n)[1][at : at + count, :]
+        return value
+
+    def advance(i, step):
+        if step > (1 if i == 3 else 0):
+            copies[i, step - 1].wait_recv()
+        if step == steps:
+            outs[i][...] = term(i, step)
+            return
+        send, recv = buffers(i, step)
+        send[...] = term(i, step)
+        mask = (o_masks if i == 3 else masks)[step]
+        k = i * steps + step
+        copies[i, step] = remote(send, recv, e_send.at[k], e_recv.at[k], {"dp": me ^ mask})
+        copies[i, step].start()
+
+    third = masks[2] if steps > 2 else masks[-1]
+    riders = [
+        remote(src, dst, ride_send.at[i], ride_recv.at[i], {"dp": me ^ third})
+        for i, (src, dst) in enumerate(((d3_ref, d3_got_ref), (u3_ref, u3_got_ref)))
+    ]
+    advance(0, 0)
+    for r in riders:
+        r.start()
+    advance(3, 1)
+    advance(1, 0)
+    advance(2, 0)
+
+    part_cols = width // 4
+    weights = (wq_ref, wk_ref, wv_ref)
+
+    def back(row, c):
+        cols = slice(c * part_cols, (c + 1) * part_cols)
+        return sum(
+            dot_nt(v[row * half : (row + 1) * half, :], w[cols, :])
+            for v, w in zip(lhs[:3], weights)
+        )
+
+    core_copies, far_copies = [], []
+    for c in range(4):
+        cs_ref[c] = back(1, c)
+        core_copies.append(remote(cs_ref.at[c], cr_ref.at[c], c_send.at[c], c_recv.at[c], core))
+        core_copies[-1].start()
+    for c in range(4):
+        cols = pl.ds(c * part_cols, part_cols)
+        value = back(0, c)
+        core_copies[c].wait_recv()
+        part_ref[:, c * part_cols : (c + 1) * part_cols] = value + cr_ref[c]
+        far_copies.append(
+            remote(part_ref.at[:, cols], far_ref.at[:, cols], y_send.at[c], y_recv.at[c], far)
+        )
+        far_copies[-1].start()
+
+    for step in range(1, steps + 1):
+        if step > 1:
+            advance(3, step)
+        for i in range(3):
+            advance(i, step)
+    for c in core_copies:
         c.wait_send()
-
-
-def core_sum(ident, lhs, w, transposed):
-    tokens = lhs.shape[0]
+    for c in copies.values():
+        c.wait_send()
+    for c in far_copies + riders:
+        c.wait()
+
+
+def tail(ident, dp, ht, grads, weights, o_pre, d3, u3):
+    width, tokens = ht.shape
+    flat = grads[0].shape[1]
     half = tokens // 2
-    n = w.shape[0] if transposed else w.shape[1]
-    tiles = 4
-    out = jax.ShapeDtypeStruct((half, n), F32)
+    rows = width // dp
+    steps = dp.bit_length() - 1
     full = pl.BlockSpec(memory_space=pltpu.VMEM)
+    anywhere = pl.BlockSpec(memory_space=pl.ANY)
+    f32 = lambda *shape: jax.ShapeDtypeStruct(shape, F32)
+    dma = pltpu.SemaphoreType.DMA
+    bufs = []
+    for i in range(4):
+        for step in range(steps):
+            count = rows * (dp >> (step + 1)) if i < 3 or step else 8
+            bufs += [pltpu.VMEM((count, flat), F32)] * 2
     return pl.pallas_call(
-        functools.partial(core_sum_kernel, transposed, tiles),
-        out_shape=out,
-        in_specs=[full, full],
-        out_specs=full,
+        functools.partial(tail_kernel, dp, X_FIRST, Z_FIRST),
+        out_shape=[f32(rows, flat)] * 4
+        + [f32(half, width), f32(half, width), f32(*d3.shape), f32(*u3.shape)],
+        in_specs=[full] * 8 + [anywhere] * 2,
+        out_specs=[full] * 5 + [anywhere] * 3,
         scratch_shapes=[
-            pltpu.VMEM((tiles, half, n // tiles), F32),
-            pltpu.VMEM((tiles, half, n // tiles), F32),
-            pltpu.SemaphoreType.DMA((tiles,)),
-            pltpu.SemaphoreType.DMA((tiles,)),
-        ],
+            pltpu.VMEM((4, half, width // 4), F32),
+            pltpu.VMEM((4, half, width // 4), F32),
+            dma((4,)), dma((4,)), dma((4,)), dma((4,)), dma((2,)), dma((2,)),
+            dma((4 * steps,)), dma((4 * steps,)),
+        ]
+        + bufs,
         compiler_params=pltpu.CompilerParams(
-            collective_id=ident, has_side_effects=True, vmem_limit_bytes=52 << 20
+            collective_id=ident, has_side_effects=True, vmem_limit_bytes=63 << 20
         ),
         cost_estimate=pl.CostEstimate(
-            flops=2 * tokens * w.size, transcendentals=0, bytes_accessed=nbytes(lhs, w, out)
+            flops=12 * tokens * width * flat, transcendentals=0, bytes_accessed=64 << 20
         ),
-    )(lhs, w)
+    )(ht, *grads, *weights, o_pre, d3, u3)
 
 
 def core_gather_kernel(norm, tiles, v_ref, gain_ref, out_ref, send_ref, recv_ref, send_sem, recv_sem):
-    peer = greet_core()
+    peer = tensor_peer(1)
+    greet(peer)
     half = v_ref.shape[0]
     size = half // tiles
     copies = []
@@ -373,8 +560,8 @@
         out_ref[rows, :] = v.astype(BF16)
         src = send_ref if norm else v_ref
         copies.append(
-            core_copy(
-                peer, src.at[rows, :], recv_ref.at[rows, :], send_sem.at[c], recv_sem.at[c]
+            remote(
+                src.at[rows, :], recv_ref.at[rows, :], send_sem.at[c], recv_sem.at[c], peer
             )
         )
         copies[-1].start()
@@ -412,53 +599,205 @@
     )(v, gain[None, :] if norm else jnp.zeros((8, DH), F32))
 
 
-def feed_kernel(wire, off_ref, h_ref, w_ref, u_ref, *refs):
-    act_ref, dpre_ref, extra_ref = refs[-3:]
-    pre = dot(h_ref[...], w_ref[...])
-    c = 0.7978845608028654
-    sq = pre * pre
-    th = jnp.tanh(c * pre * (1.0 + 0.044715 * sq))
-    half = 0.5 * (1.0 + th)
-    act = (pre * half).astype(BF16)
-    act_ref[...] = act
-    extra_ref[...] = act.astype(F32) if wire else act
-    slope = half + 0.5 * pre * (1.0 - th * th) * (c * (1.0 + 0.134145 * sq))
-    dpre_ref[...] = (u_ref[...] * slope).astype(BF16)
-
-
-def feed(h2, w_up, up_grad, offset, count, tile, wire, held):
+TILE = 256
+SLOTS = 4
+
+
+def feed_kernel(
+    dp, turn, h_ref, ogt_ref, ht_ref, wup_hbm, wdn_hbm, ug_hbm,
+    act_ref, dpre_ref, part_ref, part2_ref, far_ref, d_ref, u_ref, d_pre_ref, u_pre_ref,
+    w_ref, ug_ref, ds_ref, us_ref, cs_ref, cr_ref,
+    w_sem, ug_sem, d_send, d_recv, u_send, u_recv, c_send, c_recv, y_send, y_recv, free_sem,
+):
+    tokens, units = act_ref.shape
+    half = tokens // 2
+    width = h_ref.shape[1]
+    cut = width // 2
+    rows = width // dp
+    me = lax.axis_index("dp")
+    core, far = tensor_peer(1), tensor_peer(2)
+    x_peer, z_peer = {"dp": me ^ 1}, {"dp": me ^ 2}
+    greet(core, far, x_peer, z_peer)
+    count = units // TILE
+
+    load_w = pltpu.make_async_copy(wup_hbm, w_ref, w_sem)
+    load_w.start()
+
+    def tile_cols(t):
+        return pl.ds(pl.multiple_of(t * TILE, TILE), TILE)
+
+    def load_ug(t, k):
+        return pltpu.make_async_copy(ug_hbm.at[:, tile_cols(t)], ug_ref.at[k], ug_sem.at[k])
+
+    load_ug(0, 0).start()
+    load_ug(1, 1).start()
+    for j in range(dp // 2 if turn else 0):
+        ht_ref[j * rows : (j + 1) * rows, :] = block_of(h_ref, dp, X_FIRST, j).T
+    load_w.wait()
+
+    def wire(t, k):
+        cols = tile_cols(t)
+        d = remote(ds_ref.at[k], d_ref.at[:, cols], d_send.at[t], d_recv.at[t], z_peer)
+        u = remote(us_ref.at[k], u_ref.at[:, cols], u_send.at[t], u_recv.at[t], x_peer)
+        return d, u
+
+    def terms(t, k):
+        cols = tile_cols(t)
+        d, u = wire(t, k)
+        ds_ref[k] = dot(ogt_ref[:cut, :], act_ref[:, cols])
+        d.start()
+        us_ref[k] = dot(ht_ref[:cut, :], dpre_ref[:, cols])
+        u.start()
+
+    @pl.loop(0, count)
+    def _(t):
+        k = t % 2
+        cols = tile_cols(t)
+        load_ug(t, k).wait()
+        pre = dot(h_ref[...], w_ref[:, cols])
+        c = 0.7978845608028654
+        sq = pre * pre
+        th = jnp.tanh(c * pre * (1.0 + 0.044715 * sq))
+        mid = 0.5 * (1.0 + th)
+        act_ref[:, cols] = (pre * mid).astype(BF16)
+        slope = mid + 0.5 * pre * (1.0 - th * th) * (c * (1.0 + 0.134145 * sq))
+        dpre_ref[:, cols] = (ug_ref[k] * slope).astype(BF16)
+
+        @pl.when(t + 2 < count)
+        def _():
+            load_ug(t + 2, k).start()
+
+        @pl.when(t < SLOTS)
+        def _():
+            terms(t, t)
+
+    part_cols = width // 4
+
+    def core_wire(c):
+        return remote(cs_ref.at[c], cr_ref.at[c], c_send.at[c], c_recv.at[c], core)
+
+    def far_wire(c):
+        cols = pl.ds(c * part_cols, part_cols)
+        return remote(part_ref.at[:, cols], far_ref.at[:, cols], y_send.at[c], y_recv.at[c], far)
+
+    def summed(lhs_ref, transposed, out_ref, travels):
+        def term(row, c):
+            cols = slice(c * part_cols, (c + 1) * part_cols)
+            lhs = lhs_ref[row * half : (row + 1) * half, :]
+            if transposed:
+                return dot_nt(lhs, w_ref[cols, :])
+            return dot(lhs, w_ref[:, cols])
+
+        for c in range(4):
+            cs_ref[c] = term(1, c)
+            core_wire(c).start()
+        for c in range(4):
+            part = term(0, c)
+            core_wire(c).wait()
+            out_ref[:, c * part_cols : (c + 1) * part_cols] = part + cr_ref[c]
+            if travels:
+                far_wire(c).start()
+
+    summed(dpre_ref, True, part_ref, True)
+    load_down = pltpu.make_async_copy(wdn_hbm, w_ref, w_sem)
+    load_down.start()
+    pl.semaphore_signal(free_sem, inc=1, device_id=core, device_id_type=pl.DeviceIdType.MESH)
+    for j in range(dp // 2, dp if turn else 0):
+        ht_ref[j * rows : (j + 1) * rows, :] = block_of(h_ref, dp, X_FIRST, j).T
+
+    @pl.loop(SLOTS, count)
+    def _(t):
+        d, u = wire(t - SLOTS, t - SLOTS)
+        d.wait_send()
+        u.wait_send()
+        terms(t, t - SLOTS)
+
+    load_down.wait()
+    pl.semaphore_wait(free_sem, 1)
+    summed(act_ref, False, part2_ref, False)
+
+    def load_got(src_ref, t, k):
+        return pltpu.make_async_copy(src_ref.at[:, tile_cols(t)], ug_ref.at[k], ug_sem.at[k])
+
+    def store_pre(dst_ref, t, k):
+        return pltpu.make_async_copy(ug_ref.at[k], dst_ref.at[:, tile_cols(t)], ug_sem.at[k])
+
+    @pl.loop(0, count)
+    def _(t):
+        d, u = wire(t, 0)
+
+        @pl.when(t > 0)
+        def _():
+            store_pre(d_pre_ref, t - 1, 0).wait()
+            store_pre(u_pre_ref, t - 1, 1).wait()
+
+        d.wait_recv()
+        load_got(d_ref, t, 0).start()
+        u.wait_recv()
+        load_got(u_ref, t, 1).start()
+        load_got(d_ref, t, 0).wait()
+        ug_ref[0] += dot(ogt_ref[cut:, :], act_ref[:, tile_cols(t)])
+        store_pre(d_pre_ref, t, 0).start()
+        load_got(u_ref, t, 1).wait()
+        ug_ref[1] += dot(ht_ref[cut:, :], dpre_ref[:, tile_cols(t)])
+        store_pre(u_pre_ref, t, 1).start()
+
+    store_pre(d_pre_ref, count - 1, 0).wait()
+    store_pre(u_pre_ref, count - 1, 1).wait()
+
+    @pl.loop(count - SLOTS, count)
+    def _(t):
+        d, u = wire(t, t - (count - SLOTS))
+        d.wait_send()
+        u.wait_send()
+
+    for c in range(4):
+        far_wire(c).wait()
+
+
+def feed(ident, dp, h2, og_t, h_t, w_up, w_down, up_grad):
     tokens, width = h2.shape
     units = w_up.shape[1]
-    full = jax.ShapeDtypeStruct((tokens, units), BF16)
-    extra = jax.ShapeDtypeStruct((tokens, count), F32 if wire else BF16)
-    at = lambda j, off: (0, off[0] + j)
-    held = list(held)
+    half = tokens // 2
+    cut = width // 2
+    count = units // TILE
+    full = pl.BlockSpec(memory_space=pltpu.VMEM)
+    anywhere = pl.BlockSpec(memory_space=pl.ANY)
+    f32 = lambda *shape: jax.ShapeDtypeStruct(shape, F32)
+    b16 = jax.ShapeDtypeStruct((tokens, units), BF16)
+    dma = pltpu.SemaphoreType.DMA
+    turn = h_t is None
+    kernel = functools.partial(feed_kernel, dp, turn)
+    if turn:
+
+        def kernel(h_ref, ogt_ref, *refs):
+            feed_kernel(dp, turn, h_ref, ogt_ref, refs[-1], *refs[:-1])
+
     return pl.pallas_call(
-        functools.partial(feed_kernel, wire),
-        out_shape=[full, full, extra],
-        grid_spec=pltpu.PrefetchScalarGridSpec(
-            num_scalar_prefetch=1,
-            grid=(count // tile,),
-            in_specs=[
-                pl.BlockSpec((tokens, width), lambda j, off: (0, 0)),
-                pl.BlockSpec((width, tile), at),
-                pl.BlockSpec((tokens, tile), at),
-            ]
-            + [pl.BlockSpec(memory_space=pl.ANY)] * len(held),
-            out_specs=[
-                pl.BlockSpec((tokens, tile), at),
-                pl.BlockSpec((tokens, tile), at),
-                pl.BlockSpec((tokens, tile), lambda j, off: (0, j)),
-            ],
+        kernel,
+        out_shape=[b16, b16, f32(half, width), f32(half, width), f32(half, width)]
+        + [f32(cut, units)] * 4,
+        in_specs=[full] * (2 if turn else 3) + [anywhere] * 3,
+        out_specs=[full] * 4 + [anywhere] * 5,
+        scratch_shapes=[
+            pltpu.VMEM((width, units), BF16),
+            pltpu.VMEM((2, tokens, TILE), F32),
+            pltpu.VMEM((SLOTS, cut, TILE), F32),
+            pltpu.VMEM((SLOTS, cut, TILE), F32),
+            pltpu.VMEM((4, half, width // 4), F32),
+            pltpu.VMEM((4, half, width // 4), F32),
+            dma, dma((2,)), dma((count,)), dma((count,)), dma((count,)), dma((count,)),
+            dma((4,)), dma((4,)), dma((4,)), dma((4,)), pltpu.SemaphoreType.REGULAR,
+        ]
+        + ([pltpu.VMEM((width, tokens), BF16)] if turn else []),
+        compiler_params=pltpu.CompilerParams(
+            collective_id=ident, has_side_effects=True, vmem_limit_bytes=62 << 20
         ),
-        input_output_aliases={4: 0, 5: 1} if held else {},
-        compiler_params=pltpu.CompilerParams(vmem_limit_bytes=48 << 20),
         cost_estimate=pl.CostEstimate(
-            flops=2 * tokens * width * count,
-            transcendentals=tokens * count,
-            bytes_accessed=2 * width * (tokens + count) + 12 * tokens * count,
+            flops=10 * tokens * width * units, transcendentals=tokens * units,
+            bytes_accessed=64 << 20,
         ),
-    )((offset // tile)[None], h2, w_up, up_grad, *held)
+    )(h2, og_t, *([] if turn else [h_t]), w_up, w_down, up_grad)
 
 
 def body(
@@ -503,30 +842,15 @@
     def swap_dp(v, mask):
         return lax.ppermute(v, "dp", [(i, i ^ mask) for i in range(dp)])
 
-    z_groups = [[z * 2 + x for z in range(dp // 2)] for x in range(2)]
-
-    def scatter_z(v):
-        return lax.psum_scatter(v, "dp", scatter_dimension=0, axis_index_groups=z_groups, tiled=True)
-
-    xi = di % 2
-
-    def columns(v):
-        ids = [2 * z + 1 - xi for z in range(dp // 2)] + [2 * z + xi for z in range(dp // 2)]
-        return block_columns(v, ids, rows)
+    def columns(v, order):
+        _, seq = halving(dp, order)
+        return block_columns(v, [di ^ k for k in seq], rows)
+
+    def blocks_for(v, order):
+        return columns(v, order) if rows % DH else v
 
     cut = width // 2
-
-    class Reduce:
-        def __init__(self, lhs, rhs):
-            self.lhs, self.rhs = lhs, rhs
-            self.term = dot_t(lhs[:, :cut], rhs)
-            self.got = swap_dp(self.term, 1)
-
-        def scatter(self, *earlier):
-            got = after(self.got, *earlier)
-            self.part = dot_t(self.lhs[:, cut:], self.rhs) + got
-            self.out = scatter_z(self.part)
-            return self.part
+    quarter = cut // 2
 
     def pick(v, index, axis):
         size = v.shape[axis] // 2
@@ -541,8 +865,6 @@
 
     def inv_rms(v):
         return lax.rsqrt(jnp.mean(v * v, axis=-1, keepdims=True) + EPS)
-
-    w_out_all = lax.all_gather(w_out.astype(F32), "tensor", axis=0, tiled=True)
 
     x_own = pick(inputs, core, 0).astype(F32)
     x_oth = pick(inputs, 1 - core, 0).astype(F32)
@@ -556,13 +878,6 @@
         0,
     )
 
-    def project(matrix):
-        return dot(h1, matrix).astype(BF16)
-
-    qh = project(w_query)
-    kh = project(w_key)
-    vh = project(w_value)
-
     sub = segs // 2
     every = jnp.arange(seg_parent.shape[0], dtype=jnp.int32)
     sub_ids = jnp.arange(sub, dtype=jnp.int32)
@@ -592,12 +907,12 @@
     zin_shape = jax.ShapeDtypeStruct((pairs, DH), F32)
     full = pl.BlockSpec(memory_space=pltpu.VMEM)
 
-    def attention_call(kernel, ident, outs, scratch, args, n_smem, flops):
+    def attention_call(kernel, ident, outs, out_specs, scratch, args, in_specs, flops):
         return pl.pallas_call(
             functools.partial(kernel, dp, heads, segs, scale),
             out_shape=outs,
-            in_specs=[SMEM] * n_smem + [full] * (len(args) - n_smem),
-            out_specs=[full] * len(outs),
+            in_specs=in_specs,
+            out_specs=out_specs,
             scratch_shapes=scratch
             + [
                 pltpu.VMEM((dp, block_rows, DH), F32),
@@ -605,7 +920,7 @@
                 pltpu.SemaphoreType.DMA((dp,)),
             ],
             compiler_params=pltpu.CompilerParams(
-                collective_id=ident, has_side_effects=True, vmem_limit_bytes=56 << 20
+                collective_id=ident, has_side_effects=True, vmem_limit_bytes=63 << 20
             ),
             cost_estimate=pl.CostEstimate(
                 flops=flops, transcendentals=0, bytes_accessed=64 << 20
@@ -613,103 +928,51 @@
         )(*args)
 
     head_flops = 2 * segs * heads * SEG * SEG * DH
-    a16, a32, local, memory, zin = attention_call(
+    dma = pltpu.SemaphoreType.DMA
+    qh, kh, vh, a16, a_pair, local, memory, zin, w_out_all = attention_call(
         attention_kernel,
         0,
-        [act_b16, act_f32, act_f32, mem_shape, zin_shape],
-        [],
-        (up_weight, gate_row, qh, kh, vh),
-        2,
-        3 * head_flops,
+        [
+            act_b16, act_b16, act_b16, act_b16,
+            jax.ShapeDtypeStruct((half, 2 * flat), F32),
+            act_f32, mem_shape, zin_shape,
+            jax.ShapeDtypeStruct((4 * flat, width), BF16),
+        ],
+        [full] * 9,
+        [
+            pltpu.VMEM((4, flat, width), F32),
+            pltpu.VMEM((half, flat), F32),
+            dma((3 * W_CHUNKS,)), dma((3 * W_CHUNKS,)), dma, dma,
+        ],
+        (up_weight, gate_row, h1, w_query, w_key, w_value, w_out),
+        [SMEM, SMEM] + [full] * 5,
+        3 * head_flops + 6 * tokens * width * flat,
     )
-    og_pair = lax.all_gather(
-        after(og_own, a32).astype(F32), "dp", axis=0, tiled=True,
-        axis_index_groups=[[2 * i, 2 * i + 1] for i in range(dp // 2)],
-    )
-
-    up_grad = dot_nt(og, after(w_down, a32))
+    up_grad = dot_nt(og, after(w_down, a_pair))
 
     step = half // AG_CHUNKS
-    a_core = [
-        swap_core(a32[half + c * step : half + (c + 1) * step]) for c in range(AG_CHUNKS)
+    a_near = [a_pair[c * step : (c + 1) * step] for c in range(AG_CHUNKS)]
+    a_far = [swap_y(v) for v in a_near]
+    near = [
+        x_own[c * step : (c + 1) * step] + dot(v.astype(BF16), w_out_all[: 2 * flat])
+        for c, v in enumerate(a_near)
     ]
-    a_pair = [
-        jnp.concatenate([a32[c * step : (c + 1) * step], a_core[c]], 1) for c in range(AG_CHUNKS)
-    ]
-    a_far = [swap_y(v) for v in a_pair]
-    ti = lax.axis_index("tensor")
-
-    def w_rows(j):
-        return low_after_wire(lax.dynamic_slice_in_dim(w_out_all, (ti ^ j) * flat, flat, 0))
-
-    w_out_core = w_rows(1)
-    w_out_far = jnp.concatenate([w_rows(2), w_rows(3)], 0)
-    near = [
-        x_own[c * step : (c + 1) * step]
-        + dot(a16[c * step : (c + 1) * step], w_out)
-        + dot(low_after_wire(a_core[c]), w_out_core)
-        for c in range(AG_CHUNKS)
-    ]
-    h1_a = columns(after(h1, up_grad))
+    og_t = columns(after(og, up_grad), Z_FIRST).T
+    h1_a = columns(after(h1, og_t), X_FIRST).T
     resids = [
-        n + dot(low_after_wire(after(f, w_out_far, h1_a)), w_out_far)
+        n + dot(low_after_wire(after(f, og_t, h1_a)), w_out_all[2 * flat :])
         for n, f in zip(near, a_far)
     ]
     resid = jnp.concatenate(resids, 0)
     inv_mlp = inv_rms(resid)
     h2 = core_gather(1, resid, gain_mlp)
 
-    part = units // 2
-    held = ()
-    act_b = []
-    at = (1 - xi) * part
-    for n in ACT_PIECES:
-        act, dpre, wire = feed(h2, w_up, up_grad, at, n, 256, True, held)
-        held = (act, dpre)
-        act_b.append(swap_dp(wire, 1))
-        at = at + n
-    act, dpre, act_keep = feed(h2, w_up, up_grad, xi * part, part, 256, False, held)
-
-    def tensor_sum_start(ident, lhs, w, transposed):
-        total = core_sum(ident, lhs, w, transposed)
-        size = half // SUM_CHUNKS
-        parts = [total[c * size : (c + 1) * size] for c in range(SUM_CHUNKS)]
-        return [(p, swap_y(p)) for p in parts]
-
-    def tensor_sum_end(parts, *earlier):
-        return jnp.concatenate([p + after(r, *earlier) for p, r in parts], 0)
-
-    dh2_parts = tensor_sum_start(2, dpre, w_up, True)
-    sent = [p for p, _ in dh2_parts]
-
-    h2_a = columns(after(h2, *sent))
-    up = []
-    starts = [0]
-    for n in UP_PIECES:
-        starts.append(starts[-1] + n)
-
-    def up_piece(p, *earlier):
-        up.append(Reduce(h2_a, after(dpre, *earlier)[:, starts[p] : starts[p + 1]]))
-        return up[-1].term
-
-    og_b_own = lax.dynamic_slice_in_dim(og_pair, (1 - xi) * half, half, 0)
-    og_b = core_gather(3, after(og_b_own, h2_a))
-    down = []
-
-    def down_piece(p, *earlier):
-        lo = sum(ACT_PIECES[:p])
-        piece = act_keep[:, lo : lo + ACT_PIECES[p]]
-        got = low_after_wire(after(act_b[p], *earlier))
-        total = dot_t(og, piece) + dot_t(og_b, got)
-        down.append(scatter_z(total))
-        return total
-
-    e = up_piece(0, *sent)
-    e = down_piece(0, e)
-    e = up_piece(1, e)
-    e = down_piece(1, e)
-
-    dh2 = tensor_sum_end(dh2_parts, e)
+    h_t = columns(h2, X_FIRST).T if rows % DH else None
+    act, dpre, dh2_part, out_part, dh2_far, _, _, d_pre, u_pre = feed(
+        2, dp, h2, og_t, h_t, w_up, w_down, up_grad
+    )
+
+    dh2 = dh2_part + dh2_far
     gs = dh2 * gain_mlp
     dresid = (
         og_own.astype(F32)
@@ -719,45 +982,52 @@
     gain_mlp_part = jnp.sum(dh2 * resid * inv_mlp, axis=0)
     dr = core_gather(4, dresid)
 
-    e = down_piece(2, dr)
-    da = dot_nt(after(dr, e), w_out).astype(BF16)
-    e = up[0].scatter(da)
-    e = up_piece(2, e)
-    dq16, dk16, dv16, gate_rows = attention_call(
+    da = dot_nt(dr, w_out).astype(BF16)
+    anywhere = pl.BlockSpec(memory_space=pl.ANY)
+    ride = jax.ShapeDtypeStruct((quarter, units), F32)
+    o_shape = jax.ShapeDtypeStruct((cut, flat), F32)
+    dq16, dk16, dv16, gate_rows, o_pre, d_rode, u_rode, out_far = attention_call(
         attention_back_kernel,
         5,
-        [act_b16, act_b16, act_b16, zin_shape],
-        [pltpu.VMEM((tokens, flat), F32)] * 3,
-        (down_weight, gate_row, qh, kh, vh, after(da, e), local, memory, zin),
-        2,
+        [
+            act_b16, act_b16, act_b16, zin_shape, o_shape, ride, ride,
+            jax.ShapeDtypeStruct((half, width), F32),
+        ],
+        [full] * 5 + [anywhere] * 3,
+        [pltpu.VMEM((tokens, flat), F32)] * 3
+        + [pltpu.VMEM((cut, flat), F32)]
+        + [dma((4,)), dma((4,))],
+        (
+            down_weight, gate_row, qh, kh, vh, da, local, memory, zin,
+            blocks_for(dr, Z_FIRST), a16, d_pre, u_pre, out_part,
+        ),
+        [SMEM, SMEM] + [full] * 9 + [anywhere] * 3,
         9 * head_flops,
     )
     gate_part = jnp.sum(gate_rows.reshape(segs, heads, DH), axis=(0, 2)) * gate * (1.0 - gate)
 
-    e = up[1].scatter(dq16)
-    e = up_piece(3, e)
-    out_w = Reduce(columns(after(dr, e)), a16)
-
-    out_parts = tensor_sum_start(6, after(act, out_w.term), w_down, False)
-    query = Reduce(h1_a, after(dq16, *[p for p, _ in out_parts]))
-
-    w_qkv = jnp.concatenate([after(w, up_grad) for w in (w_query, w_key, w_value)], 1)
-    d_qkv = jnp.concatenate([dq16, dk16, dv16], 1)
-    dh1_parts = tensor_sum_start(7, after(d_qkv, query.term), w_qkv, True)
-    sent = [p for p, _ in dh1_parts]
-    e = up[2].scatter(*sent)
-    key = Reduce(h1_a, after(dk16, e))
-    e = up[3].scatter(key.term)
-    value = Reduce(h1_a, after(dv16, e))
-    e = out_w.scatter(value.term)
-
-    out_own = (resid + tensor_sum_end(out_parts, e)).astype(BF16)
+    eighth = quarter // 2
+    third = [p[quarter : quarter + eighth] + r[:eighth] for p, r in ((d_pre, d_rode), (u_pre, u_rode))]
+    w_query_grad, w_key_grad, w_value_grad, w_out_rows, dh1_part, dh1_far, d3, u3 = tail(
+        7, dp, h1_a, (dq16, dk16, dv16), (w_query, w_key, w_value), o_pre, *third
+    )
+    w_out_grad = w_out_rows.T
+
+    def finish(pre, rode, got, order):
+        masks, _ = halving(dp, order)
+        value = pre[quarter + eighth :] + rode[eighth:] + got
+        for m in masks[3:]:
+            n = value.shape[0] // 2
+            value = value[n:] + swap_dp(value[:n], m)
+        return value
+
+    w_down_grad = finish(d_pre, d_rode, d3, Z_FIRST).T
+    w_up_grad = finish(u_pre, u_rode, u3, X_FIRST)
+
+    out_own = (resid + out_part + out_far).astype(BF16)
     outputs = place(out_own, low_after_wire(swap_core(out_own.astype(F32))), core, 0)
 
-    e = query.scatter(out_own)
-    e = key.scatter(e)
-
-    dh1 = tensor_sum_end(dh1_parts, e)
+    dh1 = dh1_part + dh1_far
     gs1 = dh1 * gain_attn
     dx = (
         dresid
@@ -767,15 +1037,6 @@
     gain_attn_part = jnp.sum(dh1 * x_own * inv_own, axis=0)
     dx_own = dx.astype(BF16)
     input_grad = place(dx_own, low_after_wire(swap_core(dx_own.astype(F32))), core, 0)
-
-    e = value.scatter(dx_own)
-
-    down = jnp.concatenate(down, 1)
-    down_theirs = swap_dp(pick(down, 1 - xi, 0), 1)
-    w_down_grad = place(pick(down, xi, 0), down_theirs, xi, 1).T
-    w_up_grad = jnp.concatenate([v.out for v in up], 1)
-    w_out_grad = out_w.out.T
-    w_query_grad, w_key_grad, w_value_grad = query.out, key.out, value.out
 
     gains = jnp.concatenate([gain_attn_part, gain_mlp_part])
     small = jnp.concatenate([gains + swap_core(gains), jnp.pad(gate_part, (0, DH - heads))])

time: 1190 us -> 1010 us (0.85)
  waiting for transfers between devices: 531 us -> 8.31 us
  Pallas kernels: 334 us -> 843 us
  matrix products: 115 us -> 27 us
  starting transfers between devices: 41.9 us -> 8.1 us
  other arithmetic: 98.4 us -> 83.4 us
  local copies, waits for them, and re-layouts: 47.4 us -> 33.1 us
  between operations: 15.1 us -> 1.46 us
    pallas_call x7 -> x2, Pallas kernels: 80.4 us -> 501 us  [the longest x1 296 us: tail(): pl.pallas_call(functools.partial(tail_kernel, dp, X_FIRST, Z_FIRST), out_...]
    ppermute x15 -> x3, waiting for transfers between devices: 189 us -> 2.3 us  [swap_dp(): return lax.ppermute(v, 'dp', [(i, i ^ mask) for i in range(dp)])]
    ppermute x8 -> x2, waiting for transfers between devices: 185 us -> 0.01 us  [swap_y(): return lax.ppermute(v, 'tensor', [(i, i ^ 2) for i in range(tn)])]
    all_gather x2 -> x0, waiting for transfers between devices: 156 us -> none  [the longest x1 103 us: body(): w_out_all = lax.all_gather(w_out.astype(F32), 'tensor', axis=0, tiled=True)]
    pallas_call x2, Pallas kernels: 202 us -> 307 us  [attention_call(): pl.pallas_call(functools.partial(kernel, dp, heads, segs, scale), out_sha...]
    dot_general x22 -> x0, matrix products: 77 us -> none  [dot_t(): lax.dot_general(a, b, (((0,), (0,)), ((), ())), preferred_element_type=F32)]
    ppermute x15 -> x3, starting transfers between devices: 19.8 us -> 5.5 us  [swap_dp(): return lax.ppermute(v, 'dp', [(i, i ^ mask) for i in range(dp)])]
    slice x4 -> x1, local copies, waits for them, and re-layouts: 16.5 us -> 3.32 us  [body(): a_near = [a_pair[c * step:(c + 1) * step] for c in range(AG_CHUNKS)]]
  transfers between devices with their start and end apart: 41 -> 8, of which waited for: 18 -> 2; matrix products, arithmetic and copies ran while one was open for 17% -> 8% of each run, Pallas kernels for 21% -> 31%
where the time goes in v3:
time: 1010 us; the launch traced here: 1000 us
  Pallas kernels  843 us (83%)
  other arithmetic  83.4 us (8%)
  local copies, waits for them, and re-layouts  33.1 us (3%)
  matrix products  27 us (3%)
    pallas_call x2, Pallas kernels, attention_call(): pl.pallas_call(functools.partial(kernel, dp, heads, segs, scale), out_sha...  307 us
    pallas_call x1, Pallas kernels, tail(): pl.pallas_call(functools.partial(tail_kernel, dp, X_FIRST, Z_FIRST), out_...  296 us
    pallas_call x1, Pallas kernels, feed(): pl.pallas_call(kernel, out_shape=[b16, b16, f32(half, width), f32(half, w...  205 us
  transfers between devices with their start and end apart: 8, of which 2 were waited for; matrix products, arithmetic and copies ran while one was open for 8% of the time, Pallas kernels for 31%

profile of v3, /device:TPU:0, one launch (start us, length us, event | category | flops | bytes accessed | tf_op | source)
XLA Modules:
  0.0 1004.0 jit_solution(11264147412661385009)
XLA Ops:
  15.0 109.3 %shard_map.203 = (bf16[1024,512]{1,0:T(8,128)(2,1)}, bf16[1024,512]{1,0:T(8,128)(2,1)}, bf16[1024,512]{1,0:T(8,128)(2,1)}, bf16[1024,512]{1,0:T(8,128)(2,1)}, f3...) custom-call(f32[2,16]{1,0:T(2,128)} %fusion.47.w_ref, ...), custom_call_target="tpu_custom_call" | custom-call | flops 8053063680 | bytes 67108864 | tf_op jit(solution)/shard_map/pallas_call | solution.py:911
  137.9 11.1 %fusion.42.refs_2_ = f32[1024,2048]{1,0:T(8,128)} fusion(bf16[2048,2048]{1,0:T(8,128)(2,1)S(1)} %bitcast.31, bf16[512,2048]{1,0:T(8,128)(2,1)S(1)} %get-tuple-element.119, bf16[512,2048]{1,0:T(8,128)(2,1)S(1)} %get-tuple-element.120), kind=kOutput, calls=%fused_computation.107 | convolution fusion | flops 8598323200 | bytes 20971520 | tf_op jit(solution)/shard_map/dot_general | solution.py:53
  150.8 7.4 shard_map.204
  158.2 6.4 copy.27
  164.7 7.4 shard_map.205
  172.0 6.7 copy.28
  178.8 4.3 fusion.16
  183.1 3.6 fusion.13
  194.2 9.7 shard_map.206.h_ref
  206.0 205.2 %shard_map.207 = (bf16[1024,2048]{1,0:T(8,128)(2,1)}, bf16[1024,2048]{1,0:T(8,128)(2,1)}, f32[512,2048]{1,0:T(8,128)}, f32[512,2048]{1,0:T(8,128)}, f32[512,2048...) custom-call(bf16[1024,2048]{1,0:T(8,128)(2,1)} %copy-done.1, ...), custom_call_target="tpu_custom_call" | custom-call | flops 42949672960 | bytes 67108864 | tf_op jit(solution)/shard_map/pallas_call | solution.py:776
  411.2 6.1 multiply_reduce_fusion
  418.9 6.2 multiply_subtract_fusion.v_ref
  425.1 9.7 shard_map.208.dr_ref
  438.2 198.1 %shard_map.209 = (bf16[1024,512]{1,0:T(8,128)(2,1)}, bf16[1024,512]{1,0:T(8,128)(2,1)}, bf16[1024,512]{1,0:T(8,128)(2,1)}, f32[8,128]{1,0:T(8,128)}, f32[1024,51...) custom-call(f32[2,16]{1,0:T(2,128)} %fusion.48.w_ref, f32[1,4]{1,0:T(1,128)} %fusion.52.g_ref, ...), custom_call_target="tpu_custom_call" | custom-call | flops 4831838208 | bytes 67108864 | tf_op jit(solution)/shard_map/pallas_call | solution.py:911
  636.3 9.5 fusion.44
  652.3 295.9 %shard_map.210 = (f32[256,512]{1,0:T(8,128)}, f32[256,512]{1,0:T(8,128)}, f32[256,512]{1,0:T(8,128)}, f32[256,512]{1,0:T(8,128)}, f32[512,2048]{1,0:T(8,128)}, /...) custom-call(bf16[2048,1024]{1,0:T(8,128)(2,1)} %bitcast.26, ...), custom_call_target="tpu_custom_call" | custom-call | flops 12884901888 | bytes 67108864 | tf_op jit(solution)/shard_map/pallas_call | solution.py:525
  948.2 5.7 multiply_reduce_fusion.1
  954.7 5.9 fusion.43
  961.5 6.0 collective-permute-done.4
  971.4 3.8 collective-permute-start.6
  975.2 5.0 add_add_fusion
  980.3 3.5 add_bitcast_fusion
  991.5 3.6 maximum_select_fusion
  997.8 3.5 maximum_select_fusion.1
  (148 shorter events, 69.0 us)
Async XLA Ops:
  0.6 9.8 copy-start.26
  127.6 59.2 %collective-permute-start.1 = (f32[256,1024]{1,0:T(8,128)}, f32[256,1024]{1,0:T(8,128)S(1)}, u32[]{:S(2)}, u32[]{:S(2)}) collective-permute-start(f32[256,1024]{1,0:T(8,128)} %get-tuple-element.122), channel_id=1, source_target_pairs={{0,2},{1,3},{2,0},{3,1},{4,6},{5,7},{6,4},{7,5},{8,10},{9,11},{10,... | collective-permute-start | bytes 3145736 | tf_op jit(solution)/shard_map/ppermute | solution.py:840
  128.1 58.7 %collective-permute-start = (f32[256,1024]{1,0:T(8,128)}, f32[256,1024]{1,0:T(8,128)}, u32[]{:S(2)}, u32[]{:S(2)}) collective-permute-start(f32[256,1024]{1,0:T(8,128)} %get-tuple-element.121), channel_id=1, source_target_pairs={{0,2},{1,3},{2,0},{3,1},{4,6},{5,7},{6,4},{7,5},{8,10},{9,11},{10,... | collective-permute-start | bytes 3145736 | tf_op jit(solution)/shard_map/ppermute | solution.py:840
  172.0 6.7 copy-start.31
  172.0 6.7 copy-start.15
  178.8 8.0 slice-start
  411.2 6.2 copy-start.4
  411.2 6.2 copy-start.6
  411.2 6.5 copy-start.12
  411.2 7.7 copy-start.13
  425.1 9.7 copy-start.32
  636.3 9.5 copy-start.18
  645.7 343.1 %collective-permute-start.2 = (f32[512,2048]{1,0:T(8,128)}, f32[512,2048]{1,0:T(8,128)}, u32[]{:S(2)}, u32[]{:S(2)}) collective-permute-start(f32[512,2048]{1,0:T(8,128)} %get-tuple-element.111), channel_id=1, source_target_pairs={{0,1},{1,0},{2,3},{3,2},{4,5},{5,4},{6,7},{7,6},{8,9},{9,8},{10,11... | collective-permute-start | bytes 12582920 | tf_op jit(solution)/shard_map/ppermute | solution.py:837
  652.3 295.9 %copy-start.27 = (f32[2048]{0:T(1024)S(1)}, f32[2048]{0:T(1024)}, u32[]{:S(2)}) copy-start(f32[2048]{0:T(1024)} %param.13) | copy-start | bytes 24580
  652.3 295.9 %copy-start.29 = (f32[512]{0:T(512)S(1)}, f32[512]{0:T(512)}, u32[]{:S(2)}) copy-start(f32[512]{0:T(512)} %copy-done.28) | copy-start | bytes 6148
  948.2 5.7 copy-start.9
  948.2 6.5 copy-start.10
  954.7 5.9 copy-start.30
  954.7 6.7 copy-start.33
  960.7 34.5 %collective-permute-start.3 = (f32[512,2048]{1,0:T(8,128)}, f32[512,2048]{1,0:T(8,128)}, u32[]{:S(2)}, u32[]{:S(2)}) collective-permute-start(f32[512,2048]{1,0:T(8,128)} %get-tuple-element.109), channel_id=1, source_target_pairs={{0,1},{1,0},{2,3},{3,2},{4,5},{5,4},{6,7},{7,6},{8,9},{9,8},{10,11... | collective-permute-start | bytes 12582920 | tf_op jit(solution)/shard_map/ppermute | solution.py:837
  960.9 6.6 collective-permute-start.4
  967.5 3.9 collective-permute-start.5
  971.4 8.8 collective-permute-start.6
  980.2 7.5 collective-permute-start.7
  (22 other events, 83.0 us)

commit v4 on v3

--- a/solution.py
+++ b/solution.py
@@ -152,6 +152,10 @@
     for m in reversed(masks):
         seq = [m ^ v for v in seq] + seq
     return masks, seq
+
+
+def near_units(dp, units):
+    return units // 4 if dp == 8 else units
 
 
 def block_of(ref, dp, order, k):
@@ -327,19 +331,33 @@
     me = lax.axis_index("dp")
     far = tensor_peer(2)
     greet(*dp_peers(dp), far)
-    quarter = d_rode_ref.shape[0]
-    first = pl.ds(0, quarter)
+    legs = [
+        (d_pre_ref, d_rode_ref, {"dp": me ^ 1}),
+        (out_part_ref, out_far_ref, far),
+        (os_ref, o_pre_ref, {"dp": me ^ 2}),
+    ]
+    quarter, units = d_rode_ref.shape
+    eighth = quarter // 2
+    legs[0] = (d_pre_ref.at[pl.ds(0, quarter), :], d_rode_ref, {"dp": me ^ 1})
+    near = near_units(dp, units)
+    cols = pl.ds(0, near)
+    legs.append((u_pre_ref.at[pl.ds(0, quarter), cols], u_rode_ref.at[:, cols], {"dp": me ^ 2}))
+    if near < units:
+        cols = pl.ds(near, units - near)
+        for k in range(2):
+            legs.append(
+                (
+                    u_pre_ref.at[pl.ds(2 * k * eighth, eighth), cols],
+                    u_rode_ref.at[pl.ds(k * eighth, eighth), cols],
+                    {"dp": me ^ 4},
+                )
+            )
     riders = [
         remote(src, dst, ride_send.at[i], ride_recv.at[i], peer)
-        for i, (src, dst, peer) in enumerate(
-            (
-                (d_pre_ref.at[first, :], d_rode_ref, {"dp": me ^ 1}),
-                (u_pre_ref.at[first, :], u_rode_ref, {"dp": me ^ 2}),
-                (out_part_ref, out_far_ref, far),
-                (os_ref, o_pre_ref, {"dp": me ^ 2}),
-            )
-        )
+        for i, (src, dst, peer) in enumerate(legs)
     ]
+    o_rider = riders[2]
+    plain = riders[:2] + riders[3:]
 
     @pl.loop(0, pairs)
     def _(p):
@@ -366,13 +384,13 @@
     half_blocks = dp // 2
 
     def compute():
-        for r in riders[:3]:
+        for r in plain:
             r.start()
         for j in range(half_blocks):
             os_ref[j * rows : (j + 1) * rows, :] = dot_t(
                 block_of(dr_ref, dp, Z_FIRST, j), a16_ref[...]
             )
-        riders[3].start()
+        o_rider.start()
 
         @pl.loop(0, pairs)
         def _(p):
@@ -399,28 +417,38 @@
         dk_ref[at] = (dkl_ref[at] + dsk * feature_slope(kf)).astype(BF16)
         dv_ref[at] = (dvl_ref[at] + dot(feature_map(kf).astype(BF16), dd16)).astype(BF16)
 
-    riders[3].wait()
+    o_rider.wait()
     for j in range(half_blocks):
         o_pre_ref[j * rows : (j + 1) * rows, :] += dot_t(
             block_of(dr_ref, dp, Z_FIRST, half_blocks + j), a16_ref[...]
         )
-    for r in riders[:3]:
+    for r in plain:
         r.wait()
 
 
+ROWS = 128
+
+
 def tail_kernel(
-    dp, order, o_order, ht_ref, dq_ref, dk_ref, dv_ref, wq_ref, wk_ref, wv_ref, o_pre_ref, d3_ref, u3_ref,
-    gq_ref, gk_ref, gv_ref, go_ref, part_ref, far_ref, d3_got_ref, u3_got_ref,
-    cs_ref, cr_ref, c_send, c_recv, y_send, y_recv, ride_send, ride_recv, e_send, e_recv, *bufs,
+    dp, turn, order, o_order,
+    h_ref, dq_ref, dk_ref, dv_ref, wq_ref, wk_ref, wv_ref, o_pre_ref, gain_ref, vec_ref,
+    d3_ref, u3_ref, resid_hbm, out_part_hbm, out_far_hbm, dresid_hbm, x_hbm,
+    gq_ref, gk_ref, gv_ref, go_ref, vec_out_ref, far_ref, d3_got_ref, u3_got_ref, out_hbm, dx_hbm,
+    part_ref, cs_ref, cr_ref, in_ref, own_ref, other_ref, vec_got_ref,
+    c_send, c_recv, y_send, y_recv, ride_send, ride_recv, e_send, e_recv, v_send, v_recv,
+    in_sem, st_sem, free_sem, *bufs,
 ):
     me = lax.axis_index("dp")
+    side = lax.axis_index("tensor") % 2
     core, far = tensor_peer(1), tensor_peer(2)
     greet(*dp_peers(dp), core, far)
     masks, _ = halving(dp, order)
     o_masks, _ = halving(dp, o_order)
     steps = len(masks)
-    rows = ht_ref.shape[0] // dp
-    half, width = part_ref.shape
+    half, width = far_ref.shape
+    rows = width // dp
+    chunks = half // ROWS
+    ht_ref = bufs[-1] if turn else h_ref
     lhs = (dq_ref, dk_ref, dv_ref, None)
     outs = (gq_ref, gk_ref, gv_ref, go_ref)
     copies = {}
@@ -457,58 +485,132 @@
         copies[i, step] = remote(send, recv, e_send.at[k], e_recv.at[k], {"dp": me ^ mask})
         copies[i, step].start()
 
-    third = masks[2] if steps > 2 else masks[-1]
+    third = {"dp": me ^ masks[2]}
+    units = u3_ref.shape[1]
+    near = near_units(dp, units)
+    cols = pl.ds(0, near)
+    legs = [(d3_ref, d3_got_ref, third), (u3_ref.at[:, cols], u3_got_ref.at[:, cols], third)]
+    if near < units:
+        cols = pl.ds(near, units - near)
+        legs.append((u3_ref.at[:, cols], u3_got_ref.at[:, cols], {"dp": me ^ 2}))
     riders = [
-        remote(src, dst, ride_send.at[i], ride_recv.at[i], {"dp": me ^ third})
-        for i, (src, dst) in enumerate(((d3_ref, d3_got_ref), (u3_ref, u3_got_ref)))
+        remote(src, dst, ride_send.at[i], ride_recv.at[i], peer)
+        for i, (src, dst, peer) in enumerate(legs)
     ]
-    advance(0, 0)
     for r in riders:
         r.start()
     advance(3, 1)
-    advance(1, 0)
-    advance(2, 0)
-
-    part_cols = width // 4
-    weights = (wq_ref, wk_ref, wv_ref)
-
-    def back(row, c):
-        cols = slice(c * part_cols, (c + 1) * part_cols)
+    for j in range(dp // 2 if turn else 0):
+        ht_ref[j * rows : (j + 1) * rows, :] = block_of(h_ref, dp, order, j).T
+    for i in range(3):
+        advance(i, 0)
+
+    def part_rows(c):
+        return pl.ds(c * ROWS, ROWS)
+
+    def core_wire(c):
+        return remote(cs_ref.at[c], cr_ref.at[c], c_send.at[c], c_recv.at[c], core)
+
+    def core_free():
+        pl.semaphore_signal(free_sem, inc=1, device_id=core, device_id_type=pl.DeviceIdType.MESH)
+
+    def far_wire(c):
+        return remote(part_ref.at[c], far_ref.at[part_rows(c), :], y_send.at[c], y_recv.at[c], far)
+
+    def back(lo):
         return sum(
-            dot_nt(v[row * half : (row + 1) * half, :], w[cols, :])
-            for v, w in zip(lhs[:3], weights)
+            dot_nt(v[lo : lo + ROWS, :], w[...])
+            for v, w in zip(lhs[:3], (wq_ref, wk_ref, wv_ref))
         )
 
-    core_copies, far_copies = [], []
-    for c in range(4):
-        cs_ref[c] = back(1, c)
-        core_copies.append(remote(cs_ref.at[c], cr_ref.at[c], c_send.at[c], c_recv.at[c], core))
-        core_copies[-1].start()
-    for c in range(4):
-        cols = pl.ds(c * part_cols, part_cols)
-        value = back(0, c)
-        core_copies[c].wait_recv()
-        part_ref[:, c * part_cols : (c + 1) * part_cols] = value + cr_ref[c]
-        far_copies.append(
-            remote(part_ref.at[:, cols], far_ref.at[:, cols], y_send.at[c], y_recv.at[c], far)
-        )
-        far_copies[-1].start()
-
-    for step in range(1, steps + 1):
-        if step > 1:
-            advance(3, step)
-        for i in range(3):
+    for c in range(chunks):
+        cs_ref[c] = back(half + c * ROWS)
+        core_wire(c).start()
+    for c in range(chunks):
+        value = back(c * ROWS)
+        core_wire(c).wait()
+        part_ref[c] = value + cr_ref[c]
+        far_wire(c).start()
+    core_free()
+
+    def both_cores(sources, compute, dst_hbm):
+        pl.semaphore_wait(free_sem, 1)
+        for c in range(chunks):
+            loads = [
+                pltpu.make_async_copy(src.at[part_rows(c), :], in_ref.at[k], in_sem.at[k])
+                for k, src in enumerate(sources)
+            ]
+            for load in loads:
+                load.start()
+            for load in loads:
+                load.wait()
+            value = compute(c).astype(BF16)
+            own_ref[...] = value
+            cs_ref[c] = value.astype(F32)
+            core_wire(c).start()
+            at = pl.ds(pl.multiple_of(side * half + c * ROWS, ROWS), ROWS)
+            store = pltpu.make_async_copy(own_ref, dst_hbm.at[at, :], st_sem.at[0])
+            store.start()
+            store.wait()
+        for c in range(chunks):
+            core_wire(c).wait()
+            other_ref[...] = cr_ref[c].astype(BF16)
+            at = pl.ds(pl.multiple_of((1 - side) * half + c * ROWS, ROWS), ROWS)
+            store = pltpu.make_async_copy(other_ref, dst_hbm.at[at, :], st_sem.at[1])
+            store.start()
+            store.wait()
+
+    def output_rows(c):
+        return in_ref[0] + in_ref[1] + in_ref[2]
+
+    def input_rows(c):
+        x, grad = in_ref[2], part_ref[c] + in_ref[0]
+        inv = lax.rsqrt(jnp.mean(x * x, axis=-1, keepdims=True) + EPS)
+        gs = grad * gain_ref[...]
+        inner = jnp.mean(gs * x, axis=-1, keepdims=True)
+        vec_out_ref[0:1, :] += jnp.sum(grad * x * inv, axis=0, keepdims=True)
+        return in_ref[1] + inv * gs - x * inv * inv * inv * inner
+
+    for j in range(dp // 2, dp if turn else 0):
+        ht_ref[j * rows : (j + 1) * rows, :] = block_of(h_ref, dp, order, j).T
+    if steps == 3:
+        advance(3, 2)
+    both_cores((resid_hbm, out_part_hbm, out_far_hbm), output_rows, out_hbm)
+    core_free()
+    if steps == 3:
+        for i, step in ((0, 1), (1, 1), (0, 2), (1, 2), (2, 1), (3, 3)):
             advance(i, step)
-    for c in core_copies:
-        c.wait_send()
+        rest = ((0, 3), (2, 2), (1, 3), (2, 3))
+    else:
+        for step in range(1, steps):
+            for i in (3, 0, 1, 2) if step > 1 else (0, 1, 2):
+                advance(i, step)
+        rest = [(i, steps) for i in (3, 0, 1, 2)]
+
+    for c in range(chunks):
+        far_wire(c).wait()
+    vec_out_ref[...] = vec_ref[...]
+    both_cores((far_ref, dresid_hbm, x_hbm), input_rows, dx_hbm)
+    for i, step in rest:
+        advance(i, step)
+
+    for k, peer in enumerate([core] + dp_peers(dp)):
+        hop = remote(vec_out_ref, vec_got_ref.at[k], v_send.at[k], v_recv.at[k], peer)
+        hop.start()
+        hop.wait()
+        got = vec_got_ref[k]
+        if k == 0:
+            got = jnp.where(lax.broadcasted_iota(jnp.int32, got.shape, 0) < 2, got, 0.0)
+        vec_out_ref[...] += got
     for c in copies.values():
         c.wait_send()
-    for c in far_copies + riders:
-        c.wait()
-
-
-def tail(ident, dp, ht, grads, weights, o_pre, d3, u3):
-    width, tokens = ht.shape
+    for r in riders:
+        r.wait()
+
+
+def tail(ident, dp, h1, h1_t, grads, weights, o_pre, gain, vec, d3, u3, streams):
+    tokens, width = h1.shape
+    turn = h1_t is None
     flat = grads[0].shape[1]
     half = tokens // 2
     rows = width // dp
@@ -522,26 +624,38 @@
         for step in range(steps):
             count = rows * (dp >> (step + 1)) if i < 3 or step else 8
             bufs += [pltpu.VMEM((count, flat), F32)] * 2
+    chunks = half // ROWS
+    b16 = jax.ShapeDtypeStruct((tokens, width), BF16)
     return pl.pallas_call(
-        functools.partial(tail_kernel, dp, X_FIRST, Z_FIRST),
+        functools.partial(tail_kernel, dp, turn, X_FIRST, Z_FIRST),
         out_shape=[f32(rows, flat)] * 4
-        + [f32(half, width), f32(half, width), f32(*d3.shape), f32(*u3.shape)],
-        in_specs=[full] * 8 + [anywhere] * 2,
-        out_specs=[full] * 5 + [anywhere] * 3,
+        + [f32(*vec.shape), f32(half, width), f32(*d3.shape), f32(*u3.shape), b16, b16],
+        in_specs=[full] * 10 + [anywhere] * 7,
+        out_specs=[full] * 5 + [anywhere] * 5,
         scratch_shapes=[
-            pltpu.VMEM((4, half, width // 4), F32),
-            pltpu.VMEM((4, half, width // 4), F32),
-            dma((4,)), dma((4,)), dma((4,)), dma((4,)), dma((2,)), dma((2,)),
-            dma((4 * steps,)), dma((4 * steps,)),
+            pltpu.VMEM((chunks, ROWS, width), F32),
+            pltpu.VMEM((chunks, ROWS, width), F32),
+            pltpu.VMEM((chunks, ROWS, width), F32),
+            pltpu.VMEM((3, ROWS, width), F32),
+            pltpu.VMEM((ROWS, width), BF16),
+            pltpu.VMEM((ROWS, width), BF16),
+            pltpu.VMEM((steps + 1,) + vec.shape, F32),
+            dma((chunks,)), dma((chunks,)), dma((chunks,)), dma((chunks,)),
+            dma((3,)), dma((3,)), dma((4 * steps,)), dma((4 * steps,)),
+            dma((steps + 1,)), dma((steps + 1,)), dma((3,)), dma((2,)),
+            pltpu.SemaphoreType.REGULAR,
         ]
-        + bufs,
+        + bufs
+        + ([pltpu.VMEM((width, tokens), BF16)] if turn else []),
         compiler_params=pltpu.CompilerParams(
             collective_id=ident, has_side_effects=True, vmem_limit_bytes=63 << 20
         ),
         cost_estimate=pl.CostEstimate(
-            flops=12 * tokens * width * flat, transcendentals=0, bytes_accessed=64 << 20
+            flops=12 * tokens * width * flat, transcendentals=0, bytes_accessed=96 << 20
         ),
-    )(ht, *grads, *weights, o_pre, d3, u3)
+    )(
+        h1 if turn else h1_t, *grads, *weights, o_pre, gain[None, :], vec, d3, u3, *streams
+    )
 
 
 def core_gather_kernel(norm, tiles, v_ref, gain_ref, out_ref, send_ref, recv_ref, send_sem, recv_sem):
@@ -958,9 +1072,8 @@
         for c, v in enumerate(a_near)
     ]
     og_t = columns(after(og, up_grad), Z_FIRST).T
-    h1_a = columns(after(h1, og_t), X_FIRST).T
     resids = [
-        n + dot(low_after_wire(after(f, og_t, h1_a)), w_out_all[2 * flat :])
+        n + dot(low_after_wire(after(f, og_t, *near)), w_out_all[2 * flat :])
         for n, f in zip(near, a_far)
     ]
     resid = jnp.concatenate(resids, 0)
@@ -996,7 +1109,7 @@
         [full] * 5 + [anywhere] * 3,
         [pltpu.VMEM((tokens, flat), F32)] * 3
         + [pltpu.VMEM((cut, flat), F32)]
-        + [dma((4,)), dma((4,))],
+        + [dma((6,)), dma((6,))],
         (
             down_weight, gate_row, qh, kh, vh, da, local, memory, zin,
             blocks_for(dr, Z_FIRST), a16, d_pre, u_pre, out_part,
@@ -1007,9 +1120,19 @@
     gate_part = jnp.sum(gate_rows.reshape(segs, heads, DH), axis=(0, 2)) * gate * (1.0 - gate)
 
     eighth = quarter // 2
-    third = [p[quarter : quarter + eighth] + r[:eighth] for p, r in ((d_pre, d_rode), (u_pre, u_rode))]
-    w_query_grad, w_key_grad, w_value_grad, w_out_rows, dh1_part, dh1_far, d3, u3 = tail(
-        7, dp, h1_a, (dq16, dk16, dv16), (w_query, w_key, w_value), o_pre, *third
+    d3 = d_pre[quarter : quarter + eighth] + d_rode[:eighth]
+    close = near_units(dp, units)
+    u3 = u_rode[:eighth] + jnp.where(
+        jnp.arange(units)[None, :] < close, u_pre[quarter : quarter + eighth], u_pre[eighth:quarter]
+    )
+    h1_t = columns(h1, X_FIRST).T if rows % DH else None
+    lane = jnp.pad(gate_part, (0, width - heads))
+    vec = jnp.zeros((8, width), F32).at[1].set(gain_mlp_part).at[2].set(lane)
+    (
+        w_query_grad, w_key_grad, w_value_grad, w_out_rows, vec, _, d3, u3, outputs, input_grad
+    ) = tail(
+        7, dp, h1, h1_t, (dq16, dk16, dv16), (w_query, w_key, w_value), o_pre, gain_attn, vec,
+        d3, u3, (resid, out_part, out_far, dresid, x_own),
     )
     w_out_grad = w_out_rows.T
 
@@ -1024,29 +1147,9 @@
     w_down_grad = finish(d_pre, d_rode, d3, Z_FIRST).T
     w_up_grad = finish(u_pre, u_rode, u3, X_FIRST)
 
-    out_own = (resid + out_part + out_far).astype(BF16)
-    outputs = place(out_own, low_after_wire(swap_core(out_own.astype(F32))), core, 0)
-
-    dh1 = dh1_part + dh1_far
-    gs1 = dh1 * gain_attn
-    dx = (
-        dresid
-        + inv_own * gs1
-        - x_own * inv_own * inv_own * inv_own * jnp.mean(gs1 * x_own, axis=-1, keepdims=True)
-    )
-    gain_attn_part = jnp.sum(dh1 * x_own * inv_own, axis=0)
-    dx_own = dx.astype(BF16)
-    input_grad = place(dx_own, low_after_wire(swap_core(dx_own.astype(F32))), core, 0)
-
-    gains = jnp.concatenate([gain_attn_part, gain_mlp_part])
-    small = jnp.concatenate([gains + swap_core(gains), jnp.pad(gate_part, (0, DH - heads))])
-    bit = 1
-    while bit < dp:
-        small = small + swap_dp(small, bit)
-        bit *= 2
-    gain_attn_grad = lax.dynamic_slice_in_dim(small, di * rows, rows, 0)
-    gain_mlp_grad = lax.dynamic_slice_in_dim(small, width + di * rows, rows, 0)
-    gate_grad = small[2 * width : 2 * width + heads]
+    gain_attn_grad = lax.dynamic_slice_in_dim(vec[0], di * rows, rows, 0)
+    gain_mlp_grad = lax.dynamic_slice_in_dim(vec[1], di * rows, rows, 0)
+    gate_grad = vec[2, :heads]
 
     return (
         outputs,

time: 1010 us -> 943 us (0.934)
  other arithmetic: 83.4 us -> 51.7 us
  Pallas kernels: 843 us -> 813 us
    pallas_call x1, Pallas kernels: 296 us -> 274 us  [tail(): pl.pallas_call(functools.partial(tail_kernel, dp, turn, X_FIRST, Z_FIRST)...]
    convert_element_type x4 -> x0, other arithmetic: 20.7 us -> none  [the longest x1 9.48 us: body(): out_own.astype(F32)]
  transfers between devices with their start and end apart: 8 -> 2, of which waited for: 2 -> 1; matrix products, arithmetic and copies ran while one was open for 8% -> 3% of each run, Pallas kernels for 31% -> 1%
where the time goes in v4:
time: 943 us; the launch traced here: 933 us
  Pallas kernels  813 us (86%)
  other arithmetic  51.7 us (5%)
  local copies, waits for them, and re-layouts  34.6 us (4%)
  matrix products  27.1 us (3%)
    pallas_call x2, Pallas kernels, attention_call(): pl.pallas_call(functools.partial(kernel, dp, heads, segs, scale), out_sha...  307 us
    pallas_call x1, Pallas kernels, tail(): pl.pallas_call(functools.partial(tail_kernel, dp, turn, X_FIRST, Z_FIRST)...  274 us
    pallas_call x1, Pallas kernels, feed(): pl.pallas_call(kernel, out_shape=[b16, b16, f32(half, width), f32(half, w...  205 us
    unnamed x67, local copies, waits for them, and re-layouts  19.7 us
    pallas_call x2, Pallas kernels, core_gather(): pl.pallas_call(functools.partial(core_gather_kernel, norm, tiles), out_sh...  19.4 us
  transfers between devices with their start and end apart: 2, of which 1 were waited for; matrix products, arithmetic and copies ran while one was open for 3% of the time, Pallas kernels for 1%

profile of v4, /device:TPU:0, one launch (start us, length us, event | category | flops | bytes accessed | tf_op | source)
XLA Modules:
  0.0 933.1 jit_solution(1131096156267986390)
XLA Ops:
  7.1 3.3 multiply_reduce_fusion.3
  11.6 2.6 pad_maximum_fusion.h_ref
  14.9 109.2 %shard_map.203 = (bf16[1024,512]{1,0:T(8,128)(2,1)}, bf16[1024,512]{1,0:T(8,128)(2,1)}, bf16[1024,512]{1,0:T(8,128)(2,1)}, bf16[1024,512]{1,0:T(8,128)(2,1)}, f3...) custom-call(f32[2,16]{1,0:T(2,128)} %fusion.43.w_ref, ...), custom_call_target="tpu_custom_call" | custom-call | flops 8053063680 | bytes 67108864 | tf_op jit(solution)/shard_map/pallas_call | solution.py:1025
  124.1 3.3 fusion.41
  138.4 11.2 %fusion.40.refs_2_ = f32[1024,2048]{1,0:T(8,128)} fusion(bf16[2048,2048]{1,0:T(8,128)(2,1)S(1)} %bitcast.41, bf16[512,2048]{1,0:T(8,128)(2,1)S(1)} %get-tuple-element.137, bf16[512,2048]{1,0:T(8,128)(2,1)S(1)} %get-tuple-element.138), kind=kOutput, calls=%fused_computation.96 | convolution fusion | flops 8598323200 | bytes 20971520 | tf_op jit(solution)/shard_map/dot_general | solution.py:53
  150.2 7.4 shard_map.204
  157.6 6.7 copy.26
  164.4 4.3 fusion.16
  168.7 3.6 fusion.13
  172.4 3.3 collective-permute-done
  177.0 3.3 fusion.19
  180.4 2.6 pad_maximum_fusion.2
  182.9 9.7 %shard_map.205.h_ref = bf16[1024,2048]{1,0:T(8,128)(2,1)S(1)} custom-call(f32[512,2048]{1,0:T(8,128)} %get-tuple-element.135.v_ref.resid_hbm, f32[1,2048]{1,0:T(1,128)S(1)} %bitcast.29), custom_call_target="tpu_custom_call" | custom-call | bytes 16777216 | tf_op jit(solution)/shard_map/pallas_call | solution.py:696
  194.6 205.1 %shard_map.206 = (bf16[1024,2048]{1,0:T(8,128)(2,1)}, bf16[1024,2048]{1,0:T(8,128)(2,1)}, f32[512,2048]{1,0:T(8,128)}, f32[512,2048]{1,0:T(8,128)}, f32[512,2048...) custom-call(bf16[1024,2048]{1,0:T(8,128)(2,1)} %copy-done.1, ...), custom_call_target="tpu_custom_call" | custom-call | flops 42949672960 | bytes 67108864 | tf_op jit(solution)/shard_map/pallas_call | solution.py:890
  399.8 6.1 multiply_reduce_fusion
  407.4 6.7 multiply_subtract_fusion.v_ref.dresid_hbm
  414.1 9.7 %shard_map.207.dr_ref = bf16[1024,2048]{1,0:T(8,128)(2,1)S(1)} custom-call(f32[512,2048]{1,0:T(8,128)} %multiply_subtract_fusion.v_ref.dresid_hbm, f32[8,128]{1,0:T(8,128)S(1)} %broadcast_in_dim.46.gain_ref), custom_call_target="tpu_custom_call" | custom-call | bytes 16777216 | tf_op jit(solution)/shard_map/pallas_call | solution.py:696
  423.9 3.3 convolution_convert_fusion.da_ref
  427.2 197.9 %shard_map.208 = (bf16[1024,512]{1,0:T(8,128)(2,1)}, bf16[1024,512]{1,0:T(8,128)(2,1)}, bf16[1024,512]{1,0:T(8,128)(2,1)}, f32[8,128]{1,0:T(8,128)}, f32[1024,51...) custom-call(f32[2,16]{1,0:T(2,128)} %fusion.44.w_ref, f32[1,4]{1,0:T(1,128)} %fusion.48.g_ref, ...), custom_call_target="tpu_custom_call" | custom-call | flops 4831838208 | bytes 67108864 | tf_op jit(solution)/shard_map/pallas_call | solution.py:1025
  626.1 3.9 slice_add_fusion.d3_ref
  630.3 4.9 select_add_fusion.u3_ref
  635.2 274.1 %shard_map.209 = (f32[256,512]{1,0:T(8,128)}, f32[256,512]{1,0:T(8,128)}, f32[256,512]{1,0:T(8,128)}, f32[256,512]{1,0:T(8,128)}, f32[8,2048]{1,0:T(8,128)}, /*i...) custom-call(bf16[1024,2048]{1,0:T(8,128)(2,1)} %pad_maximum_fusion.h, ...), custom_call_target="tpu_custom_call" | custom-call | flops 12884901888 | bytes 100663296 | tf_op jit(solution)/shard_map/pallas_call | solution.py:629
  914.6 5.0 add_add_fusion
  923.5 4.9 copy.35
  (111 shorter events, 39.7 us)
Async XLA Ops:
  0.6 9.7 %copy-start.22 = (f32[2048]{0:T(1024)S(1)}, f32[2048]{0:T(1024)}, u32[]{:S(2)}) copy-start(f32[2048]{0:T(1024)} %param.17) | copy-start | bytes 24580
  7.1 3.4 copy-start.7
  124.1 5.3 copy-start.8
  127.4 5.3 copy-start.14
  127.4 45.0 %collective-permute-start.1 = (f32[256,1024]{1,0:T(8,128)}, f32[256,1024]{1,0:T(8,128)S(1)}, u32[]{:S(2)}, u32[]{:S(2)}) collective-permute-start(f32[256,1024]{1,0:T(8,128)} %get-tuple-element.140), channel_id=1, source_target_pairs={{0,2},{1,3},{2,0},{3,1},{4,6},{5,7},{6,4},{7,5},{8,10},{9,11},{10,... | collective-permute-start | bytes 3145736 | tf_op jit(solution)/shard_map/ppermute | solution.py:954
  127.9 47.8 %collective-permute-start = (f32[256,1024]{1,0:T(8,128)}, f32[256,1024]{1,0:T(8,128)}, u32[]{:S(2)}, u32[]{:S(2)}) collective-permute-start(f32[256,1024]{1,0:T(8,128)} %get-tuple-element.139), channel_id=1, source_target_pairs={{0,2},{1,3},{2,0},{3,1},{4,6},{5,7},{6,4},{7,5},{8,10},{9,11},{10,... | collective-permute-start | bytes 3145736 | tf_op jit(solution)/shard_map/ppermute | solution.py:954
  132.7 4.0 slice-start.2
  133.2 5.2 slice-start.3
  157.6 6.7 copy-start.23
  157.6 6.8 copy-start.13
  164.4 4.3 copy-start.12
  164.4 11.3 %slice-start = ((s8[8388608]{0:T(1024)(128)(4,1)}), s8[4194304]{0:T(1024)(128)(4,1)S(1)}, s32[]{:S(2)}) async-start(s8[8388608]{0:T(1024)(128)(4,1)} %bitcast.30), calls=%async_computation | async-start | bytes 8388608
  168.7 7.0 slice-start.1
  399.7 6.2 copy-start.4
  399.7 6.2 copy-start.6
  399.7 6.5 copy-start.10
  399.7 7.7 copy-start.11
  414.1 9.7 %copy-start.24 = (bf16[512,2048]{1,0:T(8,128)(2,1)S(1)}, bf16[512,2048]{1,0:T(8,128)(2,1)}, u32[]{:S(2)}) copy-start(bf16[512,2048]{1,0:T(8,128)(2,1)} %wo_ref.1) | copy-start | bytes 6291460
  427.2 198.8 %copy-start.25 = (f32[4]{0:T(128)S(1)}, f32[4]{0:T(128)}, u32[]{:S(2)}) copy-start(f32[4]{0:T(128)} %param.21) | copy-start | bytes 52
  630.3 4.9 copy-start.21
  914.6 5.0 copy-start.15
  914.6 5.0 copy-start.17
  923.5 4.9 copy-start.16
  928.4 3.6 copy-start.18
  (8 other events, 21.8 us)

commit v5 on v4

--- a/solution.py
+++ b/solution.py
@@ -177,7 +177,7 @@
     )
 
 
-def spread(dp, blocks_ref, send_sem, recv_sem, compute):
+def spread(dp, blocks_ref, send_sem, recv_sem, compute, then=None):
     me = lax.axis_index("dp")
     slot = {j: k for k, j in enumerate(spread_order(dp))}
     copies = {}
@@ -213,6 +213,8 @@
                         if j & n and j != n:
                             copies[j].wait_recv()
         send(m, 1)
+    if then is not None:
+        then()
     last = [j for j in near if j and j not in bits]
     for j in last:
         if j & bits[0] or len(bits) == 1:
@@ -358,6 +360,8 @@
     ]
     o_rider = riders[2]
     plain = riders[:2] + riders[3:]
+    for r in riders[:2] + riders[3:4]:
+        r.start()
 
     @pl.loop(0, pairs)
     def _(p):
@@ -384,13 +388,10 @@
     half_blocks = dp // 2
 
     def compute():
-        for r in plain:
-            r.start()
         for j in range(half_blocks):
             os_ref[j * rows : (j + 1) * rows, :] = dot_t(
                 block_of(dr_ref, dp, Z_FIRST, j), a16_ref[...]
             )
-        o_rider.start()
 
         @pl.loop(0, pairs)
         def _(p):
@@ -405,7 +406,12 @@
             dkl_ref[at] = dot_t(ds16, q) * scale
             dvl_ref[at] = (1.0 - g) * dot_t(probs.astype(BF16), da)
 
-    spread(dp, blocks_ref, send_sem, recv_sem, compute)
+    def then():
+        o_rider.start()
+        for r in riders[4:]:
+            r.start()
+
+    spread(dp, blocks_ref, send_sem, recv_sem, compute, then)
 
     @pl.loop(0, pairs)
     def _(p):
@@ -429,14 +435,21 @@
 ROWS = 128
 
 
+def tail_items(flat):
+    full = slice(0, flat)
+    return [
+        (0, full), (1, full), (2, slice(0, flat // 2)), (2, slice(flat // 2, flat)), (3, full)
+    ]
+
+
 def tail_kernel(
     dp, turn, order, o_order,
     h_ref, dq_ref, dk_ref, dv_ref, wq_ref, wk_ref, wv_ref, o_pre_ref, gain_ref, vec_ref,
     d3_ref, u3_ref, resid_hbm, out_part_hbm, out_far_hbm, dresid_hbm, x_hbm,
     gq_ref, gk_ref, gv_ref, go_ref, vec_out_ref, far_ref, d3_got_ref, u3_got_ref, out_hbm, dx_hbm,
-    part_ref, cs_ref, cr_ref, in_ref, own_ref, other_ref, vec_got_ref,
+    part_ref, cs_ref, cr_ref, in_ref, own_ref, other_ref, turn_ref, vec_got_ref,
     c_send, c_recv, y_send, y_recv, ride_send, ride_recv, e_send, e_recv, v_send, v_recv,
-    in_sem, st_sem, free_sem, *bufs,
+    in_sem, st_sem, turn_sem, free_sem, *bufs,
 ):
     me = lax.axis_index("dp")
     side = lax.axis_index("tensor") % 2
@@ -449,8 +462,11 @@
     rows = width // dp
     chunks = half // ROWS
     ht_ref = bufs[-1] if turn else h_ref
-    lhs = (dq_ref, dk_ref, dv_ref, None)
+    depth = in_ref.shape[0]
+    flat = dq_ref.shape[1]
+    lhs = (dq_ref, dk_ref, dv_ref)
     outs = (gq_ref, gk_ref, gv_ref, go_ref)
+    items = tail_items(flat)
     copies = {}
 
     def buffers(i, step):
@@ -461,8 +477,9 @@
         lo = rows * sum(dp >> (n + 1) for n in range(step))
         count = rows * (dp >> (step + 1)) if step < steps else rows
         start = 0
-        if i < 3:
-            value = dot(ht_ref[lo : lo + count, :], lhs[i][...])
+        which, cols = items[i]
+        if which < 3:
+            value = dot(ht_ref[lo : lo + count, :], lhs[which][:, cols])
         else:
             base = rows * (dp // 2)
             value = o_pre_ref[lo - base : lo - base + count, :]
@@ -473,14 +490,15 @@
         return value
 
     def advance(i, step):
-        if step > (1 if i == 3 else 0):
+        which, cols = items[i]
+        if step > (1 if which == 3 else 0):
             copies[i, step - 1].wait_recv()
         if step == steps:
-            outs[i][...] = term(i, step)
+            outs[which][:, cols] = term(i, step)
             return
         send, recv = buffers(i, step)
         send[...] = term(i, step)
-        mask = (o_masks if i == 3 else masks)[step]
+        mask = (o_masks if which == 3 else masks)[step]
         k = i * steps + step
         copies[i, step] = remote(send, recv, e_send.at[k], e_recv.at[k], {"dp": me ^ mask})
         copies[i, step].start()
@@ -497,12 +515,30 @@
         remote(src, dst, ride_send.at[i], ride_recv.at[i], peer)
         for i, (src, dst, peer) in enumerate(legs)
     ]
+    out_item = len(items) - 1
+    advance(out_item, 1)
     for r in riders:
         r.start()
-    advance(3, 1)
-    for j in range(dp // 2 if turn else 0):
-        ht_ref[j * rows : (j + 1) * rows, :] = block_of(h_ref, dp, order, j).T
-    for i in range(3):
+
+    def block_load(j):
+        at = (me ^ halving(dp, order)[1][j]) * rows
+        return pltpu.make_async_copy(
+            h_ref.at[:, pl.ds(pl.multiple_of(at, rows), rows)],
+            turn_ref.at[j % 2],
+            turn_sem.at[j % 2],
+        )
+
+    def turn_blocks(lo, hi):
+        for j in range(lo, hi if turn else lo):
+            block_load(j).wait()
+            ht_ref[j * rows : (j + 1) * rows, :] = turn_ref[j % 2].T
+            if j + 2 < dp:
+                block_load(j + 2).start()
+
+    for j in range(2 if turn else 0):
+        block_load(j).start()
+    turn_blocks(0, dp // 2)
+    for i in range(out_item):
         advance(i, 0)
 
     def part_rows(c):
@@ -519,73 +555,90 @@
 
     def back(lo):
         return sum(
-            dot_nt(v[lo : lo + ROWS, :], w[...])
-            for v, w in zip(lhs[:3], (wq_ref, wk_ref, wv_ref))
+            dot_nt(v[lo : lo + 2 * ROWS, :], w[...])
+            for v, w in zip(lhs, (wq_ref, wk_ref, wv_ref))
         )
 
-    for c in range(chunks):
-        cs_ref[c] = back(half + c * ROWS)
-        core_wire(c).start()
-    for c in range(chunks):
+    for c in range(0, chunks, 2):
+        value = back(half + c * ROWS)
+        for k in range(2):
+            cs_ref[c + k] = value[k * ROWS : (k + 1) * ROWS, :]
+            core_wire(c + k).start()
+    for c in range(0, chunks, 2):
         value = back(c * ROWS)
-        core_wire(c).wait()
-        part_ref[c] = value + cr_ref[c]
-        far_wire(c).start()
+        for k in range(2):
+            core_wire(c + k).wait()
+            part_ref[c + k] = value[k * ROWS : (k + 1) * ROWS, :] + cr_ref[c + k]
+            far_wire(c + k).start()
     core_free()
 
     def both_cores(sources, compute, dst_hbm):
+        def loads(c):
+            k = c % depth
+            return [
+                pltpu.make_async_copy(src.at[part_rows(c), :], in_ref.at[k, i], in_sem.at[k, i])
+                for i, src in enumerate(sources)
+            ]
+
+        def begin(c):
+            if c < chunks:
+                for load in loads(c):
+                    load.start()
+
+        def store(src_ref, which, c, k):
+            at = pl.ds(pl.multiple_of(which * half + c * ROWS, ROWS), ROWS)
+            return pltpu.make_async_copy(src_ref, dst_hbm.at[at, :], st_sem.at[k])
+
         pl.semaphore_wait(free_sem, 1)
+        for c in range(depth):
+            begin(c)
         for c in range(chunks):
-            loads = [
-                pltpu.make_async_copy(src.at[part_rows(c), :], in_ref.at[k], in_sem.at[k])
-                for k, src in enumerate(sources)
-            ]
-            for load in loads:
-                load.start()
-            for load in loads:
+            for load in loads(c):
                 load.wait()
-            value = compute(c).astype(BF16)
+            value = compute(c, *(in_ref[c % depth, i] for i in range(3))).astype(BF16)
+            if c:
+                store(own_ref, side, c - 1, 0).wait()
             own_ref[...] = value
+            store(own_ref, side, c, 0).start()
             cs_ref[c] = value.astype(F32)
             core_wire(c).start()
-            at = pl.ds(pl.multiple_of(side * half + c * ROWS, ROWS), ROWS)
-            store = pltpu.make_async_copy(own_ref, dst_hbm.at[at, :], st_sem.at[0])
-            store.start()
-            store.wait()
+            begin(c + depth)
         for c in range(chunks):
             core_wire(c).wait()
+            if c:
+                store(other_ref, 1 - side, c - 1, 1).wait()
             other_ref[...] = cr_ref[c].astype(BF16)
-            at = pl.ds(pl.multiple_of((1 - side) * half + c * ROWS, ROWS), ROWS)
-            store = pltpu.make_async_copy(other_ref, dst_hbm.at[at, :], st_sem.at[1])
-            store.start()
-            store.wait()
-
-    def output_rows(c):
-        return in_ref[0] + in_ref[1] + in_ref[2]
-
-    def input_rows(c):
-        x, grad = in_ref[2], part_ref[c] + in_ref[0]
+            store(other_ref, 1 - side, c, 1).start()
+        store(own_ref, side, chunks - 1, 0).wait()
+        store(other_ref, 1 - side, chunks - 1, 1).wait()
+
+    def output_rows(c, a, b, d):
+        return a + b + d
+
+    def input_rows(c, there, dresid, x):
+        grad = part_ref[c] + there
         inv = lax.rsqrt(jnp.mean(x * x, axis=-1, keepdims=True) + EPS)
         gs = grad * gain_ref[...]
         inner = jnp.mean(gs * x, axis=-1, keepdims=True)
         vec_out_ref[0:1, :] += jnp.sum(grad * x * inv, axis=0, keepdims=True)
-        return in_ref[1] + inv * gs - x * inv * inv * inv * inner
-
-    for j in range(dp // 2, dp if turn else 0):
-        ht_ref[j * rows : (j + 1) * rows, :] = block_of(h_ref, dp, order, j).T
+        return dresid + inv * gs - x * inv * inv * inv * inner
+
+    turn_blocks(dp // 2, dp)
     if steps == 3:
-        advance(3, 2)
+        advance(out_item, 2)
     both_cores((resid_hbm, out_part_hbm, out_far_hbm), output_rows, out_hbm)
     core_free()
     if steps == 3:
-        for i, step in ((0, 1), (1, 1), (0, 2), (1, 2), (2, 1), (3, 3)):
+        for i, step in ((0, 1), (1, 1), (0, 2), (2, 1), (1, 2)):
             advance(i, step)
-        rest = ((0, 3), (2, 2), (1, 3), (2, 3))
+        rest = ((3, 1), (2, 2), (3, 2))
     else:
         for step in range(1, steps):
-            for i in (3, 0, 1, 2) if step > 1 else (0, 1, 2):
-                advance(i, step)
-        rest = [(i, steps) for i in (3, 0, 1, 2)]
+            for i in range(len(items)):
+                if step > 1 or i < out_item:
+                    advance(i, step)
+        rest = ()
+    last = [(i, steps) for i in (out_item,) + tuple(range(out_item))]
 
     for c in range(chunks):
         far_wire(c).wait()
@@ -602,6 +655,8 @@
         if k == 0:
             got = jnp.where(lax.broadcasted_iota(jnp.int32, got.shape, 0) < 2, got, 0.0)
         vec_out_ref[...] += got
+    for i, step in last:
+        advance(i, step)
     for c in copies.values():
         c.wait_send()
     for r in riders:
@@ -620,29 +675,31 @@
     f32 = lambda *shape: jax.ShapeDtypeStruct(shape, F32)
     dma = pltpu.SemaphoreType.DMA
     bufs = []
-    for i in range(4):
+    items = tail_items(flat)
+    for which, cols in items:
         for step in range(steps):
-            count = rows * (dp >> (step + 1)) if i < 3 or step else 8
-            bufs += [pltpu.VMEM((count, flat), F32)] * 2
+            count = rows * (dp >> (step + 1)) if which < 3 or step else 8
+            bufs += [pltpu.VMEM((count, cols.stop - cols.start), F32)] * 2
     chunks = half // ROWS
     b16 = jax.ShapeDtypeStruct((tokens, width), BF16)
     return pl.pallas_call(
         functools.partial(tail_kernel, dp, turn, X_FIRST, Z_FIRST),
         out_shape=[f32(rows, flat)] * 4
         + [f32(*vec.shape), f32(half, width), f32(*d3.shape), f32(*u3.shape), b16, b16],
-        in_specs=[full] * 10 + [anywhere] * 7,
+        in_specs=[anywhere if turn else full] + [full] * 9 + [anywhere] * 7,
         out_specs=[full] * 5 + [anywhere] * 5,
         scratch_shapes=[
             pltpu.VMEM((chunks, ROWS, width), F32),
             pltpu.VMEM((chunks, ROWS, width), F32),
             pltpu.VMEM((chunks, ROWS, width), F32),
-            pltpu.VMEM((3, ROWS, width), F32),
+            pltpu.VMEM((2 if turn else 1, 3, ROWS, width), F32),
             pltpu.VMEM((ROWS, width), BF16),
             pltpu.VMEM((ROWS, width), BF16),
+            pltpu.VMEM((2, tokens, rows) if turn else (8, DH), BF16),
             pltpu.VMEM((steps + 1,) + vec.shape, F32),
             dma((chunks,)), dma((chunks,)), dma((chunks,)), dma((chunks,)),
-            dma((3,)), dma((3,)), dma((4 * steps,)), dma((4 * steps,)),
-            dma((steps + 1,)), dma((steps + 1,)), dma((3,)), dma((2,)),
+            dma((3,)), dma((3,)), dma((len(items) * steps,)), dma((len(items) * steps,)),
+            dma((steps + 1,)), dma((steps + 1,)), dma((2, 3)), dma((2,)), dma((2,)),
             pltpu.SemaphoreType.REGULAR,
         ]
         + bufs

time: 943 us -> 911 us (0.966)
  Pallas kernels: 813 us -> 781 us
    pallas_call x1, Pallas kernels: 274 us -> 248 us  [tail(): pl.pallas_call(functools.partial(tail_kernel, dp, turn, X_FIRST, Z_FIRST)...]
  transfers between devices with their start and end apart: 2 -> 2, of which waited for: 1 -> 1; matrix products, arithmetic and copies ran while one was open for 3% -> 4% of each run, Pallas kernels for 1% -> 1%
where the time goes in v5:
time: 911 us; the launch traced here: 901 us
  Pallas kernels  781 us (86%)
  other arithmetic  51.7 us (6%)
  local copies, waits for them, and re-layouts  34.6 us (4%)
  matrix products  27.1 us (3%)
    pallas_call x2, Pallas kernels, attention_call(): pl.pallas_call(functools.partial(kernel, dp, heads, segs, scale), out_sha...  301 us
    pallas_call x1, Pallas kernels, tail(): pl.pallas_call(functools.partial(tail_kernel, dp, turn, X_FIRST, Z_FIRST)...  248 us
    pallas_call x1, Pallas kernels, feed(): pl.pallas_call(kernel, out_shape=[b16, b16, f32(half, width), f32(half, w...  205 us
    unnamed x67, local copies, waits for them, and re-layouts  19.7 us
    pallas_call x2, Pallas kernels, core_gather(): pl.pallas_call(functools.partial(core_gather_kernel, norm, tiles), out_sh...  19.4 us
  transfers between devices with their start and end apart: 2, of which 1 were waited for; matrix products, arithmetic and copies ran while one was open for 4% of the time, Pallas kernels for 1%

profile of v5, /device:TPU:0, one launch (start us, length us, event | category | flops | bytes accessed | tf_op | source)
XLA Modules:
  0.0 901.4 jit_solution(5961382520389065789)
XLA Ops:
  7.1 3.3 multiply_reduce_fusion.3
  11.6 2.6 pad_maximum_fusion.h_ref
  14.9 109.2 %shard_map.203 = (bf16[1024,512]{1,0:T(8,128)(2,1)}, bf16[1024,512]{1,0:T(8,128)(2,1)}, bf16[1024,512]{1,0:T(8,128)(2,1)}, bf16[1024,512]{1,0:T(8,128)(2,1)}, f3...) custom-call(f32[2,16]{1,0:T(2,128)} %fusion.43.w_ref, ...), custom_call_target="tpu_custom_call" | custom-call | flops 8053063680 | bytes 67108864 | tf_op jit(solution)/shard_map/pallas_call | solution.py:1082
  124.1 3.3 fusion.41
  138.4 11.2 %fusion.40.refs_2_ = f32[1024,2048]{1,0:T(8,128)} fusion(bf16[2048,2048]{1,0:T(8,128)(2,1)S(1)} %bitcast.41, bf16[512,2048]{1,0:T(8,128)(2,1)S(1)} %get-tuple-element.137, bf16[512,2048]{1,0:T(8,128)(2,1)S(1)} %get-tuple-element.138), kind=kOutput, calls=%fused_computation.96 | convolution fusion | flops 8598323200 | bytes 20971520 | tf_op jit(solution)/shard_map/dot_general | solution.py:53
  150.2 7.4 shard_map.204
  157.6 6.7 copy.26
  164.4 4.3 fusion.16
  168.7 3.6 fusion.13
  172.4 3.3 collective-permute-done
  177.0 3.3 fusion.19
  180.4 2.6 pad_maximum_fusion.2
  182.9 9.7 %shard_map.205.h_ref = bf16[1024,2048]{1,0:T(8,128)(2,1)S(1)} custom-call(f32[512,2048]{1,0:T(8,128)} %get-tuple-element.135.v_ref.resid_hbm, f32[1,2048]{1,0:T(1,128)S(1)} %bitcast.29), custom_call_target="tpu_custom_call" | custom-call | bytes 16777216 | tf_op jit(solution)/shard_map/pallas_call | solution.py:753
  194.6 205.1 %shard_map.206 = (bf16[1024,2048]{1,0:T(8,128)(2,1)}, bf16[1024,2048]{1,0:T(8,128)(2,1)}, f32[512,2048]{1,0:T(8,128)}, f32[512,2048]{1,0:T(8,128)}, f32[512,2048...) custom-call(bf16[1024,2048]{1,0:T(8,128)(2,1)} %copy-done.1, ...), custom_call_target="tpu_custom_call" | custom-call | flops 42949672960 | bytes 67108864 | tf_op jit(solution)/shard_map/pallas_call | solution.py:947
  399.8 6.1 multiply_reduce_fusion
  407.4 6.7 multiply_subtract_fusion.v_ref.dresid_hbm
  414.1 9.7 %shard_map.207.dr_ref = bf16[1024,2048]{1,0:T(8,128)(2,1)S(1)} custom-call(f32[512,2048]{1,0:T(8,128)} %multiply_subtract_fusion.v_ref.dresid_hbm, f32[8,128]{1,0:T(8,128)S(1)} %broadcast_in_dim.46.gain_ref), custom_call_target="tpu_custom_call" | custom-call | bytes 16777216 | tf_op jit(solution)/shard_map/pallas_call | solution.py:753
  423.9 3.3 convolution_convert_fusion.da_ref
  427.2 192.1 %shard_map.208 = (bf16[1024,512]{1,0:T(8,128)(2,1)}, bf16[1024,512]{1,0:T(8,128)(2,1)}, bf16[1024,512]{1,0:T(8,128)(2,1)}, f32[8,128]{1,0:T(8,128)}, f32[1024,51...) custom-call(f32[2,16]{1,0:T(2,128)} %fusion.44.w_ref, f32[1,4]{1,0:T(1,128)} %fusion.48.g_ref, ...), custom_call_target="tpu_custom_call" | custom-call | flops 4831838208 | bytes 67108864 | tf_op jit(solution)/shard_map/pallas_call | solution.py:1082
  620.3 3.9 slice_add_fusion.d3_ref
  624.5 4.9 select_add_fusion.u3_ref
  629.4 248.3 %shard_map.209 = (f32[256,512]{1,0:T(8,128)}, f32[256,512]{1,0:T(8,128)}, f32[256,512]{1,0:T(8,128)}, f32[256,512]{1,0:T(8,128)}, f32[8,2048]{1,0:T(8,128)}, /*i...) custom-call(bf16[1024,2048]{1,0:T(8,128)(2,1)} %pad_maximum_fusion.h, ...), custom_call_target="tpu_custom_call" | custom-call | flops 12884901888 | bytes 100663296 | tf_op jit(solution)/shard_map/pallas_call | solution.py:685
  882.9 5.0 add_add_fusion
  891.8 4.9 copy.35
  (111 shorter events, 39.7 us)
Async XLA Ops:
  0.6 9.7 %copy-start.22 = (f32[2048]{0:T(1024)S(1)}, f32[2048]{0:T(1024)}, u32[]{:S(2)}) copy-start(f32[2048]{0:T(1024)} %param.17) | copy-start | bytes 24580
  7.1 3.4 copy-start.7
  124.1 5.3 copy-start.8
  127.4 5.3 copy-start.14
  127.4 45.0 %collective-permute-start.1 = (f32[256,1024]{1,0:T(8,128)}, f32[256,1024]{1,0:T(8,128)S(1)}, u32[]{:S(2)}, u32[]{:S(2)}) collective-permute-start(f32[256,1024]{1,0:T(8,128)} %get-tuple-element.140), channel_id=1, source_target_pairs={{0,2},{1,3},{2,0},{3,1},{4,6},{5,7},{6,4},{7,5},{8,10},{9,11},{10,... | collective-permute-start | bytes 3145736 | tf_op jit(solution)/shard_map/ppermute | solution.py:1011
  127.9 47.8 %collective-permute-start = (f32[256,1024]{1,0:T(8,128)}, f32[256,1024]{1,0:T(8,128)}, u32[]{:S(2)}, u32[]{:S(2)}) collective-permute-start(f32[256,1024]{1,0:T(8,128)} %get-tuple-element.139), channel_id=1, source_target_pairs={{0,2},{1,3},{2,0},{3,1},{4,6},{5,7},{6,4},{7,5},{8,10},{9,11},{10,... | collective-permute-start | bytes 3145736 | tf_op jit(solution)/shard_map/ppermute | solution.py:1011
  132.7 4.0 slice-start.2
  133.2 5.2 slice-start.3
  157.6 6.7 copy-start.23
  157.6 6.8 copy-start.13
  164.4 4.3 copy-start.12
  164.4 11.3 %slice-start = ((s8[8388608]{0:T(1024)(128)(4,1)}), s8[4194304]{0:T(1024)(128)(4,1)S(1)}, s32[]{:S(2)}) async-start(s8[8388608]{0:T(1024)(128)(4,1)} %bitcast.30), calls=%async_computation | async-start | bytes 8388608
  168.7 7.0 slice-start.1
  399.7 6.2 copy-start.4
  399.7 6.2 copy-start.6
  399.7 6.5 copy-start.10
  399.7 7.7 copy-start.11
  414.1 9.7 %copy-start.24 = (bf16[512,2048]{1,0:T(8,128)(2,1)S(1)}, bf16[512,2048]{1,0:T(8,128)(2,1)}, u32[]{:S(2)}) copy-start(bf16[512,2048]{1,0:T(8,128)(2,1)} %wo_ref.1) | copy-start | bytes 6291460
  427.2 193.1 %copy-start.25 = (f32[4]{0:T(128)S(1)}, f32[4]{0:T(128)}, u32[]{:S(2)}) copy-start(f32[4]{0:T(128)} %param.21) | copy-start | bytes 52
  624.5 4.9 copy-start.21
  882.9 5.0 copy-start.15
  882.9 5.0 copy-start.17
  891.8 4.9 copy-start.16
  896.8 3.6 copy-start.18
  (8 other events, 21.8 us)

commit v6 on v5

--- a/solution.py
+++ b/solution.py
@@ -15,7 +15,7 @@
 F32 = jnp.float32
 BF16 = jnp.bfloat16
 
-AG_CHUNKS = 2
+AG_CHUNKS = 1
 Z_FIRST = (1, 0)
 X_FIRST = (0, 1)
 
@@ -770,6 +770,96 @@
     )(v, gain[None, :] if norm else jnp.zeros((8, DH), F32))
 
 
+def norm_back_kernel(
+    part_hbm, far_hbm, resid_hbm, grad_hbm, gain_ref, dresid_hbm, dr_ref, sum_ref,
+    in_ref, og_ref, send_ref, recv_ref, c_send, c_recv, in_sem, og_sem, out_sem,
+):
+    peer = tensor_peer(1)
+    greet(peer)
+    half, width = dresid_hbm.shape
+    chunks = half // ROWS
+    sources = (part_hbm, far_hbm, resid_hbm)
+
+    def rows(c):
+        return pl.ds(c * ROWS, ROWS)
+
+    def loads(c):
+        k = c % 2
+        wide = [
+            pltpu.make_async_copy(src.at[rows(c), :], in_ref.at[k, i], in_sem.at[k, i])
+            for i, src in enumerate(sources)
+        ]
+        return wide + [
+            pltpu.make_async_copy(grad_hbm.at[rows(c), :], og_ref.at[k], og_sem.at[k])
+        ]
+
+    def wire(c):
+        return remote(send_ref.at[c], recv_ref.at[c], c_send.at[c], c_recv.at[c], peer)
+
+    def store(c):
+        return pltpu.make_async_copy(send_ref.at[c], dresid_hbm.at[rows(c), :], out_sem.at[c])
+
+    for c in range(2):
+        for load in loads(c):
+            load.start()
+    sum_ref[...] = jnp.zeros_like(sum_ref)
+    for c in range(chunks):
+        k = c % 2
+        for load in loads(c):
+            load.wait()
+        grad = in_ref[k, 0] + in_ref[k, 1]
+        x = in_ref[k, 2]
+        inv = lax.rsqrt(jnp.mean(x * x, axis=-1, keepdims=True) + EPS)
+        gs = grad * gain_ref[...]
+        inner = jnp.mean(gs * x, axis=-1, keepdims=True)
+        sum_ref[0:1, :] += jnp.sum(grad * x * inv, axis=0, keepdims=True)
+        value = og_ref[k].astype(F32) + inv * gs - x * inv * inv * inv * inner
+        send_ref[c] = value
+        wire(c).start()
+        store(c).start()
+        dr_ref[c * ROWS : (c + 1) * ROWS, :] = value.astype(BF16)
+        if c + 2 < chunks:
+            for load in loads(c + 2):
+                load.start()
+    for c in range(chunks):
+        wire(c).wait()
+        dr_ref[half + c * ROWS : half + (c + 1) * ROWS, :] = recv_ref[c].astype(BF16)
+    for c in range(chunks):
+        store(c).wait()
+
+
+def norm_back(ident, part, far, resid, out_grad, gain):
+    half, width = resid.shape
+    chunks = half // ROWS
+    outs = [
+        jax.ShapeDtypeStruct((half, width), F32),
+        jax.ShapeDtypeStruct((2 * half, width), BF16),
+        jax.ShapeDtypeStruct((8, width), F32),
+    ]
+    full = pl.BlockSpec(memory_space=pltpu.VMEM)
+    anywhere = pl.BlockSpec(memory_space=pl.ANY)
+    dma = pltpu.SemaphoreType.DMA
+    return pl.pallas_call(
+        norm_back_kernel,
+        out_shape=outs,
+        in_specs=[anywhere] * 4 + [full],
+        out_specs=[anywhere, full, full],
+        scratch_shapes=[
+            pltpu.VMEM((2, 3, ROWS, width), F32),
+            pltpu.VMEM((2, ROWS, width), BF16),
+            pltpu.VMEM((chunks, ROWS, width), F32),
+            pltpu.VMEM((chunks, ROWS, width), F32),
+            dma((chunks,)), dma((chunks,)), dma((2, 3)), dma((2,)), dma((chunks,)),
+        ],
+        compiler_params=pltpu.CompilerParams(
+            collective_id=ident, has_side_effects=True, vmem_limit_bytes=48 << 20
+        ),
+        cost_estimate=pl.CostEstimate(
+            flops=0, transcendentals=0, bytes_accessed=nbytes(part, far, resid, out_grad, *outs)
+        ),
+    )(part, far, resid, out_grad, gain[None, :])
+
+
 TILE = 256
 SLOTS = 4
 
@@ -1134,7 +1224,6 @@
         for n, f in zip(near, a_far)
     ]
     resid = jnp.concatenate(resids, 0)
-    inv_mlp = inv_rms(resid)
     h2 = core_gather(1, resid, gain_mlp)
 
     h_t = columns(h2, X_FIRST).T if rows % DH else None
@@ -1142,15 +1231,8 @@
         2, dp, h2, og_t, h_t, w_up, w_down, up_grad
     )
 
-    dh2 = dh2_part + dh2_far
-    gs = dh2 * gain_mlp
-    dresid = (
-        og_own.astype(F32)
-        + inv_mlp * gs
-        - resid * inv_mlp * inv_mlp * inv_mlp * jnp.mean(gs * resid, axis=-1, keepdims=True)
-    )
-    gain_mlp_part = jnp.sum(dh2 * resid * inv_mlp, axis=0)
-    dr = core_gather(4, dresid)
+    dresid, dr, gain_mlp_sum = norm_back(4, dh2_part, dh2_far, resid, og_own, gain_mlp)
+    gain_mlp_part = gain_mlp_sum[0]
 
     da = dot_nt(dr, w_out).astype(BF16)
     anywhere = pl.BlockSpec(memory_space=pl.ANY)

time: 911 us -> 901 us (0.989)
  other arithmetic: 51.7 us -> 39.5 us
    pallas_call x0 -> x1, Pallas kernels: none -> 13 us  [norm_back(): pl.pallas_call(norm_back_kernel, out_shape=outs, in_specs=[anywhere] * 4...]
    pallas_call x2 -> x1, Pallas kernels: 19.4 us -> 9.69 us  [core_gather(): pl.pallas_call(functools.partial(core_gather_kernel, norm, tiles), out_sh...]
    unnamed x67 -> x41, local copies, waits for them, and re-layouts: 19.7 us -> 17.1 us
  transfers between devices with their start and end apart: 2 -> 1, of which waited for: 1 -> 1; matrix products, arithmetic and copies ran while one was open for 4% -> 4% of each run, Pallas kernels for 1% -> 1%
where the time goes in v6:
time: 901 us; the launch traced here: 891 us
  Pallas kernels  785 us (87%)
  other arithmetic  39.5 us (4%)
  matrix products  31.2 us (3%)
  local copies, waits for them, and re-layouts  28.2 us (3%)
    pallas_call x2, Pallas kernels, attention_call(): pl.pallas_call(functools.partial(kernel, dp, heads, segs, scale), out_sha...  302 us
    pallas_call x1, Pallas kernels, tail(): pl.pallas_call(functools.partial(tail_kernel, dp, turn, X_FIRST, Z_FIRST)...  248 us
    pallas_call x1, Pallas kernels, feed(): pl.pallas_call(kernel, out_shape=[b16, b16, f32(half, width), f32(half, w...  205 us
    dot_general x2, matrix products, dot_nt(): lax.dot_general(a, b, (((1,), (1,)), ((), ())), preferred_element_type=F32)  18.7 us
  transfers between devices with their start and end apart: 1, of which 1 were waited for; matrix products, arithmetic and copies ran while one was open for 4% of the time, Pallas kernels for 1%

profile of v6, /device:TPU:0, one launch (start us, length us, event | category | flops | bytes accessed | tf_op | source)
XLA Modules:
  0.0 891.4 jit_solution(11425729381258114096)
XLA Ops:
  7.1 3.3 multiply_reduce_fusion
  11.6 2.6 pad_maximum_fusion.h_ref
  14.9 109.3 %shard_map.203 = (bf16[1024,512]{1,0:T(8,128)(2,1)}, bf16[1024,512]{1,0:T(8,128)(2,1)}, bf16[1024,512]{1,0:T(8,128)(2,1)}, bf16[1024,512]{1,0:T(8,128)(2,1)}, f3...) custom-call(f32[2,16]{1,0:T(2,128)} %fusion.28.w_ref, ...), custom_call_target="tpu_custom_call" | custom-call | flops 8053063680 | bytes 67108864 | tf_op jit(solution)/shard_map/pallas_call | solution.py:1172
  124.8 5.7 constant_dynamic-slice_fusion.3
  130.4 2.5 pad_maximum_fusion.1.in_ref
  133.1 13.2 %fusion.25.refs_2_ = f32[1024,2048]{1,0:T(8,128)} fusion(bf16[2048,2048]{1,0:T(8,128)(2,1)} %refs_1_.1, bf16[512,2048]{1,0:T(8,128)(2,1)S(1)} %get-tuple-element.138, bf16[512,2048]{1,0:T(8,128)(2,1)S(1)} %get-tuple-element.137.grad_hbm), kind=kOutput, calls=%fused_computation.78 | convolution fusion | flops 8598323200 | bytes 20971520 | tf_op jit(solution)/shard_map/dot_general | solution.py:53
  146.9 7.3 shard_map.204
  154.3 6.7 copy.26
  161.8 5.2 convert_add_fusion
  167.1 5.5 collective-permute-done
  172.5 7.2 fusion.11.v_ref.resid_hbm
  179.8 9.7 %shard_map.205.h_ref = bf16[1024,2048]{1,0:T(8,128)(2,1)S(1)} custom-call(f32[512,2048]{1,0:T(8,128)} %fusion.11.v_ref.resid_hbm, f32[1,2048]{1,0:T(1,128)S(1)} %bitcast.28), custom_call_target="tpu_custom_call" | custom-call | bytes 16777216 | tf_op jit(solution)/shard_map/pallas_call | solution.py:753
  191.4 205.2 %shard_map.206 = (bf16[1024,2048]{1,0:T(8,128)(2,1)}, bf16[1024,2048]{1,0:T(8,128)(2,1)}, f32[512,2048]{1,0:T(8,128)}, f32[512,2048]{1,0:T(8,128)}, f32[512,2048...) custom-call(bf16[1024,2048]{1,0:T(8,128)(2,1)} %copy-done.2, ...), custom_call_target="tpu_custom_call" | custom-call | flops 42949672960 | bytes 67108864 | tf_op jit(solution)/shard_map/pallas_call | solution.py:1037
  398.2 13.0 %shard_map.207 = (f32[512,2048]{1,0:T(8,128)}, bf16[1024,2048]{1,0:T(8,128)(2,1)}, f32[8,2048]{1,0:T(8,128)S(1)}) custom-call(f32[512,2048]{1,0:T(8,128)} %get-tuple-element.80.part_hbm, f32[512,2048]{1,0:T(8,128)} %get-tuple-element.81.far_hbm, f32[512,2048]{1,0:T(8,128)} %fusion.11.v_ref.resid_hbm, bf16[512,2048]{1,0:T(8,128)(2,1)S(1)} %copy-done.1, ...), custom_call_target="tpu_custom_call" | custom-call | bytes 23134208 | tf_op jit(solution)/shard_map/pallas_call | solution.py:842
  411.2 5.5 convolution_convert_fusion.da_ref
  416.7 192.3 %shard_map.208 = (bf16[1024,512]{1,0:T(8,128)(2,1)}, bf16[1024,512]{1,0:T(8,128)(2,1)}, bf16[1024,512]{1,0:T(8,128)(2,1)}, f32[8,128]{1,0:T(8,128)}, f32[1024,51...) custom-call(f32[2,16]{1,0:T(2,128)} %fusion.27.w_ref, f32[1,4]{1,0:T(1,128)} %fusion.32.g_ref, ...), custom_call_target="tpu_custom_call" | custom-call | flops 4831838208 | bytes 67108864 | tf_op jit(solution)/shard_map/pallas_call | solution.py:1172
  610.0 3.9 slice_add_fusion.d3_ref
  614.2 4.9 select_add_fusion.u3_ref
  619.1 248.3 %shard_map.209 = (f32[256,512]{1,0:T(8,128)}, f32[256,512]{1,0:T(8,128)}, f32[256,512]{1,0:T(8,128)}, f32[256,512]{1,0:T(8,128)}, f32[8,2048]{1,0:T(8,128)}, /*i...) custom-call(bf16[1024,2048]{1,0:T(8,128)(2,1)} %pad_maximum_fusion.h, ...), custom_call_target="tpu_custom_call" | custom-call | flops 12884901888 | bytes 100663296 | tf_op jit(solution)/shard_map/pallas_call | solution.py:685
  869.6 2.0 copy.27
  872.8 5.0 add_add_fusion
  877.7 2.1 add_bitcast_fusion
  881.6 4.9 copy.35
  886.6 2.0 copy.36
  (72 shorter events, 22.7 us)
Async XLA Ops:
  0.6 9.7 %copy-start.12 = (f32[2048]{0:T(1024)S(1)}, f32[2048]{0:T(1024)}, u32[]{:S(2)}) copy-start(f32[2048]{0:T(1024)} %param.17) | copy-start | bytes 24580
  7.1 3.4 copy-start.4
  124.2 48.4 %collective-permute-start = (f32[512,1024]{1,0:T(8,128)}, f32[512,1024]{1,0:T(8,128)}, u32[]{:S(2)}, u32[]{:S(2)}) collective-permute-start(f32[512,1024]{1,0:T(8,128)} %get-tuple-element.75), channel_id=1, source_target_pairs={{0,2},{1,3},{2,0},{3,1},{4,6},{5,7},{6,4},{7,5},{8,10},{9,11},{10,... | collective-permute-start | bytes 6291464 | tf_op jit(solution)/shard_map/ppermute | solution.py:1101
  130.4 2.7 copy-start
  154.3 6.7 copy-start.13
  154.3 7.5 copy-start.15
  172.5 7.2 copy-start.3
  189.5 1.9 copy-start.2
  396.6 1.6 copy-start.1
  398.2 13.0 %copy-start.14 = (bf16[512,2048]{1,0:T(8,128)(2,1)S(1)}, bf16[512,2048]{1,0:T(8,128)(2,1)}, u32[]{:S(2)}) copy-start(bf16[512,2048]{1,0:T(8,128)(2,1)} %wo_ref.1) | copy-start | bytes 6291460
  416.7 193.2 %copy-start.16 = (f32[4]{0:T(128)S(1)}, f32[4]{0:T(128)}, u32[]{:S(2)}) copy-start(f32[4]{0:T(128)} %param.21) | copy-start | bytes 52
  614.2 4.9 copy-start.11
  872.7 5.0 copy-start.5
  872.8 5.0 copy-start.7
  881.6 4.9 copy-start.6
  886.6 2.0 copy-start.10
  886.6 2.8 copy-start.9
  886.6 3.6 copy-start.8

commit v7 on v6

--- a/solution.py
+++ b/solution.py
@@ -143,6 +143,26 @@
 
 def tensor_peer(mask):
     return {"tensor": lax.axis_index("tensor") ^ mask}
+
+
+def preload(kernel, ins, which):
+    def wrapped(*refs):
+        extra = refs[len(refs) - len(which) - 1 :]
+        refs = list(refs[: len(refs) - len(which) - 1])
+        loads = {}
+        for k, i in enumerate(which):
+            loads[i] = pltpu.make_async_copy(refs[i], extra[k], extra[-1].at[k])
+            loads[i].start()
+            refs[i] = extra[k]
+
+        def ready(*places):
+            for i in places or tuple(loads):
+                loads.pop(i).wait()
+
+        kernel(ready, *refs)
+
+    scratch = [pltpu.VMEM(ins[i].shape, ins[i].dtype) for i in which]
+    return wrapped, scratch + [pltpu.SemaphoreType.DMA((len(which),))]
 
 
 def halving(dp, order):
@@ -230,7 +250,7 @@
 
 
 def attention_kernel(
-    dp, heads, segs, scale, w_ref, g_ref, h_ref, wq_ref, wk_ref, wv_ref, wo_ref,
+    dp, heads, segs, scale, ready, w_ref, g_ref, h_ref, wq_ref, wk_ref, wv_ref, wo_ref,
     q_ref, k_ref, v_ref, a16_ref, pair_ref, local_ref, mem_ref, zin_ref, all_ref,
     wf_ref, asend_ref, w_send, w_recv, a_send, a_recv, blocks_ref, send_sem, recv_sem,
 ):
@@ -258,6 +278,7 @@
             BF16
         )
 
+    ready(6)
     for c in range(W_CHUNKS):
         rows = slice(c * size, (c + 1) * size)
         wf_ref[0, rows, :] = wo_ref[rows, :].astype(F32)
@@ -271,6 +292,7 @@
             rows = pl.ds(pl.multiple_of(i * 256, 256), 256)
             out_ref[rows, :] = dot(h_ref[rows, :], matrix_ref[...]).astype(BF16)
 
+    ready()
     project(wk_ref, k_ref)
     project(wv_ref, v_ref)
 
@@ -324,8 +346,8 @@
 
 
 def attention_back_kernel(
-    dp, heads, segs, scale, w_ref, g_ref, q_ref, k_ref, v_ref, da_ref, local_ref, mem_ref, zin_ref,
-    dr_ref, a16_ref, d_pre_ref, u_pre_ref, out_part_ref,
+    dp, heads, segs, scale, ready, w_ref, g_ref, q_ref, k_ref, v_ref, da_ref, local_ref, mem_ref,
+    zin_ref, dr_ref, a16_ref, d_pre_ref, u_pre_ref, out_part_ref,
     dq_ref, dk_ref, dv_ref, gate_ref, o_pre_ref, d_rode_ref, u_rode_ref, out_far_ref,
     dqm_ref, dkl_ref, dvl_ref, os_ref, ride_send, ride_recv, blocks_ref, send_sem, recv_sem,
 ):
@@ -362,6 +384,7 @@
     plain = riders[:2] + riders[3:]
     for r in riders[:2] + riders[3:4]:
         r.start()
+    ready()
 
     @pl.loop(0, pairs)
     def _(p):
@@ -443,7 +466,7 @@
 
 
 def tail_kernel(
-    dp, turn, order, o_order,
+    dp, turn, order, o_order, ready,
     h_ref, dq_ref, dk_ref, dv_ref, wq_ref, wk_ref, wv_ref, o_pre_ref, gain_ref, vec_ref,
     d3_ref, u3_ref, resid_hbm, out_part_hbm, out_far_hbm, dresid_hbm, x_hbm,
     gq_ref, gk_ref, gv_ref, go_ref, vec_out_ref, far_ref, d3_got_ref, u3_got_ref, out_hbm, dx_hbm,
@@ -516,6 +539,7 @@
         for i, (src, dst, peer) in enumerate(legs)
     ]
     out_item = len(items) - 1
+    ready(7)
     advance(out_item, 1)
     for r in riders:
         r.start()
@@ -537,6 +561,7 @@
 
     for j in range(2 if turn else 0):
         block_load(j).start()
+    ready()
     turn_blocks(0, dp // 2)
     for i in range(out_item):
         advance(i, 0)
@@ -682,11 +707,19 @@
             bufs += [pltpu.VMEM((count, cols.stop - cols.start), F32)] * 2
     chunks = half // ROWS
     b16 = jax.ShapeDtypeStruct((tokens, width), BF16)
+    operands = (
+        h1 if turn else h1_t, *grads, *weights, o_pre, gain[None, :], vec, d3, u3, *streams
+    )
+    kernel, held = preload(
+        functools.partial(tail_kernel, dp, turn, X_FIRST, Z_FIRST),
+        operands,
+        range(1 if turn else 0, 10),
+    )
     return pl.pallas_call(
-        functools.partial(tail_kernel, dp, turn, X_FIRST, Z_FIRST),
+        kernel,
         out_shape=[f32(rows, flat)] * 4
         + [f32(*vec.shape), f32(half, width), f32(*d3.shape), f32(*u3.shape), b16, b16],
-        in_specs=[anywhere if turn else full] + [full] * 9 + [anywhere] * 7,
+        in_specs=[anywhere] * len(operands),
         out_specs=[full] * 5 + [anywhere] * 5,
         scratch_shapes=[
             pltpu.VMEM((chunks, ROWS, width), F32),
@@ -703,16 +736,15 @@
             pltpu.SemaphoreType.REGULAR,
         ]
         + bufs
-        + ([pltpu.VMEM((width, tokens), BF16)] if turn else []),
+        + ([pltpu.VMEM((width, tokens), BF16)] if turn else [])
+        + held,
         compiler_params=pltpu.CompilerParams(
             collective_id=ident, has_side_effects=True, vmem_limit_bytes=63 << 20
         ),
         cost_estimate=pl.CostEstimate(
             flops=12 * tokens * width * flat, transcendentals=0, bytes_accessed=96 << 20
         ),
-    )(
-        h1 if turn else h1_t, *grads, *weights, o_pre, gain[None, :], vec, d3, u3, *streams
-    )
+    )(*operands)
 
 
 def core_gather_kernel(norm, tiles, v_ref, gain_ref, out_ref, send_ref, recv_ref, send_sem, recv_sem):
@@ -865,7 +897,7 @@
 
 
 def feed_kernel(
-    dp, turn, h_ref, ogt_ref, ht_ref, wup_hbm, wdn_hbm, ug_hbm,
+    dp, turn, ready, h_ref, ogt_ref, ht_ref, wup_hbm, wdn_hbm, ug_hbm,
     act_ref, dpre_ref, part_ref, part2_ref, far_ref, d_ref, u_ref, d_pre_ref, u_pre_ref,
     w_ref, ug_ref, ds_ref, us_ref, cs_ref, cr_ref,
     w_sem, ug_sem, d_send, d_recv, u_send, u_recv, c_send, c_recv, y_send, y_recv, free_sem,
@@ -892,8 +924,10 @@
 
     load_ug(0, 0).start()
     load_ug(1, 1).start()
+    ready(0)
     for j in range(dp // 2 if turn else 0):
         ht_ref[j * rows : (j + 1) * rows, :] = block_of(h_ref, dp, X_FIRST, j).T
+    ready()
     load_w.wait()
 
     def wire(t, k):
@@ -1031,14 +1065,16 @@
     kernel = functools.partial(feed_kernel, dp, turn)
     if turn:
 
-        def kernel(h_ref, ogt_ref, *refs):
-            feed_kernel(dp, turn, h_ref, ogt_ref, refs[-1], *refs[:-1])
-
+        def kernel(ready, h_ref, ogt_ref, *refs):
+            feed_kernel(dp, turn, ready, h_ref, ogt_ref, refs[-1], *refs[:-1])
+
+    operands = (h2, og_t, *([] if turn else [h_t]), w_up, w_down, up_grad)
+    kernel, held = preload(kernel, operands, range(len(operands) - 3))
     return pl.pallas_call(
         kernel,
         out_shape=[b16, b16, f32(half, width), f32(half, width), f32(half, width)]
         + [f32(cut, units)] * 4,
-        in_specs=[full] * (2 if turn else 3) + [anywhere] * 3,
+        in_specs=[anywhere] * len(operands),
         out_specs=[full] * 4 + [anywhere] * 5,
         scratch_shapes=[
             pltpu.VMEM((width, units), BF16),
@@ -1050,7 +1086,8 @@
             dma, dma((2,)), dma((count,)), dma((count,)), dma((count,)), dma((count,)),
             dma((4,)), dma((4,)), dma((4,)), dma((4,)), pltpu.SemaphoreType.REGULAR,
         ]
-        + ([pltpu.VMEM((width, tokens), BF16)] if turn else []),
+        + ([pltpu.VMEM((width, tokens), BF16)] if turn else [])
+        + held,
         compiler_params=pltpu.CompilerParams(
             collective_id=ident, has_side_effects=True, vmem_limit_bytes=62 << 20
         ),
@@ -1058,7 +1095,7 @@
             flops=10 * tokens * width * units, transcendentals=tokens * units,
             bytes_accessed=64 << 20,
         ),
-    )(h2, og_t, *([] if turn else [h_t]), w_up, w_down, up_grad)
+    )(*operands)
 
 
 def body(
@@ -1168,9 +1205,14 @@
     zin_shape = jax.ShapeDtypeStruct((pairs, DH), F32)
     full = pl.BlockSpec(memory_space=pltpu.VMEM)
 
+    anywhere = pl.BlockSpec(memory_space=pl.ANY)
+
     def attention_call(kernel, ident, outs, out_specs, scratch, args, in_specs, flops):
+        which = [i for i, spec in enumerate(in_specs) if spec is full]
+        in_specs = [anywhere if spec is full else spec for spec in in_specs]
+        wrapped, held = preload(functools.partial(kernel, dp, heads, segs, scale), args, which)
         return pl.pallas_call(
-            functools.partial(kernel, dp, heads, segs, scale),
+            wrapped,
             out_shape=outs,
             in_specs=in_specs,
             out_specs=out_specs,
@@ -1179,7 +1221,8 @@
                 pltpu.VMEM((dp, block_rows, DH), F32),
                 pltpu.SemaphoreType.DMA((dp,)),
                 pltpu.SemaphoreType.DMA((dp,)),
-            ],
+            ]
+            + held,
             compiler_params=pltpu.CompilerParams(
                 collective_id=ident, has_side_effects=True, vmem_limit_bytes=63 << 20
             ),

time: 901 us -> 891 us (0.989)
  Pallas kernels: 785 us -> 775 us
where the time goes in v7:
time: 891 us; the launch traced here: 882 us
  Pallas kernels  775 us (87%)
  other arithmetic  39.6 us (4%)
  matrix products  31.2 us (4%)
  local copies, waits for them, and re-layouts  28.2 us (3%)
    pallas_call x2, Pallas kernels, attention_call(): pl.pallas_call(wrapped, out_shape=outs, in_specs=in_specs, out_specs=out_...  298 us
    pallas_call x1, Pallas kernels, tail(): pl.pallas_call(kernel, out_shape=[f32(rows, flat)] * 4 + [f32(*vec.shape)...  245 us
    pallas_call x1, Pallas kernels, feed(): pl.pallas_call(kernel, out_shape=[b16, b16, f32(half, width), f32(half, w...  203 us
    dot_general x2, matrix products, dot_nt(): lax.dot_general(a, b, (((1,), (1,)), ((), ())), preferred_element_type=F32)  18.7 us
  transfers between devices with their start and end apart: 1, of which 1 were waited for; matrix products, arithmetic and copies ran while one was open for 4% of the time, Pallas kernels for 1%

profile of v7, /device:TPU:0, one launch (start us, length us, event | category | flops | bytes accessed | tf_op | source)
XLA Modules:
  0.0 881.7 jit_solution(4239563200538712955)
XLA Ops:
  7.1 3.3 multiply_reduce_fusion
  11.6 2.6 pad_maximum_fusion.refs_2_.refs_0_
  14.9 107.7 %shard_map.203 = (bf16[1024,512]{1,0:T(8,128)(2,1)}, bf16[1024,512]{1,0:T(8,128)(2,1)}, bf16[1024,512]{1,0:T(8,128)(2,1)}, bf16[1024,512]{1,0:T(8,128)(2,1)}, f3...) custom-call(f32[2,16]{1,0:T(2,128)} %fusion.28.refs_0_, ...), custom_call_target="tpu_custom_call" | custom-call | flops 8053063680 | bytes 67108864 | tf_op jit(solution)/shard_map/pallas_call | solution.py:1214
  122.7 5.7 constant_dynamic-slice_fusion.3
  128.3 2.5 pad_maximum_fusion.1.in_ref
  131.0 13.2 %fusion.25.refs_4_ = f32[1024,2048]{1,0:T(8,128)} fusion(bf16[2048,2048]{1,0:T(8,128)(2,1)} %refs_3_.3, bf16[512,2048]{1,0:T(8,128)(2,1)S(1)} %get-tuple-element.138, bf16[512,2048]{1,0:T(8,128)(2,1)S(1)} %get-tuple-element.137.grad_hbm), kind=kOutput, calls=%fused_computation.78 | convolution fusion | flops 8598323200 | bytes 20971520 | tf_op jit(solution)/shard_map/dot_general | solution.py:53
  144.9 7.3 shard_map.204
  152.2 6.7 copy.26
  159.7 5.2 convert_add_fusion
  165.0 6.0 collective-permute-done
  170.9 7.2 fusion.11.v_ref.resid_hbm.refs_12_
  178.2 9.7 %shard_map.205.refs_0_ = bf16[1024,2048]{1,0:T(8,128)(2,1)S(1)} custom-call(f32[512,2048]{1,0:T(8,128)} %fusion.11.v_ref.resid_hbm.refs_12_, f32[1,2048]{1,0:T(1,128)S(1)} %bitcast.28), custom_call_target="tpu_custom_call" | custom-call | bytes 16777216 | tf_op jit(solution)/shard_map/pallas_call | solution.py:785
  189.8 202.7 %shard_map.206 = (bf16[1024,2048]{1,0:T(8,128)(2,1)}, bf16[1024,2048]{1,0:T(8,128)(2,1)}, f32[512,2048]{1,0:T(8,128)}, f32[512,2048]{1,0:T(8,128)}, f32[512,2048...) custom-call(bf16[1024,2048]{1,0:T(8,128)(2,1)} %copy-done.2, ...), custom_call_target="tpu_custom_call" | custom-call | flops 42949672960 | bytes 67108864 | tf_op jit(solution)/shard_map/pallas_call | solution.py:1073
  394.1 13.0 %shard_map.207 = (f32[512,2048]{1,0:T(8,128)}, bf16[1024,2048]{1,0:T(8,128)(2,1)}, f32[8,2048]{1,0:T(8,128)S(1)}) custom-call(f32[512,2048]{1,0:T(8,128)} %get-tuple-element.80.part_hbm, f32[512,2048]{1,0:T(8,128)} %get-tuple-element.81.far_hbm, f32[512,2048]{1,0:T(8,128)} %fusion.11.v_ref.resid_hbm.refs_12_, bf16[512,2048]{1,0:T(8,128)(2,1)S(1)} %copy-done.1, ...), custom_call_target="tpu_custom_call" | custom-call | bytes 23134208 | tf_op jit(solution)/shard_map/pallas_call | solution.py:874
  407.1 5.5 convolution_convert_fusion.refs_5_
  412.6 190.3 %shard_map.208 = (bf16[1024,512]{1,0:T(8,128)(2,1)}, bf16[1024,512]{1,0:T(8,128)(2,1)}, bf16[1024,512]{1,0:T(8,128)(2,1)}, f32[8,128]{1,0:T(8,128)}, f32[1024,51...) custom-call(f32[2,16]{1,0:T(2,128)} %fusion.27.refs_0_, f32[1,4]{1,0:T(1,128)} %fusion.32.refs_1_, ...), custom_call_target="tpu_custom_call" | custom-call | flops 4831838208 | bytes 67108864 | tf_op jit(solution)/shard_map/pallas_call | solution.py:1214
  603.9 3.9 slice_add_fusion.refs_10_
  608.1 4.9 select_add_fusion.refs_11_
  613.0 244.7 %shard_map.209 = (f32[256,512]{1,0:T(8,128)}, f32[256,512]{1,0:T(8,128)}, f32[256,512]{1,0:T(8,128)}, f32[256,512]{1,0:T(8,128)}, f32[8,2048]{1,0:T(8,128)}, /*i...) custom-call(bf16[1024,2048]{1,0:T(8,128)(2,1)} %pad_maximum_fusion.r, ...), custom_call_target="tpu_custom_call" | custom-call | flops 12884901888 | bytes 100663296 | tf_op jit(solution)/shard_map/pallas_call | solution.py:718
  859.8 2.0 copy.27
  863.0 5.0 add_add_fusion
  868.0 2.1 add_bitcast_fusion
  871.9 4.9 copy.35
  876.8 2.0 copy.36
  (72 shorter events, 22.2 us)
Async XLA Ops:
  0.6 9.7 %copy-start.12 = (f32[2048]{0:T(1024)S(1)}, f32[2048]{0:T(1024)}, u32[]{:S(2)}) copy-start(f32[2048]{0:T(1024)} %param.17) | copy-start | bytes 24580
  7.1 3.4 copy-start.4
  122.6 48.4 %collective-permute-start = (f32[512,1024]{1,0:T(8,128)}, f32[512,1024]{1,0:T(8,128)}, u32[]{:S(2)}, u32[]{:S(2)}) collective-permute-start(f32[512,1024]{1,0:T(8,128)} %get-tuple-element.75), channel_id=1, source_target_pairs={{0,2},{1,3},{2,0},{3,1},{4,6},{5,7},{6,4},{7,5},{8,10},{9,11},{10,... | collective-permute-start | bytes 6291464 | tf_op jit(solution)/shard_map/ppermute | solution.py:1138
  128.3 2.7 copy-start
  152.2 6.7 copy-start.13
  152.2 7.5 copy-start.15
  170.9 7.2 copy-start.3
  187.9 1.9 copy-start.2
  392.5 1.6 copy-start.1
  394.1 13.0 %copy-start.14 = (bf16[512,2048]{1,0:T(8,128)(2,1)S(1)}, bf16[512,2048]{1,0:T(8,128)(2,1)}, u32[]{:S(2)}) copy-start(bf16[512,2048]{1,0:T(8,128)(2,1)} %refs_6_.2) | copy-start | bytes 6291460
  412.6 191.2 %copy-start.16 = (f32[4]{0:T(128)S(1)}, f32[4]{0:T(128)}, u32[]{:S(2)}) copy-start(f32[4]{0:T(128)} %param.21) | copy-start | bytes 52
  608.1 4.9 copy-start.11
  863.0 5.0 copy-start.5
  863.0 5.0 copy-start.7
  871.9 4.9 copy-start.6
  876.8 2.0 copy-start.10
  876.8 2.8 copy-start.9
  876.8 3.6 copy-start.8

commit v8 on v7

--- a/solution.py
+++ b/solution.py
@@ -175,7 +175,7 @@
 
 
 def near_units(dp, units):
-    return units // 4 if dp == 8 else units
+    return units // 16 if dp == 8 else units
 
 
 def block_of(ref, dp, order, k):

time: 891 us -> 899 us (level)
    pallas_call x2, Pallas kernels: 298 us -> 315 us  [attention_call(): pl.pallas_call(wrapped, out_shape=outs, in_specs=in_specs, out_specs=out_...]
    pallas_call x1, Pallas kernels: 245 us -> 235 us  [tail(): pl.pallas_call(kernel, out_shape=[f32(rows, flat)] * 4 + [f32(*vec.shape)...]
where the time goes in v8:
time: 899 us; the launch traced here: 889 us
  Pallas kernels  783 us (87%)
  other arithmetic  39.6 us (4%)
  matrix products  31.2 us (3%)
  local copies, waits for them, and re-layouts  28.2 us (3%)
    pallas_call x2, Pallas kernels, attention_call(): pl.pallas_call(wrapped, out_shape=outs, in_specs=in_specs, out_specs=out_...  315 us
    pallas_call x1, Pallas kernels, tail(): pl.pallas_call(kernel, out_shape=[f32(rows, flat)] * 4 + [f32(*vec.shape)...  235 us
    pallas_call x1, Pallas kernels, feed(): pl.pallas_call(kernel, out_shape=[b16, b16, f32(half, width), f32(half, w...  203 us
    dot_general x2, matrix products, dot_nt(): lax.dot_general(a, b, (((1,), (1,)), ((), ())), preferred_element_type=F32)  18.7 us
  transfers between devices with their start and end apart: 1, of which 1 were waited for; matrix products, arithmetic and copies ran while one was open for 4% of the time, Pallas kernels for 1%

profile of v8, /device:TPU:0, one launch (start us, length us, event | category | flops | bytes accessed | tf_op | source)
XLA Modules:
  0.0 889.3 jit_solution(1380520194298024799)
XLA Ops:
  7.1 3.3 multiply_reduce_fusion
  11.6 2.6 pad_maximum_fusion.refs_2_.refs_0_
  14.9 107.7 %shard_map.203 = (bf16[1024,512]{1,0:T(8,128)(2,1)}, bf16[1024,512]{1,0:T(8,128)(2,1)}, bf16[1024,512]{1,0:T(8,128)(2,1)}, bf16[1024,512]{1,0:T(8,128)(2,1)}, f3...) custom-call(f32[2,16]{1,0:T(2,128)} %fusion.28.refs_0_, ...), custom_call_target="tpu_custom_call" | custom-call | flops 8053063680 | bytes 67108864 | tf_op jit(solution)/shard_map/pallas_call | solution.py:1214
  122.7 5.7 constant_dynamic-slice_fusion.3
  128.3 2.5 pad_maximum_fusion.1.in_ref
  131.0 13.2 %fusion.25.refs_4_ = f32[1024,2048]{1,0:T(8,128)} fusion(bf16[2048,2048]{1,0:T(8,128)(2,1)} %refs_3_.3, bf16[512,2048]{1,0:T(8,128)(2,1)S(1)} %get-tuple-element.138, bf16[512,2048]{1,0:T(8,128)(2,1)S(1)} %get-tuple-element.137.grad_hbm), kind=kOutput, calls=%fused_computation.78 | convolution fusion | flops 8598323200 | bytes 20971520 | tf_op jit(solution)/shard_map/dot_general | solution.py:53
  144.9 7.3 shard_map.204
  152.2 6.7 copy.26
  159.7 5.2 convert_add_fusion
  165.0 6.0 collective-permute-done
  170.9 7.2 fusion.11.v_ref.resid_hbm.refs_12_
  178.2 9.7 %shard_map.205.refs_0_ = bf16[1024,2048]{1,0:T(8,128)(2,1)S(1)} custom-call(f32[512,2048]{1,0:T(8,128)} %fusion.11.v_ref.resid_hbm.refs_12_, f32[1,2048]{1,0:T(1,128)S(1)} %bitcast.28), custom_call_target="tpu_custom_call" | custom-call | bytes 16777216 | tf_op jit(solution)/shard_map/pallas_call | solution.py:785
  189.8 202.7 %shard_map.206 = (bf16[1024,2048]{1,0:T(8,128)(2,1)}, bf16[1024,2048]{1,0:T(8,128)(2,1)}, f32[512,2048]{1,0:T(8,128)}, f32[512,2048]{1,0:T(8,128)}, f32[512,2048...) custom-call(bf16[1024,2048]{1,0:T(8,128)(2,1)} %copy-done.2, ...), custom_call_target="tpu_custom_call" | custom-call | flops 42949672960 | bytes 67108864 | tf_op jit(solution)/shard_map/pallas_call | solution.py:1073
  394.1 13.0 %shard_map.207 = (f32[512,2048]{1,0:T(8,128)}, bf16[1024,2048]{1,0:T(8,128)(2,1)}, f32[8,2048]{1,0:T(8,128)S(1)}) custom-call(f32[512,2048]{1,0:T(8,128)} %get-tuple-element.80.part_hbm, f32[512,2048]{1,0:T(8,128)} %get-tuple-element.81.far_hbm, f32[512,2048]{1,0:T(8,128)} %fusion.11.v_ref.resid_hbm.refs_12_, bf16[512,2048]{1,0:T(8,128)(2,1)S(1)} %copy-done.1, ...), custom_call_target="tpu_custom_call" | custom-call | bytes 23134208 | tf_op jit(solution)/shard_map/pallas_call | solution.py:874
  407.1 5.5 convolution_convert_fusion.refs_5_
  412.6 207.4 %shard_map.208 = (bf16[1024,512]{1,0:T(8,128)(2,1)}, bf16[1024,512]{1,0:T(8,128)(2,1)}, bf16[1024,512]{1,0:T(8,128)(2,1)}, f32[8,128]{1,0:T(8,128)}, f32[1024,51...) custom-call(f32[2,16]{1,0:T(2,128)} %fusion.27.refs_0_, f32[1,4]{1,0:T(1,128)} %fusion.32.refs_1_, ...), custom_call_target="tpu_custom_call" | custom-call | flops 4831838208 | bytes 67108864 | tf_op jit(solution)/shard_map/pallas_call | solution.py:1214
  620.9 3.9 slice_add_fusion.refs_10_
  625.2 4.9 select_add_fusion.refs_11_
  630.1 235.3 %shard_map.209 = (f32[256,512]{1,0:T(8,128)}, f32[256,512]{1,0:T(8,128)}, f32[256,512]{1,0:T(8,128)}, f32[256,512]{1,0:T(8,128)}, f32[8,2048]{1,0:T(8,128)}, /*i...) custom-call(bf16[1024,2048]{1,0:T(8,128)(2,1)} %pad_maximum_fusion.r, ...), custom_call_target="tpu_custom_call" | custom-call | flops 12884901888 | bytes 100663296 | tf_op jit(solution)/shard_map/pallas_call | solution.py:718
  867.5 2.0 copy.27
  870.6 5.0 add_add_fusion
  875.6 2.1 add_bitcast_fusion
  879.5 4.9 copy.35
  884.5 2.0 copy.36
  (72 shorter events, 22.2 us)
Async XLA Ops:
  0.6 9.7 %copy-start.12 = (f32[2048]{0:T(1024)S(1)}, f32[2048]{0:T(1024)}, u32[]{:S(2)}) copy-start(f32[2048]{0:T(1024)} %param.17) | copy-start | bytes 24580
  7.1 3.4 copy-start.4
  122.6 48.4 %collective-permute-start = (f32[512,1024]{1,0:T(8,128)}, f32[512,1024]{1,0:T(8,128)}, u32[]{:S(2)}, u32[]{:S(2)}) collective-permute-start(f32[512,1024]{1,0:T(8,128)} %get-tuple-element.75), channel_id=1, source_target_pairs={{0,2},{1,3},{2,0},{3,1},{4,6},{5,7},{6,4},{7,5},{8,10},{9,11},{10,... | collective-permute-start | bytes 6291464 | tf_op jit(solution)/shard_map/ppermute | solution.py:1138
  128.3 2.7 copy-start
  152.2 6.7 copy-start.13
  152.2 7.5 copy-start.15
  170.9 7.2 copy-start.3
  187.9 1.9 copy-start.2
  392.5 1.6 copy-start.1
  394.1 13.0 %copy-start.14 = (bf16[512,2048]{1,0:T(8,128)(2,1)S(1)}, bf16[512,2048]{1,0:T(8,128)(2,1)}, u32[]{:S(2)}) copy-start(bf16[512,2048]{1,0:T(8,128)(2,1)} %refs_6_.2) | copy-start | bytes 6291460
  412.6 208.3 %copy-start.16 = (f32[4]{0:T(128)S(1)}, f32[4]{0:T(128)}, u32[]{:S(2)}) copy-start(f32[4]{0:T(128)} %param.21) | copy-start | bytes 52
  625.2 4.9 copy-start.11
  870.6 5.0 copy-start.5
  870.6 5.0 copy-start.7
  879.5 4.9 copy-start.6
  884.5 2.0 copy-start.10
  884.5 2.8 copy-start.9
  884.5 3.6 copy-start.8

commit v9 on v7

--- a/solution.py
+++ b/solution.py
@@ -541,7 +541,7 @@
     out_item = len(items) - 1
     ready(7)
     advance(out_item, 1)
-    for r in riders:
+    for r in reversed(riders):
         r.start()
 
     def block_load(j):

time: 891 us -> 885 us (level)
  no operation moved by 1% of the time
where the time goes in v9:
time: 885 us; the launch traced here: 876 us
  Pallas kernels  770 us (87%)
  other arithmetic  39.6 us (4%)
  matrix products  31.2 us (4%)
  local copies, waits for them, and re-layouts  28.2 us (3%)
    pallas_call x2, Pallas kernels, attention_call(): pl.pallas_call(wrapped, out_shape=outs, in_specs=in_specs, out_specs=out_...  298 us
    pallas_call x1, Pallas kernels, tail(): pl.pallas_call(kernel, out_shape=[f32(rows, flat)] * 4 + [f32(*vec.shape)...  239 us
    pallas_call x1, Pallas kernels, feed(): pl.pallas_call(kernel, out_shape=[b16, b16, f32(half, width), f32(half, w...  203 us
    dot_general x2, matrix products, dot_nt(): lax.dot_general(a, b, (((1,), (1,)), ((), ())), preferred_element_type=F32)  18.7 us
  transfers between devices with their start and end apart: 1, of which 1 were waited for; matrix products, arithmetic and copies ran while one was open for 4% of the time, Pallas kernels for 1%

profile of v9, /device:TPU:0, one launch (start us, length us, event | category | flops | bytes accessed | tf_op | source)
XLA Modules:
  0.0 876.1 jit_solution(13074059802725167783)
XLA Ops:
  7.1 3.3 multiply_reduce_fusion
  11.6 2.6 pad_maximum_fusion.refs_2_.refs_0_
  14.9 107.7 %shard_map.203 = (bf16[1024,512]{1,0:T(8,128)(2,1)}, bf16[1024,512]{1,0:T(8,128)(2,1)}, bf16[1024,512]{1,0:T(8,128)(2,1)}, bf16[1024,512]{1,0:T(8,128)(2,1)}, f3...) custom-call(f32[2,16]{1,0:T(2,128)} %fusion.28.refs_0_, ...), custom_call_target="tpu_custom_call" | custom-call | flops 8053063680 | bytes 67108864 | tf_op jit(solution)/shard_map/pallas_call | solution.py:1214
  122.7 5.7 constant_dynamic-slice_fusion.3
  128.3 2.5 pad_maximum_fusion.1.in_ref
  131.0 13.2 %fusion.25.refs_4_ = f32[1024,2048]{1,0:T(8,128)} fusion(bf16[2048,2048]{1,0:T(8,128)(2,1)} %refs_3_.3, bf16[512,2048]{1,0:T(8,128)(2,1)S(1)} %get-tuple-element.138, bf16[512,2048]{1,0:T(8,128)(2,1)S(1)} %get-tuple-element.137.grad_hbm), kind=kOutput, calls=%fused_computation.78 | convolution fusion | flops 8598323200 | bytes 20971520 | tf_op jit(solution)/shard_map/dot_general | solution.py:53
  144.9 7.3 shard_map.204
  152.2 6.7 copy.26
  159.7 5.2 convert_add_fusion
  165.0 6.0 collective-permute-done
  170.9 7.2 fusion.11.v_ref.resid_hbm.refs_12_
  178.2 9.7 %shard_map.205.refs_0_ = bf16[1024,2048]{1,0:T(8,128)(2,1)S(1)} custom-call(f32[512,2048]{1,0:T(8,128)} %fusion.11.v_ref.resid_hbm.refs_12_, f32[1,2048]{1,0:T(1,128)S(1)} %bitcast.28), custom_call_target="tpu_custom_call" | custom-call | bytes 16777216 | tf_op jit(solution)/shard_map/pallas_call | solution.py:785
  189.8 202.7 %shard_map.206 = (bf16[1024,2048]{1,0:T(8,128)(2,1)}, bf16[1024,2048]{1,0:T(8,128)(2,1)}, f32[512,2048]{1,0:T(8,128)}, f32[512,2048]{1,0:T(8,128)}, f32[512,2048...) custom-call(bf16[1024,2048]{1,0:T(8,128)(2,1)} %copy-done.2, ...), custom_call_target="tpu_custom_call" | custom-call | flops 42949672960 | bytes 67108864 | tf_op jit(solution)/shard_map/pallas_call | solution.py:1073
  394.1 13.0 %shard_map.207 = (f32[512,2048]{1,0:T(8,128)}, bf16[1024,2048]{1,0:T(8,128)(2,1)}, f32[8,2048]{1,0:T(8,128)S(1)}) custom-call(f32[512,2048]{1,0:T(8,128)} %get-tuple-element.80.part_hbm, f32[512,2048]{1,0:T(8,128)} %get-tuple-element.81.far_hbm, f32[512,2048]{1,0:T(8,128)} %fusion.11.v_ref.resid_hbm.refs_12_, bf16[512,2048]{1,0:T(8,128)(2,1)S(1)} %copy-done.1, ...), custom_call_target="tpu_custom_call" | custom-call | bytes 23134208 | tf_op jit(solution)/shard_map/pallas_call | solution.py:874
  407.1 5.5 convolution_convert_fusion.refs_5_
  412.6 190.3 %shard_map.208 = (bf16[1024,512]{1,0:T(8,128)(2,1)}, bf16[1024,512]{1,0:T(8,128)(2,1)}, bf16[1024,512]{1,0:T(8,128)(2,1)}, f32[8,128]{1,0:T(8,128)}, f32[1024,51...) custom-call(f32[2,16]{1,0:T(2,128)} %fusion.27.refs_0_, f32[1,4]{1,0:T(1,128)} %fusion.32.refs_1_, ...), custom_call_target="tpu_custom_call" | custom-call | flops 4831838208 | bytes 67108864 | tf_op jit(solution)/shard_map/pallas_call | solution.py:1214
  603.9 3.9 slice_add_fusion.refs_10_
  608.1 4.9 select_add_fusion.refs_11_
  613.0 239.1 %shard_map.209 = (f32[256,512]{1,0:T(8,128)}, f32[256,512]{1,0:T(8,128)}, f32[256,512]{1,0:T(8,128)}, f32[256,512]{1,0:T(8,128)}, f32[8,2048]{1,0:T(8,128)}, /*i...) custom-call(bf16[1024,2048]{1,0:T(8,128)(2,1)} %pad_maximum_fusion.r, ...), custom_call_target="tpu_custom_call" | custom-call | flops 12884901888 | bytes 100663296 | tf_op jit(solution)/shard_map/pallas_call | solution.py:718
  854.2 2.0 copy.27
  857.4 5.0 add_add_fusion
  862.4 2.1 add_bitcast_fusion
  866.3 4.9 copy.35
  871.2 2.0 copy.36
  (72 shorter events, 22.2 us)
Async XLA Ops:
  0.6 9.7 %copy-start.12 = (f32[2048]{0:T(1024)S(1)}, f32[2048]{0:T(1024)}, u32[]{:S(2)}) copy-start(f32[2048]{0:T(1024)} %param.17) | copy-start | bytes 24580
  7.1 3.4 copy-start.4
  122.6 48.4 %collective-permute-start = (f32[512,1024]{1,0:T(8,128)}, f32[512,1024]{1,0:T(8,128)}, u32[]{:S(2)}, u32[]{:S(2)}) collective-permute-start(f32[512,1024]{1,0:T(8,128)} %get-tuple-element.75), channel_id=1, source_target_pairs={{0,2},{1,3},{2,0},{3,1},{4,6},{5,7},{6,4},{7,5},{8,10},{9,11},{10,... | collective-permute-start | bytes 6291464 | tf_op jit(solution)/shard_map/ppermute | solution.py:1138
  128.3 2.7 copy-start
  152.2 6.7 copy-start.13
  152.2 7.5 copy-start.15
  170.9 7.2 copy-start.3
  187.9 1.9 copy-start.2
  392.5 1.6 copy-start.1
  394.1 13.0 %copy-start.14 = (bf16[512,2048]{1,0:T(8,128)(2,1)S(1)}, bf16[512,2048]{1,0:T(8,128)(2,1)}, u32[]{:S(2)}) copy-start(bf16[512,2048]{1,0:T(8,128)(2,1)} %refs_6_.2) | copy-start | bytes 6291460
  412.6 191.2 %copy-start.16 = (f32[4]{0:T(128)S(1)}, f32[4]{0:T(128)}, u32[]{:S(2)}) copy-start(f32[4]{0:T(128)} %param.21) | copy-start | bytes 52
  608.1 4.9 copy-start.11
  857.4 5.0 copy-start.5
  857.4 5.0 copy-start.7
  866.3 4.9 copy-start.6
  871.2 2.0 copy-start.10
  871.2 2.8 copy-start.9
  871.2 3.6 copy-start.8
